TPU v7x, 32 devices: a whole 2x2x4 slice. The times are simulated.
32 devices in a mesh: py: 4 (over y, x), pz: 8 (over z, core).
Axes of the slice: x: 2, y: 2, z: 4, core: 2. Of those that a mesh axis runs over, the one named last changes fastest.
Arguments:
- field_one: float32 [256, 256, 512], P('py', 'pz'), may hold values from -6 to 6
- field_two: float32 [256, 256, 512], P('py', 'pz'), may hold values from -6 to 6
- coef: float32 [2, 2, 8], replicated, may hold values from -4 to 4
Outputs:
- potential_one: float32 [256, 256, 512], P('py', 'pz')
- potential_two: float32 [256, 256, 512], P('py', 'pz')
All inputs are finite; a program needn't handle non-finite values.
Results may differ from a plain program's by a relative error of at most 0.00013.
Values sent between devices are 32-bit elements; how exact they have to be, the bound alone decides.
No kernel may reach another device: no remote copies, remote signals or barrier semaphores. Data moves between devices by JAX's collectives and lax.ppermute only.
A program may use at most 256 MiB of HBM per device.

v0:
```python
import math

import jax
import jax.numpy as jnp
from jax import lax
from jax.sharding import PartitionSpec as P

HIGH = lax.Precision.HIGHEST


def padded_2(value, sides, width):
    for axis, dim in sides:
        size, length = (lax.axis_size(axis), value.shape[dim])
        up = [(i, (i + 1) % size) for i in range(size)]
        down = [(j, i) for i, j in up]
        last = lax.slice_in_dim(value, length - width, length, axis=dim)
        leading = lax.slice_in_dim(value, 0, width, axis=dim)
        before = lax.ppermute(last, axis, up)
        after = lax.ppermute(leading, axis, down)
        value = jnp.concatenate([before, value, after], axis=dim)
    return value


def freq_at(position, length):
    paired = position // 2
    odd_bit = position % 2
    inner = jnp.where(odd_bit == 0, paired, length - paired)
    return jnp.where(paired == 0, odd_bit * (length // 2), inner)


def scaled_signed(freq, length):
    return jnp.where(freq > length // 2, freq - length, freq).astype(jnp.float32) / length


def forward_table(length):
    indices = jnp.arange(length, dtype=jnp.int32)
    freq = freq_at(indices, length)
    phase = indices[:, None] * freq[None, :] % length
    angle = 2.0 * math.pi / length * phase.astype(jnp.float32)
    return (jnp.cos(angle), jnp.sin(angle))


def inverse_table(length):
    cosine, sine = forward_table(length)
    return (cosine.T / length, sine.T / length)


def contract(form, data, table):
    return jnp.einsum(form, data, table, precision=HIGH)


def complex_apply(form, real_part, imag_part, cosine, sine, sign):
    if imag_part is None:
        return (contract(form, real_part, cosine), -sign * contract(form, real_part, sine))
    real_out = contract(form, real_part, cosine) + sign * contract(form, imag_part, sine)
    imag_out = contract(form, imag_part, cosine) - sign * contract(form, real_part, sine)
    return (real_out, imag_out)


def make_kernel(coef, freqs, lengths):
    radius = scaled_signed(freqs[0], lengths[0]) ** 2 + scaled_signed(freqs[1], lengths[1]) ** 2
    radius = radius + scaled_signed(freqs[2], lengths[2]) ** 2
    ratio = 4.0 * radius / 3.0
    volume = ratio * jnp.sqrt(ratio)
    basis_count = coef.shape[2]
    centres = (jnp.arange(basis_count, dtype=jnp.float32) + 0.5) / basis_count
    basis = jnp.exp(-jnp.square((volume[None] - centres[:, None, None, None]) * basis_count))
    kernel = jnp.einsum("abr,rkxm->abkxm", coef, basis, precision=HIGH)
    return kernel


def shards(field_one, field_two, coef):
    y_local, z_local, x_count = field_one.shape
    py_count = lax.axis_size("py")
    pz_count = lax.axis_size("pz")
    y_count = y_local * py_count
    z_count = z_local * pz_count
    x_block = x_count // py_count
    ky_block = y_count // pz_count
    cells = y_local * z_local
    fields = jnp.stack([field_one, field_two])
    along_x = (4.0 * fields + jnp.roll(fields, 1, 3) + jnp.roll(fields, -1, 3)) / 6.0
    padded = padded_2(along_x, (("py", 1), ("pz", 2)), 1)
    along_y = (4.0 * padded[:, 1:-1] + padded[:, 2:] + padded[:, :-2]) / 6.0
    smoothed = (4.0 * along_y[:, :, 1:-1] + along_y[:, :, 2:] + along_y[:, :, :-2]) / 6.0
    flat = smoothed.reshape(2, cells, x_count)
    x_cos, x_sin = forward_table(x_count)
    real_part, imag_part = complex_apply("bsx,xq->bqs", flat, None, x_cos, x_sin, 1.0)
    batch = real_part.shape[0]
    y_cos, y_sin = forward_table(y_count)
    z_cos, z_sin = forward_table(z_count)
    zi_cos, zi_sin = inverse_table(z_count)
    yi_cos, yi_sin = inverse_table(y_count)
    xi_cos, xi_sin = inverse_table(x_count)
    real_in = lax.all_to_all(real_part, "py", split_axis=1, concat_axis=2, tiled=True)
    imag_in = lax.all_to_all(imag_part, "py", split_axis=1, concat_axis=2, tiled=True)
    items = real_in.shape[0]

    def relay(values):
        values = values.reshape(items, x_block, y_count, z_local).transpose(0, 2, 1, 3)
        return values.reshape(items, y_count, x_block * z_local)

    real_part, imag_part = complex_apply(
        "byc,yk->bkc", relay(real_in), relay(imag_in), y_cos, y_sin, 1.0
    )
    real_in = lax.all_to_all(real_part, "pz", split_axis=1, concat_axis=2, tiled=True)
    imag_in = lax.all_to_all(imag_part, "pz", split_axis=1, concat_axis=2, tiled=True)
    lines_items = real_in.shape[0]

    def relay(values):
        values = values.reshape(lines_items, ky_block, pz_count, x_block, z_local).transpose(
            0, 1, 3, 2, 4
        )
        return values.reshape(lines_items, ky_block, x_block, z_count)

    real_part, imag_part = complex_apply(
        "bkxz,zm->bkxm", relay(real_in), relay(imag_in), z_cos, z_sin, 1.0
    )
    ky_start = lax.axis_index("pz") * ky_block
    kx_start = lax.axis_index("py") * x_block
    freq_y = freq_at(ky_start + jnp.arange(ky_block, dtype=jnp.int32), y_count)
    freq_x = freq_at(kx_start + jnp.arange(x_block, dtype=jnp.int32), x_count)
    freq_z = freq_at(jnp.arange(z_count, dtype=jnp.int32), z_count)
    kernel = make_kernel(
        coef,
        (freq_y[:, None, None], freq_x[None, :, None], freq_z[None, None, :]),
        (y_count, x_count, z_count),
    )
    real_next = kernel[:, 0] * real_part[0] + kernel[:, 1] * real_part[1]
    imag_next = kernel[:, 0] * imag_part[0] + kernel[:, 1] * imag_part[1]
    real_part = real_next
    imag_part = imag_next
    real_part, imag_part = complex_apply(
        "bkxm,mz->bkxz", real_part, imag_part, zi_cos, zi_sin, -1.0
    )

    def relay_back(values):
        values = values.reshape(batch, ky_block, x_block, pz_count, z_local).transpose(
            0, 1, 3, 2, 4
        )
        return values.reshape(batch, ky_block, pz_count * x_block * z_local)

    real_part = relay_back(real_part)
    imag_part = relay_back(imag_part)
    real_in = lax.all_to_all(real_part, "pz", split_axis=2, concat_axis=1, tiled=True)
    imag_in = lax.all_to_all(imag_part, "pz", split_axis=2, concat_axis=1, tiled=True)
    back_items = real_in.shape[0]
    real_out, imag_out = complex_apply("bkc,ky->byc", real_in, imag_in, yi_cos, yi_sin, -1.0)

    def relay(values):
        values = values.reshape(back_items, y_count, x_block, z_local).transpose(0, 2, 1, 3)
        return values.reshape(back_items, x_block, y_count * z_local)

    real_part = relay(real_out)
    imag_part = relay(imag_out)
    real_in = lax.all_to_all(real_part, "py", split_axis=2, concat_axis=1, tiled=True)
    imag_in = lax.all_to_all(imag_part, "py", split_axis=2, concat_axis=1, tiled=True)
    result = contract("bqs,qx->bsx", real_in, xi_cos) - contract("bqs,qx->bsx", imag_in, xi_sin)
    return (
        result[0].reshape(y_local, z_local, x_count),
        result[1].reshape(y_local, z_local, x_count),
    )


def solution(mesh):
    in_specs = (P("py", "pz", None), P("py", "pz", None), P())
    out_specs = (P("py", "pz", None), P("py", "pz", None))
    return jax.shard_map(shards, mesh=mesh, in_specs=in_specs, out_specs=out_specs, check_vma=False)
```

profile of v0, /device:TPU:0, one launch (start us, length us, event | category | flops | bytes accessed | tf_op | source)
XLA Modules:
  0.0 1785.4 jit_solution(6525902035825200465)
XLA Ops:
  56.9 36.3 %convolution_bitcast_fusion = f32[2,512,2048]{2,1,0:T(8,128)S(1)} fusion(f32[2,2048,512]{2,1,0:T(8,128)} %bitcast.222, s32[512]{0:T(512)S(1)} %fusion.138), kind=kOutput, calls=%fused_computation.64 | convolution fusion | flops 12888571904 | bytes 16779264 | tf_op jit(solution)/shard_map/bsx,xq->bqs/dot_general | solution.py:49
  110.0 48.6 %multiply_bitcast_fusion = f32[2,512,2048]{2,1,0:T(8,128)S(1)} fusion(f32[2,2048,512]{2,1,0:T(8,128)} %bitcast.223, s32[512]{0:T(512)S(1)} %fusion.138), kind=kOutput, calls=%fused_computation.54 | convolution fusion | flops 12890669056 | bytes 16779264 | tf_op jit(solution)/shard_map/bsx,xq->bqs/dot_general | solution.py:49
  169.8 33.0 %all-to-all-done = f32[2,512,2048]{2,0,1:T(2,128)} async-done(((f32[2,512,2048]{2,0,1:T(2,128)}), f32[2,512,2048]{2,0,1:T(2,128)}, u32[]{:S(2)}, u32[]{:S(2)}) %all-to-all-start) | async-done | bytes 8388640 | tf_op jit(solution)/shard_map/all_to_all | solution.py:95
  239.1 62.9 %all-to-all-done.1 = f32[2,512,2048]{2,0,1:T(2,128)} async-done(((f32[2,512,2048]{2,0,1:T(2,128)}), f32[2,512,2048]{2,0,1:T(2,128)}, u32[]{:S(2)}, u32[]{:S(2)}) %all-to-all-start.1) | async-done | bytes 8388640 | tf_op jit(solution)/shard_map/all_to_all | solution.py:96
  406.5 150.7 %all-to-all-done.2 = f32[2,256,4096]{2,0,1:T(2,128)} async-done(((f32[2,256,4096]{2,0,1:T(2,128)}), f32[2,256,4096]{2,0,1:T(2,128)}, u32[]{:S(2)}, u32[]{:S(2)}) %all-to-all-start.2) | async-done | bytes 8388640 | tf_op jit(solution)/shard_map/all_to_all | solution.py:106
  564.1 58.6 %fusion.10 = f32[2,2,32,128,256]{4,1,0,3,2:T(2,128)} fusion(f32[8]{0:T(128)S(1)} %add_multiply_fusion, f32[32,128,256]{2,1,0:T(8,128)S(1)} %sqrt_multiply_fusion, f32[2,2,8]{2,1,0:T(2,128)S(1)} %copy-done), kind=kOutput, calls=%fused_computation.19 | convolution fusion | flops 436207616 | bytes 20971680 | tf_op jit(solution)/shard_map/abr,rkxm->abkxm/dot_general | solution.py:68
  622.7 20.1 %fusion.246 = (f32[2,1,32,128,256]{4,1,0,3,2:T(1,128)}, f32[2,1,32,128,256]{4,1,0,3,2:T(1,128)}) fusion(f32[2,2,32,128,256]{4,1,0,3,2:T(2,128)} %fusion.10), kind=kLoop, calls=%fused_computation.302 | loop fusion | bytes 33554432 | tf_op jit(solution)/shard_map/slice | solution.py:129
  654.3 20.1 %reshape.291 = f32[2,32,8,128,32]{4,3,2,1,0:T(8,128)} reshape(f32[2,32,8,4096]{3,2,1,0:T(8,128)} %bitcast.231) | data formatting | bytes 16777216 | tf_op jit(solution)/shard_map/reshape | solution.py:111
  674.5 21.7 %copy.133 = f32[2,32,128,8,32]{2,4,3,1,0:T(8,128)} copy(f32[2,32,128,8,32]{4,2,3,1,0:T(8,128)} %bitcast.202) | data formatting | bytes 16777216 | tf_op jit(solution)/shard_map/transpose | solution.py:111
  696.2 19.7 %fusion.90 = f32[2,32,128,256]{3,2,1,0:T(8,128)} fusion(f32[2,32,128,256]{2,3,1,0:T(8,128)} %bitcast.212, s32[256]{0:T(256)S(1)} %compare_select_fusion.8), kind=kOutput, calls=%fused_computation.129 | convolution fusion | flops 6443368448 | bytes 16778240 | tf_op jit(solution)/shard_map/bkxz,zm->bkxm/dot_general | solution.py:49
  715.9 30.5 %all-to-all-done.3 = f32[2,256,4096]{2,0,1:T(2,128)} async-done(((f32[2,256,4096]{2,0,1:T(2,128)}), f32[2,256,4096]{2,0,1:T(2,128)}, u32[]{:S(2)}, u32[]{:S(2)}) %all-to-all-start.3) | async-done | bytes 8388640 | tf_op jit(solution)/shard_map/all_to_all | solution.py:107
  757.9 20.1 %reshape.293 = f32[2,32,8,128,32]{4,3,2,1,0:T(8,128)} reshape(f32[2,32,8,4096]{3,2,1,0:T(8,128)} %bitcast.232) | data formatting | bytes 16777216 | tf_op jit(solution)/shard_map/reshape | solution.py:111
  778.0 21.7 %copy.140 = f32[2,32,128,8,32]{2,4,3,1,0:T(8,128)} copy(f32[2,32,128,8,32]{4,2,3,1,0:T(8,128)} %bitcast.203) | data formatting | bytes 16777216 | tf_op jit(solution)/shard_map/transpose | solution.py:111
  799.7 19.4 %fusion.88 = f32[2,32,128,256]{3,2,1,0:T(8,128)S(1)} fusion(f32[2,32,128,256]{2,3,1,0:T(8,128)} %bitcast.216, s32[256]{0:T(256)S(1)} %compare_select_fusion.8), kind=kOutput, calls=%fused_computation.127 | convolution fusion | flops 6443368448 | bytes 16778240 | tf_op jit(solution)/shard_map/bkxz,zm->bkxm/dot_general | solution.py:49
  819.2 21.1 %convolution_add_fusion = f32[2,32,128,256]{3,2,1,0:T(8,128)} fusion(f32[2,32,128,256]{3,2,1,0:T(8,128)} %fusion.90, f32[2,32,128,256]{2,3,1,0:T(8,128)S(1)} %bitcast.217, s32[256]{0:T(256)S(1)} %compare_select_fusion.8), kind=kOutput, calls=%fused_computation.71 | convolution fusion | flops 6445465600 | bytes 25166848 | tf_op jit(solution)/shard_map/bkxz,zm->bkxm/dot_general | solution.py:49
  866.1 30.2 %fusion.27 = (f32[2,32,128,256]{3,0,2,1:T(2,128)}, f32[2,32,128,256]{3,0,2,1:T(2,128)}) fusion(f32[2,1,32,128,256]{4,1,0,3,2:T(1,128)} %get-tuple-element.5, f32[2,1,32,128,256]{4,1,0,3,2:T(1,128)} %get-tuple-element.4, f32[32,128,256]{2,1,0:T(8,128)} %get-tuple-element.20, f32[32,128,256]{2,1,0:T(8,128)} %get-tuple-element.21, ...), kind=kLoop, calls=%fused_computation.44 | loop fusion | flops 12582912 | bytes 50331648 | tf_op jit(solution)/shard_map/add | solution.py:129
  929.7 28.6 %copy.203 = f32[2,32,8,128,32]{1,0,4,3,2:T(2,128)} copy(f32[2,32,8,128,32]{3,4,2,1,0:T(8,128)} %bitcast.233) | data formatting | bytes 16777216 | tf_op jit(solution)/shard_map/reshape | solution.py:141
  958.3 35.4 %reshape.323 = f32[8,1,262144]{2,1,0:T(1,128)} reshape(f32[32768,2,32]{2,1,0:T(2,128)} %bitcast.204) | data formatting | bytes 16777216
  1034.7 28.6 %copy.208 = f32[2,32,8,128,32]{1,0,4,3,2:T(2,128)} copy(f32[2,32,8,128,32]{3,4,2,1,0:T(8,128)} %bitcast.234) | data formatting | bytes 16777216 | tf_op jit(solution)/shard_map/reshape | solution.py:141
  1063.4 35.8 %reshape.321 = f32[8,1,262144]{2,1,0:T(1,128)} reshape(f32[32768,2,32]{2,1,0:T(2,128)} %bitcast.205) | data formatting | bytes 16777216
  1099.2 83.5 %all-to-all-done.4 = f32[8,1,262144]{2,1,0:T(1,128)} async-done(((f32[8,1,262144]{2,1,0:T(1,128)}), f32[8,1,262144]{2,1,0:T(1,128)}, u32[]{:S(2)}, u32[]{:S(2)}) %all-to-all-start.4) | async-done | bytes 8388640 | tf_op jit(solution)/shard_map/all_to_all | solution.py:145
  1188.2 28.2 %reduce.1 = f32[8,262144]{1,0:T(8,128)} reduce(f32[8,1,262144]{2,1,0:T(1,128)} %all-to-all-done.4, f32[]{:T(128)} %broadcast.767), dimensions={1}, to_apply=%all_to_all.108.reduce_sub_computation | reduce | bytes 16777220 | tf_op jit(solution)/shard_map/all_to_all | solution.py:145
  1216.4 55.1 %reshape.324 = f32[32768,2,32]{2,1,0:T(2,128)} reshape(f32[8,262144]{1,0:T(8,128)} %reduce.1) | data formatting | bytes 16777216
  1271.4 40.0 %copy.205 = f32[2,32,8,4096]{3,1,2,0:T(8,128)} copy(f32[2,32,8,4096]{1,0,3,2:T(2,128)} %bitcast.206) | data formatting | bytes 16777216 | tf_op jit(solution)/shard_map/all_to_all | solution.py:145
  1311.4 60.1 %all-to-all-done.5 = f32[8,1,262144]{2,1,0:T(1,128)} async-done(((f32[8,1,262144]{2,1,0:T(1,128)}), f32[8,1,262144]{2,1,0:T(1,128)}, u32[]{:S(2)}, u32[]{:S(2)}) %all-to-all-start.5) | async-done | bytes 8388640 | tf_op jit(solution)/shard_map/all_to_all | solution.py:146
  1371.5 28.2 %reduce = f32[8,262144]{1,0:T(8,128)} reduce(f32[8,1,262144]{2,1,0:T(1,128)} %all-to-all-done.5, f32[]{:T(128)} %broadcast.767), dimensions={1}, to_apply=%all_to_all.112.reduce_sub_computation | reduce | bytes 16777220 | tf_op jit(solution)/shard_map/all_to_all | solution.py:146
  1399.7 54.9 %reshape.322 = f32[32768,2,32]{2,1,0:T(2,128)} reshape(f32[8,262144]{1,0:T(8,128)} %reduce) | data formatting | bytes 16777216
  1454.6 40.0 %copy.210 = f32[2,32,8,4096]{3,1,2,0:T(8,128)} copy(f32[2,32,8,4096]{1,0,3,2:T(2,128)} %bitcast.207) | data formatting | bytes 16777216 | tf_op jit(solution)/shard_map/all_to_all | solution.py:146
  1623.6 30.8 %all-to-all-done.7 = f32[2,128,8192]{1,0,2:T(2,128)} async-done(((f32[2,128,8192]{1,0,2:T(2,128)}), f32[2,128,8192]{1,0,2:T(2,128)}, u32[]{:S(2)}, u32[]{:S(2)}) %all-to-all-start.7) | async-done | bytes 8388640 | tf_op jit(solution)/shard_map/all_to_all | solution.py:157
  1664.1 20.1 %fusion.20 = f32[2,2048,512]{2,1,0:T(8,128)} fusion(f32[2,4,256,8,128]{4,3,2,1,0:T(8,128)S(1)} %bitcast.243, s32[512]{0:T(512)S(1)} %copy-done.10), kind=kOutput, calls=%fused_computation.31 | convolution fusion | flops 12888834048 | bytes 16779264 | tf_op jit(solution)/shard_map/bqs,qx->bsx/dot_general | solution.py:49
  1684.1 67.9 %all-to-all-done.6 = f32[2,128,8192]{1,0,2:T(2,128)} async-done(((f32[2,128,8192]{1,0,2:T(2,128)}), f32[2,128,8192]{1,0,2:T(2,128)}, u32[]{:S(2)}, u32[]{:S(2)}) %all-to-all-start.6) | async-done | bytes 8388640 | tf_op jit(solution)/shard_map/all_to_all | solution.py:156
  1759.7 21.1 %fusion.37 = f32[2,2048,512]{2,1,0:T(8,128)S(1)} fusion(f32[2,2048,512]{2,1,0:T(8,128)S(1)} %copy-done.7, f32[2,4,256,8,128]{4,3,2,1,0:T(8,128)} %bitcast.230, s32[512]{0:T(512)S(1)} %copy-done.10), kind=kOutput, calls=%fused_computation.69 | convolution fusion | flops 12890931200 | bytes 25167872 | tf_op jit(solution)/shard_map/bqs,qx->bsx/dot_general | solution.py:49
  (97 shorter events, 510.9 us)
Async XLA Ops:
  0.6 563.5 %copy-start = (f32[2,2,8]{2,1,0:T(2,128)S(1)}, f32[2,2,8]{2,1,0:T(2,128)}, u32[]{:S(2)}) copy-start(f32[2,2,8]{2,1,0:T(2,128)} %param.5) | copy-start | bytes 388
  0.6 13.7 copy-start.5
  0.7 13.6 copy-start.6
  25.9 8.3 collective-permute-start
  29.0 7.5 collective-permute-start.1
  37.0 8.5 collective-permute-start.2
  37.1 8.5 collective-permute-start.3
  40.6 69.3 %copy-start.9 = (s32[512]{0:T(512)}, s32[512]{0:T(512)S(1)}, u32[]{:S(2)}) copy-start(s32[512]{0:T(512)S(1)} %fusion.138) | copy-start | bytes 6148
  104.3 98.5 %all-to-all-start = ((f32[2,512,2048]{2,0,1:T(2,128)}), f32[2,512,2048]{2,0,1:T(2,128)}, u32[]{:S(2)}, u32[]{:S(2)}) async-start(f32[2,512,2048]{2,0,1:T(2,128)} %copy.120), calls=%async_computation | async-start | bytes 16777216 | tf_op jit(solution)/shard_map/all_to_all | solution.py:95
  202.8 99.2 %all-to-all-start.1 = ((f32[2,512,2048]{2,0,1:T(2,128)}), f32[2,512,2048]{2,0,1:T(2,128)}, u32[]{:S(2)}, u32[]{:S(2)}) async-start(f32[2,512,2048]{2,0,1:T(2,128)} %copy.126), calls=%async_computation.1 | async-start | bytes 16777216 | tf_op jit(solution)/shard_map/all_to_all | solution.py:96
  332.7 13.9 copy-start.3
  368.1 189.0 %all-to-all-start.2 = ((f32[2,256,4096]{2,0,1:T(2,128)}), f32[2,256,4096]{2,0,1:T(2,128)}, u32[]{:S(2)}, u32[]{:S(2)}) async-start(f32[2,256,4096]{2,0,1:T(2,128)} %copy.131), calls=%async_computation.2 | async-start | bytes 16777216 | tf_op jit(solution)/shard_map/all_to_all | solution.py:106
  557.1 189.2 %all-to-all-start.3 = ((f32[2,256,4096]{2,0,1:T(2,128)}), f32[2,256,4096]{2,0,1:T(2,128)}, u32[]{:S(2)}, u32[]{:S(2)}) async-start(f32[2,256,4096]{2,0,1:T(2,128)} %copy.138), calls=%async_computation.3 | async-start | bytes 16777216 | tf_op jit(solution)/shard_map/all_to_all | solution.py:107
  799.7 19.4 %copy-start.2 = (f32[2,32,128,8,32]{2,4,3,1,0:T(8,128)S(1)}, f32[2,32,128,8,32]{2,4,3,1,0:T(8,128)}, u32[]{:S(2)}) copy-start(f32[2,32,128,8,32]{2,4,3,1,0:T(8,128)} %copy.140) | copy-start | bytes 25165828
  799.7 40.6 %slice-start = ((s8[8388608]{0:T(1024)(128)(4,1)}), s8[4194304]{0:T(1024)(128)(4,1)S(1)}, s32[]{:S(2)}) async-start(s8[8388608]{0:T(1024)(128)(4,1)} %bitcast.213), calls=%async_computation.8 | async-start | bytes 8388608
  819.1 21.2 %slice-start.1 = ((s8[8388608]{0:T(1024)(128)(4,1)}), s8[4194304]{0:T(1024)(128)(4,1)S(1)}, s32[]{:S(2)}) async-start(s8[8388608]{0:T(1024)(128)(4,1)} %bitcast.213), calls=%async_computation.9 | async-start | bytes 8388608
  840.3 18.4 %copy-start.8 = (f32[2,32,128,256]{3,2,1,0:T(8,128)S(1)}, f32[2,32,128,256]{3,2,1,0:T(8,128)}, u32[]{:S(2)}) copy-start(f32[2,32,128,256]{3,2,1,0:T(8,128)} %convolution_add_fusion) | copy-start | bytes 25165828
  896.4 13.0 copy-start.4
  993.7 189.0 %all-to-all-start.4 = ((f32[8,1,262144]{2,1,0:T(1,128)}), f32[8,1,262144]{2,1,0:T(1,128)}, u32[]{:S(2)}, u32[]{:S(2)}) async-start(f32[8,1,262144]{2,1,0:T(1,128)} %reshape.323), calls=%async_computation.4 | async-start | bytes 16777216 | tf_op jit(solution)/shard_map/all_to_all | solution.py:145
  1182.7 188.8 %all-to-all-start.5 = ((f32[8,1,262144]{2,1,0:T(1,128)}), f32[8,1,262144]{2,1,0:T(1,128)}, u32[]{:S(2)}, u32[]{:S(2)}) async-start(f32[8,1,262144]{2,1,0:T(1,128)} %reshape.321), calls=%async_computation.5 | async-start | bytes 16777216 | tf_op jit(solution)/shard_map/all_to_all | solution.py:146
  1556.3 98.2 %all-to-all-start.7 = ((f32[2,128,8192]{1,0,2:T(2,128)}), f32[2,128,8192]{1,0,2:T(2,128)}, u32[]{:S(2)}, u32[]{:S(2)}) async-start(f32[2,128,8192]{1,0,2:T(2,128)} %copy.172), calls=%async_computation.7 | async-start | bytes 16777216 | tf_op jit(solution)/shard_map/all_to_all | solution.py:157
  1654.4 97.6 %all-to-all-start.6 = ((f32[2,128,8192]{1,0,2:T(2,128)}), f32[2,128,8192]{1,0,2:T(2,128)}, u32[]{:S(2)}, u32[]{:S(2)}) async-start(f32[2,128,8192]{1,0,2:T(2,128)} %copy.167), calls=%async_computation.6 | async-start | bytes 16777216 | tf_op jit(solution)/shard_map/all_to_all | solution.py:156
  1660.1 3.9 copy-start.10
  1752.0 7.7 copy-start.7
  1759.7 25.5 %copy-start.1 = (f32[2,2,8]{2,1,0:T(2,128)S(1)}, f32[2,2,8]{2,1,0:T(2,128)}, u32[]{:S(2)}) copy-start(f32[2,2,8]{2,1,0:T(2,128)} %param.5) | copy-start | bytes 388
where the time goes:
time: 1800 us; the launch traced here: 1790 us
  local copies, waits for them, and re-layouts  661 us (37%)
  waiting for transfers between devices  531 us (30%)
  matrix products  416 us (23%)
  other arithmetic  125 us (7%)
  starting transfers between devices  51 us (3%)
    dot_general x20, matrix products, contract(): return jnp.einsum(form, data, table, precision=HIGH)  357 us
    unnamed x30, local copies, waits for them, and re-layouts  181 us
    all_to_all x1, waiting for transfers between devices, shards(): lax.all_to_all(real_part, 'pz', split_axis=1, concat_axis=2, tiled=True)  151 us
    all_to_all x1, waiting for transfers between devices, shards(): lax.all_to_all(real_part, 'pz', split_axis=2, concat_axis=1, tiled=True)  83.5 us
    all_to_all x1, waiting for transfers between devices, shards(): lax.all_to_all(real_part, 'py', split_axis=2, concat_axis=1, tiled=True)  67.9 us
    all_to_all x1, waiting for transfers between devices, shards(): lax.all_to_all(imag_part, 'py', split_axis=1, concat_axis=2, tiled=True)  62.9 us
    all_to_all x1, waiting for transfers between devices, shards(): lax.all_to_all(imag_part, 'pz', split_axis=2, concat_axis=1, tiled=True)  60.1 us
    dot_general x1, matrix products, make_kernel(): kernel = jnp.einsum('abr,rkxm->abkxm', coef, basis, precision=HIGH)  58.6 us
  transfers between devices with their start and end apart: 12, of which 11 were waited for; matrix products, arithmetic and copies ran while one was open for 33% of the time, Pallas kernels for 0%

commit v1 on v0

v1 whole, which is shorter than its diff:
```python
import jax
import jax.numpy as jnp
import numpy as np
from jax import lax
from jax.sharding import PartitionSpec as P

HIGH = lax.Precision.HIGHEST
AXES = ("py", "pz")


def channel_freq(length):
    channel = np.arange(length)
    return np.where(channel == 1, length // 2, channel // 2)


def real_table(length):
    freq = channel_freq(length)
    phase = (freq[:, None] * np.arange(length)[None, :]) % length
    angle = 2.0 * np.pi / length * phase
    odd = (np.arange(length) % 2 == 1) & (np.arange(length) > 1)
    single = np.arange(length) < 2
    table = np.where(odd[:, None], np.sin(angle), np.cos(angle))
    return (table * np.sqrt(np.where(single, 1.0, 2.0) / length)[:, None]).astype(np.float32)


def spline(freq, length):
    return (4.0 + 2.0 * jnp.cos(2.0 * jnp.pi / length * freq.astype(jnp.float32))) / 6.0


def make_kernel(coef, freqs, lengths):
    scaled = [freq.astype(jnp.float32) / length for freq, length in zip(freqs, lengths)]
    ratio = 4.0 * (scaled[0] ** 2 + scaled[1] ** 2 + scaled[2] ** 2) / 3.0
    volume = ratio * jnp.sqrt(ratio)
    smooth = spline(freqs[0], lengths[0]) * spline(freqs[1], lengths[1]) * spline(freqs[2], lengths[2])
    count = coef.shape[2]
    total = [[0.0, 0.0], [0.0, 0.0]]
    for index in range(count):
        basis = jnp.exp(-jnp.square((volume - (index + 0.5) / count) * count))
        for a in range(2):
            for b in range(2):
                total[a][b] = total[a][b] + coef[a, b, index] * basis
    return [[total[a][b] * smooth for b in range(2)] for a in range(2)]


def shards(field_one, field_two, coef):
    y_local, z_local, x_count = field_one.shape
    py_count = lax.axis_size("py")
    pz_count = lax.axis_size("pz")
    y_count = y_local * py_count
    z_count = z_local * pz_count
    world = py_count * pz_count
    per_device = x_count // world
    groups = min(2, per_device)
    rows = per_device // groups
    fields = (field_one, field_two)
    x_table = real_table(x_count).reshape(world, groups, rows, x_count)
    y_table = jnp.asarray(real_table(y_count))
    z_table = jnp.asarray(real_table(z_count))
    me = lax.axis_index("py") * pz_count + lax.axis_index("pz")
    freq_y = jnp.asarray(channel_freq(y_count))
    freq_z = jnp.asarray(channel_freq(z_count))

    arrived = []
    for group in range(groups):
        table = jnp.asarray(x_table[:, group].reshape(world * rows, x_count))
        pair = []
        for field in fields:
            spectrum = jnp.einsum("qx,yzx->qyz", table, field, precision=HIGH)
            spectrum = spectrum.reshape(world, rows, y_local * z_local)
            pair.append(lax.all_to_all(spectrum, AXES, split_axis=0, concat_axis=0, tiled=True))
        arrived.append(pair)

    sent_back = []
    for group in range(groups):
        channel = me * per_device + group * rows + jnp.arange(rows)
        freq_x = jnp.where(channel == 1, x_count // 2, channel // 2)
        kernel = make_kernel(
            coef,
            (freq_y[None, :, None], freq_z[None, None, :], freq_x[:, None, None]),
            (y_count, z_count, x_count),
        )
        spectra = []
        for value in arrived[group]:
            value = value.reshape(py_count, pz_count, rows, y_local, z_local)
            value = value.transpose(2, 0, 3, 1, 4).reshape(rows, y_count, z_count)
            value = jnp.einsum("ryz,mz->rym", value, z_table, precision=HIGH)
            spectra.append(jnp.einsum("rym,ky->rkm", value, y_table, precision=HIGH))
        pair = []
        for a in range(2):
            value = kernel[a][0] * spectra[0] + kernel[a][1] * spectra[1]
            value = jnp.einsum("rkm,ky->rym", value, y_table, precision=HIGH)
            value = jnp.einsum("rym,mz->ryz", value, z_table, precision=HIGH)
            value = value.reshape(rows, py_count, y_local, pz_count, z_local).transpose(1, 3, 0, 2, 4)
            value = value.reshape(world, rows, y_local * z_local)
            pair.append(lax.all_to_all(value, AXES, split_axis=0, concat_axis=0, tiled=True))
        sent_back.append(pair)

    results = []
    for a in range(2):
        total = None
        for group in range(groups):
            table = jnp.asarray(x_table[:, group].reshape(world * rows, x_count))
            value = sent_back[group][a].reshape(world * rows, y_local, z_local)
            part = jnp.einsum("qyz,qx->yzx", value, table, precision=HIGH)
            total = part if total is None else total + part
        results.append(total)
    return tuple(results)


def solution(mesh):
    in_specs = (P("py", "pz", None), P("py", "pz", None), P())
    out_specs = (P("py", "pz", None), P("py", "pz", None))
    return jax.shard_map(shards, mesh=mesh, in_specs=in_specs, out_specs=out_specs, check_vma=False)
```

time: 1800 us -> 621 us (0.34)
  waiting for transfers between devices: 531 us -> 93.7 us
  local copies, waits for them, and re-layouts: 661 us -> 246 us
  matrix products: 416 us -> 233 us
  other arithmetic: 125 us -> 0.24 us
    all_to_all x8, waiting for transfers between devices: 519 us -> 93.7 us  [the longest x4 81.3 us: shards(): lax.all_to_all(spectrum, AXES, split_axis=0, concat_axis=0, tiled=True)]
    dot_general x21 -> x24, matrix products: 416 us -> 233 us  [the longest x4 92.3 us: shards(): part = jnp.einsum('qyz,qx->yzx', value, table, precision=HIGH)]
    unnamed x30 -> x36, local copies, waits for them, and re-layouts: 181 us -> 1.45 us
    all_to_all x11 -> x0, local copies, waits for them, and re-layouts: 156 us -> none  [the longest x2 40.5 us: shards(): lax.all_to_all(imag_part, 'pz', split_axis=2, concat_axis=1, tiled=True)]
    all_to_all x2 -> x0, other arithmetic: 56.3 us -> none  [the longest x1 28.2 us: shards(): lax.all_to_all(imag_part, 'pz', split_axis=2, concat_axis=1, tiled=True)]
    transpose x7 -> x8, local copies, waits for them, and re-layouts: 97.6 us -> 62.3 us  [the longest x4 31.2 us: shards(): value.reshape(rows, py_count, y_local, pz_count, z_local)]
    dot_general x0 -> x4, local copies, waits for them, and re-layouts: none -> 30.4 us  [shards(): spectrum = jnp.einsum('qx,yzx->qyz', table, field, precision=HIGH)]
    add x2 -> x0, other arithmetic: 30.3 us -> none  [the longest x1 30.2 us: shards(): real_next = kernel[:, 0] * real_part[0] + kernel[:, 1] * real_part[1]]
  transfers between devices with their start and end apart: 12 -> 8, of which waited for: 11 -> 5; matrix products, arithmetic and copies ran while one was open for 33% -> 69% of each run, Pallas kernels for 0% -> 0%
where the time goes in v1:
time: 621 us; the launch traced here: 612 us
  local copies, waits for them, and re-layouts  246 us (40%)
  matrix products  233 us (38%)
  waiting for transfers between devices  93.7 us (15%)
  starting transfers between devices  37.3 us (6%)
    dot_general x4, matrix products, shards(): part = jnp.einsum('qyz,qx->yzx', value, table, precision=HIGH)  92.3 us
    all_to_all x4, waiting for transfers between devices, shards(): lax.all_to_all(spectrum, AXES, split_axis=0, concat_axis=0, tiled=True)  81.3 us
    dot_general x4, matrix products, shards(): value = jnp.einsum('rkm,ky->rym', value, y_table, precision=HIGH)  76.9 us
    dot_general x4, matrix products, shards(): spectrum = jnp.einsum('qx,yzx->qyz', table, field, precision=HIGH)  31.3 us
    transpose x4, local copies, waits for them, and re-layouts, shards(): value.reshape(rows, py_count, y_local, pz_count, z_local)  31.2 us
    transpose x4, local copies, waits for them, and re-layouts, shards(): value = value.transpose(2, 0, 3, 1, 4).reshape(rows, y_count, z_count)  31.1 us
    dot_general x4, local copies, waits for them, and re-layouts, shards(): spectrum = jnp.einsum('qx,yzx->qyz', table, field, precision=HIGH)  30.4 us
    reshape x4, local copies, waits for them, and re-layouts, shards(): value = value.reshape(world, rows, y_local * z_local)  30 us
  transfers between devices with their start and end apart: 8, of which 5 were waited for; matrix products, arithmetic and copies ran while one was open for 69% of the time, Pallas kernels for 0%

profile of v1, /device:TPU:0, one launch (start us, length us, event | category | flops | bytes accessed | tf_op | source)
XLA Modules:
  0.0 611.8 jit_solution(5428284861449269264)
XLA Ops:
  0.6 7.9 %fusion.12 = f32[256,64,32]{0,1,2:T(8,128)S(1)} fusion(f32[256,512,1]{1,0,2:T(8,128)} %constant.129, f32[64,32,512]{2,1,0:T(8,128)} %param.13), kind=kOutput, calls=%fused_computation.20 | convolution fusion | flops 3221225472 | bytes 6815744 | tf_op jit(solution)/shard_map/qx,yzx->qyz/dot_general | solution.py:68
  8.6 7.6 %copy.29 = f32[256,64,32]{2,1,0:T(8,128)} copy(f32[256,64,32]{0,1,2:T(8,128)S(1)} %fusion.12) | data formatting | bytes 4194304 | tf_op jit(solution)/shard_map/qx,yzx->qyz/dot_general | solution.py:68
  16.2 7.5 %reshape.243 = f32[32,8,2048]{2,1,0:T(8,128)} reshape(f32[256,64,32]{2,1,0:T(8,128)} %copy.29) | data formatting | bytes 4194304 | tf_op jit(solution)/shard_map/reshape | solution.py:69
  23.7 7.6 %all-to-all-start.3 = ((f32[32,8,2048]{2,1,0:T(8,128)}), f32[32,8,2048]{2,1,0:T(8,128)}, u32[]{:S(2)}, u32[]{:S(2)}) async-start(f32[32,8,2048]{2,1,0:T(8,128)} %reshape.243), calls=%async_computation.3 | async-start | bytes 4194304 | tf_op jit(solution)/shard_map/all_to_all | solution.py:70
  31.3 7.8 %fusion.8 = f32[256,64,32]{0,1,2:T(8,128)S(1)} fusion(f32[256,512,1]{1,0,2:T(8,128)S(1)} %copy-done.4, f32[64,32,512]{2,1,0:T(8,128)} %param.14), kind=kOutput, calls=%fused_computation.16 | convolution fusion | flops 3221225472 | bytes 6815744 | tf_op jit(solution)/shard_map/qx,yzx->qyz/dot_general | solution.py:68
  39.1 7.6 %copy.32 = f32[256,64,32]{2,1,0:T(8,128)} copy(f32[256,64,32]{0,1,2:T(8,128)S(1)} %fusion.8) | data formatting | bytes 4194304 | tf_op jit(solution)/shard_map/qx,yzx->qyz/dot_general | solution.py:68
  54.2 27.1 %all-to-all-done.3 = f32[32,8,2048]{2,1,0:T(8,128)} async-done(((f32[32,8,2048]{2,1,0:T(8,128)}), f32[32,8,2048]{2,1,0:T(8,128)}, u32[]{:S(2)}, u32[]{:S(2)}) %all-to-all-start.3) | async-done | bytes 2097184 | tf_op jit(solution)/shard_map/all_to_all | solution.py:70
  84.8 7.8 %fusion.14 = f32[256,64,32]{0,1,2:T(8,128)S(1)} fusion(f32[256,512,1]{1,0,2:T(8,128)S(1)} %copy-done.2, f32[64,32,512]{2,1,0:T(8,128)} %param.13), kind=kOutput, calls=%fused_computation.22 | convolution fusion | flops 3221225472 | bytes 6815744 | tf_op jit(solution)/shard_map/qx,yzx->qyz/dot_general | solution.py:68
  92.6 7.6 %copy.20 = f32[256,64,32]{2,1,0:T(8,128)} copy(f32[256,64,32]{0,1,2:T(8,128)S(1)} %fusion.14) | data formatting | bytes 4194304 | tf_op jit(solution)/shard_map/qx,yzx->qyz/dot_general | solution.py:68
  107.7 27.1 %all-to-all-done.4 = f32[32,8,2048]{2,1,0:T(8,128)} async-done(((f32[32,8,2048]{2,1,0:T(8,128)}), f32[32,8,2048]{2,1,0:T(8,128)}, u32[]{:S(2)}, u32[]{:S(2)}) %all-to-all-start.4) | async-done | bytes 2097184 | tf_op jit(solution)/shard_map/all_to_all | solution.py:70
  138.7 7.8 %fusion.10 = f32[256,64,32]{0,1,2:T(8,128)S(1)} fusion(f32[256,512,1]{1,0,2:T(8,128)S(1)} %copy-done.2, f32[64,32,512]{2,1,0:T(8,128)} %param.14), kind=kOutput, calls=%fused_computation.18 | convolution fusion | flops 3221225472 | bytes 6815744 | tf_op jit(solution)/shard_map/qx,yzx->qyz/dot_general | solution.py:68
  146.5 7.6 %copy.23 = f32[256,64,32]{2,1,0:T(8,128)} copy(f32[256,64,32]{0,1,2:T(8,128)S(1)} %fusion.10) | data formatting | bytes 4194304 | tf_op jit(solution)/shard_map/qx,yzx->qyz/dot_general | solution.py:68
  154.1 7.5 %reshape.237 = f32[32,8,2048]{2,1,0:T(8,128)} reshape(f32[256,64,32]{2,1,0:T(8,128)} %copy.23) | data formatting | bytes 4194304 | tf_op jit(solution)/shard_map/reshape | solution.py:69
  161.6 27.1 %all-to-all-done = f32[32,8,2048]{2,1,0:T(8,128)} async-done(((f32[32,8,2048]{2,1,0:T(8,128)}), f32[32,8,2048]{2,1,0:T(8,128)}, u32[]{:S(2)}, u32[]{:S(2)}) %all-to-all-start) | async-done | bytes 2097184 | tf_op jit(solution)/shard_map/all_to_all | solution.py:70
  199.4 7.8 %copy.30 = f32[8,4,64,8,32]{2,1,4,3,0:T(4,128)} copy(f32[8,4,64,8,32]{4,2,0,3,1:T(8,128)} %bitcast.147) | data formatting | bytes 4194304 | tf_op jit(solution)/shard_map/transpose | solution.py:85
  218.8 7.8 %copy.33 = f32[8,4,64,8,32]{2,1,4,3,0:T(4,128)} copy(f32[8,4,64,8,32]{4,2,0,3,1:T(8,128)} %bitcast.148) | data formatting | bytes 4194304 | tf_op jit(solution)/shard_map/transpose | solution.py:85
  241.6 18.5 %fusion.42 = f32[8,256,256]{1,2,0:T(8,128)S(1)} fusion(f32[256,256,1]{1,0,2:T(8,128)S(1)} %copy-done, f32[8,256,256]{2,1,0:T(8,128)S(1)} %fusion.351, f32[8,256,256]{2,1,0:T(8,128)S(1)} %fusion.349, f32[]{:T(128)} %bitcast.46, f32[]{:T(128)} %bitcast.45, f32[]{:T(128)} %bitcast.44, f32[]{:T(128)} %bitcast.43, f32[]{:T(128)} %bitcast.42, f32[]{:T(128)} %bitcast.41, ...), kind=kOutput, calls=%fused_computation.42 | convolution fusion | flops 1647837184 | bytes 7078016 | tf_op jit(solution)/shard_map/rkm,ky->rym/dot_general | solution.py:91
  268.5 7.8 %copy.41 = f32[4,8,8,64,32]{4,3,2,1,0:T(8,128)} copy(f32[4,8,8,64,32]{3,0,4,1,2:T(4,128)} %bitcast.153) | data formatting | bytes 4194304 | tf_op jit(solution)/shard_map/transpose | solution.py:93
  276.3 7.5 %reshape.256 = f32[32,8,2048]{2,1,0:T(8,128)} reshape(f32[4,8,8,64,32]{4,3,2,1,0:T(8,128)} %copy.41) | data formatting | bytes 4194304 | tf_op jit(solution)/shard_map/reshape | solution.py:94
  297.4 7.8 %copy.21 = f32[8,4,64,8,32]{2,1,4,3,0:T(4,128)} copy(f32[8,4,64,8,32]{4,2,0,3,1:T(8,128)} %bitcast.149) | data formatting | bytes 4194304 | tf_op jit(solution)/shard_map/transpose | solution.py:85
  316.8 7.8 %copy.24 = f32[8,4,64,8,32]{2,1,4,3,0:T(4,128)} copy(f32[8,4,64,8,32]{4,2,0,3,1:T(8,128)} %bitcast.150) | data formatting | bytes 4194304 | tf_op jit(solution)/shard_map/transpose | solution.py:85
  339.6 18.3 %fusion.30 = f32[8,256,256]{1,2,0:T(8,128)S(1)} fusion(f32[256,256,1]{1,0,2:T(8,128)S(1)} %copy-done, f32[8,256,256]{2,1,0:T(8,128)S(1)} %fusion.347, f32[8,256,256]{2,1,0:T(8,128)S(1)} %fusion.345, f32[]{:T(128)} %bitcast.46, f32[]{:T(128)} %bitcast.45, f32[]{:T(128)} %bitcast.44, f32[]{:T(128)} %bitcast.43, f32[]{:T(128)} %bitcast.42, f32[]{:T(128)} %bitcast.41, ...), kind=kOutput, calls=%fused_computation.34 | convolution fusion | flops 1647837184 | bytes 7078016 | tf_op jit(solution)/shard_map/rkm,ky->rym/dot_general | solution.py:91
  366.4 7.8 %copy.38 = f32[4,8,8,64,32]{4,3,2,1,0:T(8,128)} copy(f32[4,8,8,64,32]{3,0,4,1,2:T(4,128)} %bitcast.154) | data formatting | bytes 4194304 | tf_op jit(solution)/shard_map/transpose | solution.py:93
  374.2 7.5 %reshape.253 = f32[32,8,2048]{2,1,0:T(8,128)} reshape(f32[4,8,8,64,32]{4,3,2,1,0:T(8,128)} %copy.38) | data formatting | bytes 4194304 | tf_op jit(solution)/shard_map/reshape | solution.py:94
  388.1 20.1 %fusion.36 = f32[8,256,256]{1,2,0:T(8,128)S(1)} fusion(f32[256,256,1]{1,0,2:T(8,128)S(1)} %copy-done, f32[8,256,256]{2,1,0:T(8,128)} %copy-done.10, f32[8,256,256]{2,1,0:T(8,128)} %copy-done.9, f32[8]{0:T(128)S(1)} %get-tuple-element.36, f32[8]{0:T(128)S(1)} %get-tuple-element.37, f32[]{:T(128)} %bitcast.19, f32[]{:T(128)} %bitcast.18, f32[]{:T(128)} %bitcast.17, ...), kind=kOutput, calls=%fused_computation.38 | convolution fusion | flops 1647837184 | bytes 7078016 | tf_op jit(solution)/shard_map/rkm,ky->rym/dot_general | solution.py:91
  416.6 7.8 %copy.35 = f32[4,8,8,64,32]{4,3,2,1,0:T(8,128)} copy(f32[4,8,8,64,32]{3,0,4,1,2:T(4,128)} %bitcast.155) | data formatting | bytes 4194304 | tf_op jit(solution)/shard_map/transpose | solution.py:93
  441.7 20.1 %fusion.24 = f32[8,256,256]{1,2,0:T(8,128)S(1)} fusion(f32[256,256,1]{1,0,2:T(8,128)S(1)} %copy-done, f32[8,256,256]{2,1,0:T(8,128)} %copy-done.12, f32[8,256,256]{2,1,0:T(8,128)} %copy-done.11, f32[]{:T(128)} %bitcast.19, f32[]{:T(128)} %bitcast.18, f32[]{:T(128)} %bitcast.17, f32[]{:T(128)} %bitcast.16, f32[]{:T(128)} %bitcast.15, f32[]{:T(128)} %bitcast.14, ...), kind=kOutput, calls=%fused_computation.30 | convolution fusion | flops 1647837184 | bytes 7078016 | tf_op jit(solution)/shard_map/rkm,ky->rym/dot_general | solution.py:91
  470.2 7.8 %copy.26 = f32[4,8,8,64,32]{4,3,2,1,0:T(8,128)} copy(f32[4,8,8,64,32]{3,0,4,1,2:T(4,128)} %bitcast.156) | data formatting | bytes 4194304 | tf_op jit(solution)/shard_map/transpose | solution.py:93
  512.9 21.6 %fusion = f32[64,32,512]{2,1,0:T(8,128)S(1)} fusion(f32[256,512,1]{1,0,2:T(8,128)S(1)} %copy-done.5, f32[256,64,32]{2,1,0:T(8,128)} %reshape.257), kind=kOutput, calls=%fused_computation | convolution fusion | flops 3221225472 | bytes 6815744 | tf_op jit(solution)/shard_map/qyz,qx->yzx/dot_general | solution.py:104
  534.5 23.4 %fusion.4 = f32[64,32,512]{2,1,0:T(8,128)} fusion(f32[256,512,1]{1,0,2:T(8,128)S(1)} %copy-done.5, f32[256,64,32]{2,1,0:T(8,128)S(1)} %copy-done.1), kind=kOutput, calls=%fused_computation.4 | convolution fusion | flops 3221225472 | bytes 6815744 | tf_op jit(solution)/shard_map/qyz,qx->yzx/dot_general | solution.py:104
  558.0 23.7 %fusion.19 = f32[64,32,512]{2,1,0:T(8,128)} fusion(f32[64,32,512]{2,1,0:T(8,128)S(1)} %fusion, f32[256,512,1]{1,0,2:T(8,128)S(1)} %copy-done.3, f32[256,64,32]{2,1,0:T(8,128)S(1)} %bitcast.152), kind=kOutput, calls=%fused_computation.27 | convolution fusion | flops 3222274048 | bytes 11010048 | tf_op jit(solution)/shard_map/qyz,qx->yzx/dot_general | solution.py:104
  588.0 23.6 %fusion.16 = f32[64,32,512]{2,1,0:T(8,128)} fusion(f32[64,32,512]{2,1,0:T(8,128)} %fusion.4, f32[256,512,1]{1,0,2:T(8,128)S(1)} %copy-done.3, f32[256,64,32]{2,1,0:T(8,128)} %reshape.242), kind=kOutput, calls=%fused_computation.26 | convolution fusion | flops 3222274048 | bytes 11010048 | tf_op jit(solution)/shard_map/qyz,qx->yzx/dot_general | solution.py:104
  (86 shorter events, 198.4 us)
Async XLA Ops:
  23.7 7.7 %copy-start.4 = (f32[256,512,1]{1,0,2:T(8,128)S(1)}, f32[256,512,1]{1,0,2:T(8,128)}, u32[]{:S(2)}) copy-start(f32[256,512,1]{1,0,2:T(8,128)} %constant.129) | copy-start | bytes 1572868
  23.7 57.6 %all-to-all-start.3 = ((f32[32,8,2048]{2,1,0:T(8,128)}), f32[32,8,2048]{2,1,0:T(8,128)}, u32[]{:S(2)}, u32[]{:S(2)}) async-start(f32[32,8,2048]{2,1,0:T(8,128)} %reshape.243), calls=%async_computation.3 | async-start | bytes 4194304 | tf_op jit(solution)/shard_map/all_to_all | solution.py:70
  54.2 30.6 %copy-start.2 = (f32[256,512,1]{1,0,2:T(8,128)S(1)}, f32[256,512,1]{1,0,2:T(8,128)}, u32[]{:S(2)}) copy-start(f32[256,512,1]{1,0,2:T(8,128)} %constant.127) | copy-start | bytes 1572868
  81.3 53.5 %all-to-all-start.4 = ((f32[32,8,2048]{2,1,0:T(8,128)}), f32[32,8,2048]{2,1,0:T(8,128)}, u32[]{:S(2)}, u32[]{:S(2)}) async-start(f32[32,8,2048]{2,1,0:T(8,128)} %reshape.246), calls=%async_computation.4 | async-start | bytes 4194304 | tf_op jit(solution)/shard_map/all_to_all | solution.py:70
  134.8 53.9 %all-to-all-start = ((f32[32,8,2048]{2,1,0:T(8,128)}), f32[32,8,2048]{2,1,0:T(8,128)}, u32[]{:S(2)}, u32[]{:S(2)}) async-start(f32[32,8,2048]{2,1,0:T(8,128)} %reshape.234), calls=%async_computation | async-start | bytes 4194304 | tf_op jit(solution)/shard_map/all_to_all | solution.py:70
  161.6 29.9 %copy-start.13 = (f32[2,2,8]{2,1,0:T(2,128)S(1)}, f32[2,2,8]{2,1,0:T(2,128)}, u32[]{:S(2)}) copy-start(f32[2,2,8]{2,1,0:T(2,128)} %param.15) | copy-start | bytes 388
  161.6 31.3 %copy-start.14 = (f32[256]{0:T(256)S(1)}, f32[256]{0:T(256)}, u32[]{:S(2)}) copy-start(f32[256]{0:T(256)} %constant.121) | copy-start | bytes 3076
  161.6 31.3 %copy-start.15 = (f32[256]{0:T(256)S(1)}, f32[256]{0:T(256)}, u32[]{:S(2)}) copy-start(f32[256]{0:T(256)} %constant.126) | copy-start | bytes 3076
  188.7 95.1 %all-to-all-start.1 = ((f32[32,8,2048]{2,1,0:T(8,128)}), f32[32,8,2048]{2,1,0:T(8,128)S(1)}, u32[]{:S(2)}, u32[]{:S(2)}) async-start(f32[32,8,2048]{2,1,0:T(8,128)} %reshape.237), calls=%async_computation.1 | async-start | bytes 4194304 | tf_op jit(solution)/shard_map/all_to_all | solution.py:70
  226.5 5.5 copy-start
  235.6 1.9 copy-start.7
  237.6 4.0 copy-start.9
  241.6 18.5 %copy-start.10 = (f32[8,256,256]{2,1,0:T(8,128)}, f32[8,256,256]{2,1,0:T(8,128)S(1)}, u32[]{:S(2)}) copy-start(f32[8,256,256]{2,1,0:T(8,128)S(1)} %fusion.351) | copy-start | bytes 6291460
  283.8 1.4 copy-start.6
  285.2 96.4 %all-to-all-start.7 = ((f32[32,8,2048]{2,1,0:T(8,128)}), f32[32,8,2048]{2,1,0:T(8,128)S(1)}, u32[]{:S(2)}, u32[]{:S(2)}) async-start(f32[32,8,2048]{2,1,0:T(8,128)} %reshape.256), calls=%async_computation.7 | async-start | bytes 4194304 | tf_op jit(solution)/shard_map/all_to_all | solution.py:95
  333.7 2.0 copy-start.8
  335.6 4.0 copy-start.11
  339.6 18.3 %copy-start.12 = (f32[8,256,256]{2,1,0:T(8,128)}, f32[8,256,256]{2,1,0:T(8,128)S(1)}, u32[]{:S(2)}) copy-start(f32[8,256,256]{2,1,0:T(8,128)S(1)} %fusion.347) | copy-start | bytes 6291460
  381.7 56.4 %all-to-all-start.6 = ((f32[32,8,2048]{2,1,0:T(8,128)}), f32[32,8,2048]{2,1,0:T(8,128)}, u32[]{:S(2)}, u32[]{:S(2)}) async-start(f32[32,8,2048]{2,1,0:T(8,128)} %reshape.253), calls=%async_computation.6 | async-start | bytes 4194304 | tf_op jit(solution)/shard_map/all_to_all | solution.py:95
  438.0 53.7 %all-to-all-start.5 = ((f32[32,8,2048]{2,1,0:T(8,128)}), f32[32,8,2048]{2,1,0:T(8,128)}, u32[]{:S(2)}, u32[]{:S(2)}) async-start(f32[32,8,2048]{2,1,0:T(8,128)} %reshape.250), calls=%async_computation.5 | async-start | bytes 4194304 | tf_op jit(solution)/shard_map/all_to_all | solution.py:95
  491.7 90.0 %all-to-all-start.2 = ((f32[32,8,2048]{2,1,0:T(8,128)}), f32[32,8,2048]{2,1,0:T(8,128)}, u32[]{:S(2)}, u32[]{:S(2)}) async-start(f32[32,8,2048]{2,1,0:T(8,128)} %reshape.241), calls=%async_computation.2 | async-start | bytes 4194304 | tf_op jit(solution)/shard_map/all_to_all | solution.py:95
  506.5 6.4 %copy-start.5 = (f32[256,512,1]{1,0,2:T(8,128)S(1)}, f32[256,512,1]{1,0,2:T(8,128)}, u32[]{:S(2)}) copy-start(f32[256,512,1]{1,0,2:T(8,128)} %constant.129) | copy-start | bytes 1572868
  512.9 21.6 %copy-start.1 = (f32[256,64,32]{2,1,0:T(8,128)S(1)}, f32[256,64,32]{2,1,0:T(8,128)}, u32[]{:S(2)}) copy-start(f32[256,64,32]{2,1,0:T(8,128)} %reshape.251) | copy-start | bytes 6291460
  512.9 45.1 %slice-start = ((s8[8388608]{0:T(1024)(128)(4,1)}), s8[4194304]{0:T(1024)(128)(4,1)S(1)}, s32[]{:S(2)}) async-start(s8[8388608]{0:T(1024)(128)(4,1)} %bitcast.151), calls=%async_computation.8 | async-start | bytes 8388608
  534.5 23.4 %slice-start.1 = ((s8[8388608]{0:T(1024)(128)(4,1)}), s8[4194304]{0:T(1024)(128)(4,1)S(1)}, s32[]{:S(2)}) async-start(s8[8388608]{0:T(1024)(128)(4,1)} %bitcast.151), calls=%async_computation.9 | async-start | bytes 8388608
  534.5 23.4 %copy-start.3 = (f32[256,512,1]{1,0,2:T(8,128)S(1)}, f32[256,512,1]{1,0,2:T(8,128)}, u32[]{:S(2)}) copy-start(f32[256,512,1]{1,0,2:T(8,128)} %constant.127) | copy-start | bytes 1572868

commit v2 on v1

v2 whole, which is shorter than its diff:
```python
import functools

import jax
import jax.numpy as jnp
import numpy as np
from jax import lax
from jax.experimental import pallas as pl
from jax.experimental.pallas import tpu as pltpu
from jax.sharding import PartitionSpec as P

HIGH = lax.Precision.HIGHEST
AXES = ("py", "pz")
LANES = 128
SUBLANES = 8
VMEM_LIMIT = 56 * 1024 * 1024


def channel_freq(length):
    channel = np.arange(length)
    return np.where(channel == 1, length // 2, channel // 2)


def real_table(length):
    freq = channel_freq(length)
    phase = (freq[:, None] * np.arange(length)[None, :]) % length
    angle = 2.0 * np.pi / length * phase
    odd = (np.arange(length) % 2 == 1) & (np.arange(length) > 1)
    single = np.arange(length) < 2
    table = np.where(odd[:, None], np.sin(angle), np.cos(angle))
    return (table * np.sqrt(np.where(single, 1.0, 2.0) / length)[:, None]).astype(np.float32)


def spline(freq, length):
    return (4.0 + 2.0 * jnp.cos(2.0 * jnp.pi / length * freq.astype(jnp.float32))) / 6.0


def make_kernel(coef, freqs, lengths):
    scaled = [freq.astype(jnp.float32) / length for freq, length in zip(freqs, lengths)]
    ratio = 4.0 * (scaled[0] ** 2 + scaled[1] ** 2 + scaled[2] ** 2) / 3.0
    volume = ratio * jnp.sqrt(ratio)
    smooth = spline(freqs[0], lengths[0]) * spline(freqs[1], lengths[1]) * spline(freqs[2], lengths[2])
    count = coef.shape[2]
    total = [[0.0, 0.0], [0.0, 0.0]]
    for index in range(count):
        basis = jnp.exp(-jnp.square((volume - (index + 0.5) / count) * count))
        for a in range(2):
            for b in range(2):
                total[a][b] = total[a][b] + coef[a, b, index] * basis
    return [total[a][b] * smooth for a in range(2) for b in range(2)]


def dot(left, right, left_dim, right_dim):
    dims = (((left_dim,), (right_dim,)), ((), ()))
    return lax.dot_general(left, right, dims, precision=HIGH, preferred_element_type=jnp.float32)


def params():
    return pltpu.CompilerParams(vmem_limit_bytes=VMEM_LIMIT)


def x_forward_body(table_ref, one_ref, two_ref, out_ref):
    world, _, rows, cells = out_ref.shape
    for a, ref in enumerate((one_ref, two_ref)):
        values = ref[...].reshape(cells, ref.shape[-1])
        out_ref[:, a] = dot(table_ref[...], values, 1, 1).reshape(world, rows, cells)


def cell_blocks(y_local, z_local):
    blocks = 4
    while y_local % blocks or (y_local // blocks * z_local) % LANES:
        blocks //= 2
    return blocks


def x_forward(table, fields, world, rows):
    y_local, z_local, x_count = fields[0].shape
    blocks = cell_blocks(y_local, z_local)
    part = y_local // blocks
    field_spec = pl.BlockSpec((part, z_local, x_count), lambda i: (i, 0, 0))
    return pl.pallas_call(
        x_forward_body,
        grid=(blocks,),
        in_specs=[pl.BlockSpec(table.shape, lambda i: (0, 0)), field_spec, field_spec],
        out_specs=pl.BlockSpec((world, 2, rows, part * z_local), lambda i: (0, 0, 0, i)),
        out_shape=jax.ShapeDtypeStruct((world, 2, rows, y_local * z_local), jnp.float32),
        compiler_params=params(),
        name="x_forward",
    )(table, *fields)


def x_inverse_body(table_ref, value_ref, *refs):
    outs = refs[-2:]
    for a, out_ref in enumerate(outs):
        world, _, rows, cells = value_ref.shape
        value = value_ref[:, a].reshape(world * rows, cells)
        total = dot(value, table_ref[...], 0, 0).reshape(out_ref.shape)
        out_ref[...] = total if len(refs) == 2 else refs[a][...] + total


def x_inverse(table, value, before, y_local, z_local):
    world, _, rows, cells = value.shape
    x_count = table.shape[1]
    blocks = cell_blocks(y_local, z_local)
    part = y_local // blocks
    field_spec = pl.BlockSpec((part, z_local, x_count), lambda i: (i, 0, 0))
    out = jax.ShapeDtypeStruct((y_local, z_local, x_count), jnp.float32)
    return pl.pallas_call(
        x_inverse_body,
        grid=(blocks,),
        in_specs=[
            pl.BlockSpec(table.shape, lambda i: (0, 0)),
            pl.BlockSpec((world, 2, rows, part * z_local), lambda i: (0, 0, 0, i)),
        ]
        + [field_spec] * len(before),
        out_specs=(field_spec, field_spec),
        out_shape=(out, out),
        compiler_params=params(),
        name="x_inverse",
    )(table, value, *before)


def swap_groups(values, width):
    values = list(values)
    count = len(values)
    lane = lax.broadcasted_iota(jnp.int32, values[0].shape, 1)
    step = 1
    while step < count:
        low = (lane // (step * width)) % 2 == 0
        for m in range(count):
            if m & step == 0:
                one, two = values[m], values[m | step]
                values[m] = jnp.where(low, one, pltpu.roll(two, step * width, 1))
                values[m | step] = jnp.where(low, pltpu.roll(one, LANES - step * width, 1), two)
        step *= 2
    return values


def yz_body(value_ref, y_ref, z_ref, k00, k01, k10, k11, out_ref, scratch):
    py, pz, _, rows, cells = value_ref.shape
    y_count = y_ref.shape[0]
    z_count = z_ref.shape[0]
    z_local = z_count // pz
    split = LANES // z_local
    tiles = cells // LANES
    block = split * tiles * rows
    halves = z_count // LANES
    r = pl.program_id(0)

    @pl.when(r == 0)
    def _():
        for a in range(2):

            def forward(i, carry):
                spread = []
                for high in range(pz // split):
                    group = []
                    for low in range(split):
                        value = value_ref[i, high * split + low, a]
                        group.append(
                            jnp.concatenate([value[:, t * LANES : (t + 1) * LANES] for t in range(tiles)], axis=0)
                        )
                    spread.append(swap_groups(group, z_local))
                lines = [jnp.concatenate([part[p] for part in spread], axis=1) for p in range(split)]
                lines = jnp.concatenate(lines, axis=0)
                lines = dot(lines, z_ref[...], 1, 1)
                for t in range(halves):
                    scratch[a, t, pl.ds(i * block, block), :] = lines[:, t * LANES : (t + 1) * LANES]
                return carry

            lax.fori_loop(0, py, forward, 0)

    spectra = []
    for a in range(2):
        plane = [scratch[a, t, pl.ds(r, y_count, stride=rows), :] for t in range(halves)]
        spectra.append(dot(y_ref[...], jnp.concatenate(plane, axis=1), 1, 0))
    for a, (first, second) in enumerate(((k00, k01), (k10, k11))):
        weighed = first[0] * spectra[0] + second[0] * spectra[1]
        plane = dot(y_ref[...], weighed, 0, 0)
        for t in range(halves):
            scratch[a, t, pl.ds(r, y_count, stride=rows), :] = plane[:, t * LANES : (t + 1) * LANES]

    @pl.when(r == rows - 1)
    def _():
        for a in range(2):

            def backward(i, carry):
                lines = [scratch[a, t, pl.ds(i * block, block), :] for t in range(halves)]
                lines = dot(jnp.concatenate(lines, axis=1), z_ref[...], 1, 0)
                size = block // split
                for high in range(pz // split):
                    lanes = slice(high * LANES, (high + 1) * LANES)
                    group = swap_groups([lines[p * size : (p + 1) * size, lanes] for p in range(split)], z_local)
                    for low in range(split):
                        for t in range(tiles):
                            piece = group[low][t * rows : (t + 1) * rows]
                            out_ref[i, high * split + low, a, :, t * LANES : (t + 1) * LANES] = piece
                return carry

            lax.fori_loop(0, py, backward, 0)


def yz_apply(value, kernel, sizes):
    py, pz, y_local, z_local = sizes
    _, _, rows, cells = value.shape
    y_count, z_count = py * y_local, pz * z_local
    y_table, z_table = real_table(y_count), jnp.asarray(real_table(z_count))
    value = value.reshape(py, pz, 2, rows, cells)
    if rows % SUBLANES or LANES % z_local or cells % LANES or z_count % LANES or pz % (LANES // z_local):
        return yz_plain(value, kernel, sizes, jnp.asarray(y_table), z_table)
    split = LANES // z_local
    order = np.arange(y_count).reshape(py, y_local // split, split).transpose(0, 2, 1).reshape(-1)
    y_table = jnp.asarray(y_table[:, order])
    whole = lambda shape: pl.BlockSpec(shape, lambda r: (0,) * len(shape))
    k_spec = pl.BlockSpec((1, y_count, z_count), lambda r: (r, 0, 0))
    out = pl.pallas_call(
        yz_body,
        grid=(rows,),
        in_specs=[whole(value.shape), whole(y_table.shape), whole(z_table.shape)] + [k_spec] * 4,
        out_specs=whole(value.shape),
        out_shape=jax.ShapeDtypeStruct(value.shape, jnp.float32),
        scratch_shapes=[pltpu.VMEM((2, z_count // LANES, y_count * rows, LANES), jnp.float32)],
        compiler_params=params(),
        name="yz_apply",
    )(value, y_table, z_table, *kernel)
    return out.reshape(py * pz, 2, rows, cells)


def yz_plain(value, kernel, sizes, y_table, z_table):
    py, pz, y_local, z_local = sizes
    rows = value.shape[3]
    value = value.reshape(py, pz, 2, rows, y_local, z_local).transpose(2, 3, 0, 4, 1, 5)
    value = value.reshape(2, rows, py * y_local, pz * z_local)
    value = jnp.einsum("aryz,mz->arym", value, z_table, precision=HIGH)
    value = jnp.einsum("arym,ky->arkm", value, y_table, precision=HIGH)
    k00, k01, k10, k11 = kernel
    value = jnp.stack([k00 * value[0] + k01 * value[1], k10 * value[0] + k11 * value[1]])
    value = jnp.einsum("arkm,ky->arym", value, y_table, precision=HIGH)
    value = jnp.einsum("arym,mz->aryz", value, z_table, precision=HIGH)
    value = value.reshape(2, rows, py, y_local, pz, z_local).transpose(2, 4, 0, 1, 3, 5)
    return value.reshape(py * pz, 2, rows, y_local * z_local)


def shards(field_one, field_two, coef):
    y_local, z_local, x_count = field_one.shape
    py_count = lax.axis_size("py")
    pz_count = lax.axis_size("pz")
    sizes = (py_count, pz_count, y_local, z_local)
    y_count = y_local * py_count
    z_count = z_local * pz_count
    world = py_count * pz_count
    per_device = x_count // world
    groups = 2 if per_device % (2 * SUBLANES) == 0 else 1
    rows = per_device // groups
    x_table = real_table(x_count).reshape(world, groups, rows, x_count)
    tables = [jnp.asarray(x_table[:, g].reshape(world * rows, x_count)) for g in range(groups)]
    me = lax.axis_index("py") * pz_count + lax.axis_index("pz")
    freq_y = jnp.asarray(channel_freq(y_count))
    freq_z = jnp.asarray(channel_freq(z_count))

    def exchange(value):
        return lax.all_to_all(value, AXES, split_axis=0, concat_axis=0, tiled=True)

    arrived = []
    for group in range(groups):
        arrived.append(exchange(x_forward(tables[group], (field_one, field_two), world, rows)))
    returned = []
    for group in range(groups):
        channel = me * per_device + group * rows + jnp.arange(rows)
        freq_x = jnp.where(channel == 1, x_count // 2, channel // 2)
        kernel = make_kernel(
            coef,
            (freq_y[None, :, None], freq_z[None, None, :], freq_x[:, None, None]),
            (y_count, z_count, x_count),
        )
        returned.append(exchange(yz_apply(arrived[group], kernel, sizes)))
    results = ()
    for group in range(groups):
        results = x_inverse(tables[group], returned[group], results, y_local, z_local)
    return tuple(results)


def solution(mesh):
    in_specs = (P("py", "pz", None), P("py", "pz", None), P())
    out_specs = (P("py", "pz", None), P("py", "pz", None))
    return jax.shard_map(shards, mesh=mesh, in_specs=in_specs, out_specs=out_specs, check_vma=False)
```

time: 621 us -> 422 us (0.68); the launches traced: 612 us -> 421 us
  local copies, waits for them, and re-layouts: 246 us -> 1.4 us
  matrix products: 233 us -> 0 us
  waiting for transfers between devices: 93.7 us -> 238 us
  Pallas kernels: 0 us -> 99.6 us
  other arithmetic: 0.24 us -> 62.3 us
  starting transfers between devices: 37.3 us -> 18.6 us
    dot_general x24 -> x0, matrix products: 233 us -> none  [the longest x4 92.3 us: shards(): part = jnp.einsum('qyz,qx->yzx', value, table, precision=HIGH)]
    reshape x24 -> x0, local copies, waits for them, and re-layouts: 151 us -> none  [the longest x4 30 us: shards(): value = value.reshape(world, rows, y_local * z_local)]
    all_to_all x8 -> x4, waiting for transfers between devices: 93.7 us -> 238 us  [exchange(): return lax.all_to_all(value, AXES, split_axis=0, concat_axis=0, tiled=True)]
    pallas_call x0 -> x6, Pallas kernels: none -> 99.6 us  [the longest x2 57.2 us: yz_apply(): pl.pallas_call(yz_body, grid=(rows,), in_specs=[whole(value.shape), whole...]
    transpose x8 -> x0, local copies, waits for them, and re-layouts: 62.3 us -> none  [the longest x4 31.2 us: shards(): value.reshape(rows, py_count, y_local, pz_count, z_local)]
    mul x0 -> x4, other arithmetic: none -> 62 us  [make_kernel(): return [total[a][b] * smooth for a in range(2) for b in range(2)]]
    dot_general x4 -> x0, local copies, waits for them, and re-layouts: 30.4 us -> none  [shards(): spectrum = jnp.einsum('qx,yzx->qyz', table, field, precision=HIGH)]
    all_to_all x8 -> x4, starting transfers between devices: 37.3 us -> 18.6 us  [exchange(): return lax.all_to_all(value, AXES, split_axis=0, concat_axis=0, tiled=True)]
  transfers between devices with their start and end apart: 8 -> 4, of which waited for: 5 -> 4; matrix products, arithmetic and copies ran while one was open for 69% -> 15% of each run, Pallas kernels for 0% -> 18%
where the time goes in v2:
time: 422 us; the launch traced here: 421 us
  waiting for transfers between devices  238 us (56%)
  Pallas kernels  99.6 us (24%)
  other arithmetic  62.3 us (15%)
  starting transfers between devices  18.6 us (4%)
    all_to_all x4, waiting for transfers between devices, exchange(): return lax.all_to_all(value, AXES, split_axis=0, concat_axis=0, tiled=True)  238 us
    mul x4, other arithmetic, make_kernel(): return [total[a][b] * smooth for a in range(2) for b in range(2)]  62 us
    pallas_call x2, Pallas kernels, yz_apply(): pl.pallas_call(yz_body, grid=(rows,), in_specs=[whole(value.shape), whole...  57.2 us
    pallas_call x2, Pallas kernels, x_inverse(): pl.pallas_call(x_inverse_body, grid=(blocks,), in_specs=[pl.BlockSpec(tab...  21.8 us
    pallas_call x2, Pallas kernels, x_forward(): pl.pallas_call(x_forward_body, grid=(blocks,), in_specs=[pl.BlockSpec(tab...  20.6 us
    all_to_all x4, starting transfers between devices, exchange(): return lax.all_to_all(value, AXES, split_axis=0, concat_axis=0, tiled=True)  18.6 us
  transfers between devices with their start and end apart: 4, of which 4 were waited for; matrix products, arithmetic and copies ran while one was open for 15% of the time, Pallas kernels for 18%

profile of v2, /device:TPU:0, one launch (start us, length us, event | category | flops | bytes accessed | tf_op | source)
XLA Modules:
  0.0 420.8 jit_solution(5706810950520634456)
XLA Ops:
  0.6 10.3 %x_forward.3 = f32[32,2,8,2048]{3,2,1,0:T(8,128)} custom-call(f32[256,512]{1,0:T(8,128)} %constant.117.clone.table_ref, f32[64,32,512]{2,1,0:T(8,128)} %one_ref.3, f32[64,32,512]{2,1,0:T(8,128)} %two_ref.3), custom_call_target="tpu_custom_call" | custom-call | tf_op jit(solution)/shard_map/x_forward/pallas_call | solution.py:80
  10.9 7.5 %all-to-all-start.2 = ((f32[32,2,8,2048]{3,2,1,0:T(8,128)}), f32[32,2,8,2048]{3,2,1,0:T(8,128)}, u32[]{:S(2)}, u32[]{:S(2)}) async-start(f32[32,2,8,2048]{3,2,1,0:T(8,128)} %x_forward.3), calls=%async_computation.2 | async-start | bytes 8388608 | tf_op jit(solution)/shard_map/all_to_all | solution.py:261
  18.4 10.3 %x_forward.2 = f32[32,2,8,2048]{3,2,1,0:T(8,128)} custom-call(f32[256,512]{1,0:T(8,128)} %constant.118.clone.table_ref, f32[64,32,512]{2,1,0:T(8,128)} %one_ref.3, f32[64,32,512]{2,1,0:T(8,128)} %two_ref.3), custom_call_target="tpu_custom_call" | custom-call | tf_op jit(solution)/shard_map/x_forward/pallas_call | solution.py:80
  28.7 0.0 copy-start
  28.7 0.0 copy-start.1
  28.7 0.0 copy-start.2
  28.7 84.6 %all-to-all-done.2 = f32[32,2,8,2048]{3,2,1,0:T(8,128)} async-done(((f32[32,2,8,2048]{3,2,1,0:T(8,128)}), f32[32,2,8,2048]{3,2,1,0:T(8,128)}, u32[]{:S(2)}, u32[]{:S(2)}) %all-to-all-start.2) | async-done | bytes 4194336 | tf_op jit(solution)/shard_map/all_to_all | solution.py:261
  113.3 3.8 all-to-all-start
  117.1 0.1 add_multiply_fusion
  117.2 0.1 add_multiply_fusion.1
  117.2 0.0 copy-done
  117.2 0.7 fusion.1
  117.9 0.7 fusion
  118.6 0.0 copy-done.1
  118.6 0.0 copy-done.2
  118.7 0.1 broadcast_multiply_fusion
  118.8 15.7 %multiply_multiply_fusion.3 = (f32[8,256,256]{2,1,0:T(8,128)}, f32[8,256,256]{2,1,0:T(8,128)}) fusion(f32[8]{0:T(128)S(1)} %get-tuple-element.46, f32[8]{0:T(128)S(1)} %get-tuple-element.47, f32[256,256]{1,0:T(8,128)S(1)} %get-tuple-element.50, f32[]{:T(128)} %bitcast.8, f32[]{:T(128)} %bitcast.7, f32[]{:T(128)} %bitcast.6, f32[]{:T(128)} %bitcast.5, ...), kind=kLoop, calls=%fused_computation.3 | loop fusion | flops 54525952 | bytes 4718752 | tf_op jit(solution)/shard_map/mul | solution.py:49
  134.4 15.4 %multiply_multiply_fusion.2 = (f32[8,256,256]{2,1,0:T(8,128)}, f32[8,256,256]{2,1,0:T(8,128)}) fusion(f32[8]{0:T(128)S(1)} %get-tuple-element.46, f32[8]{0:T(128)S(1)} %get-tuple-element.47, f32[]{:T(128)} %bitcast.16, f32[]{:T(128)} %bitcast.15, f32[]{:T(128)} %bitcast.14, f32[]{:T(128)} %bitcast.13, f32[]{:T(128)} %bitcast.12, f32[]{:T(128)} %bitcast.11, ...), kind=kLoop, calls=%fused_computation.2 | loop fusion | flops 54525952 | bytes 4718752 | tf_op jit(solution)/shard_map/mul | solution.py:49
  149.8 15.4 %multiply_multiply_fusion.1 = (f32[8,256,256]{2,1,0:T(8,128)}, f32[8,256,256]{2,1,0:T(8,128)}) fusion(f32[8]{0:T(128)S(1)} %get-tuple-element.46, f32[8]{0:T(128)S(1)} %get-tuple-element.47, f32[]{:T(128)} %bitcast.24, f32[]{:T(128)} %bitcast.23, f32[]{:T(128)} %bitcast.22, f32[]{:T(128)} %bitcast.21, f32[]{:T(128)} %bitcast.20, f32[]{:T(128)} %bitcast.19, ...), kind=kLoop, calls=%fused_computation.1 | loop fusion | flops 54525952 | bytes 4718752 | tf_op jit(solution)/shard_map/mul | solution.py:49
  165.3 15.6 %multiply_multiply_fusion = (f32[8,256,256]{2,1,0:T(8,128)}, f32[8,256,256]{2,1,0:T(8,128)}) fusion(f32[8]{0:T(128)S(1)} %get-tuple-element.46, f32[8]{0:T(128)S(1)} %get-tuple-element.47, f32[]{:T(128)} %bitcast.32, f32[]{:T(128)} %bitcast.31, f32[]{:T(128)} %bitcast.30, f32[]{:T(128)} %bitcast.29, f32[]{:T(128)} %bitcast.28, f32[]{:T(128)} %bitcast.27, ...), kind=kLoop, calls=%fused_computation | loop fusion | flops 54525952 | bytes 4718752 | tf_op jit(solution)/shard_map/mul | solution.py:49
  180.8 28.6 %yz_apply.3 = f32[4,8,2,8,2048]{4,3,2,1,0:T(8,128)} custom-call(f32[4,8,2,8,2048]{4,3,2,1,0:T(8,128)} %bitcast.34.value_ref, f32[256,256]{1,0:T(8,128)} %constant.121.clone.y_ref, f32[256,256]{1,0:T(8,128)} %constant.120.clone.z_ref, f32[8,256,256]{2,1,0:T(8,128)} %get-tuple-element.12.k00, f32[8,256,256]{2,1,0:T(8,128)} %get-tuple-element.10.k01, ...), custom_call_target="tpu_custom_call" | custom-call | tf_op jit(solution)/shard_map/yz_apply/pallas_call | solution.py:215
  209.4 2.5 all-to-all-done
  211.9 3.6 all-to-all-start.3
  215.5 28.6 %yz_apply.2 = f32[4,8,2,8,2048]{4,3,2,1,0:T(8,128)} custom-call(f32[4,8,2,8,2048]{4,3,2,1,0:T(8,128)} %bitcast.value_ref, f32[256,256]{1,0:T(8,128)} %constant.121.clone.y_ref, f32[256,256]{1,0:T(8,128)} %constant.120.clone.z_ref, f32[8,256,256]{2,1,0:T(8,128)} %get-tuple-element.13.k00, f32[8,256,256]{2,1,0:T(8,128)} %get-tuple-element.11.k01, ...), custom_call_target="tpu_custom_call" | custom-call | tf_op jit(solution)/shard_map/yz_apply/pallas_call | solution.py:215
  244.1 66.3 %all-to-all-done.3.value_ref = f32[32,2,8,2048]{3,2,1,0:T(8,128)} async-done(((f32[32,2,8,2048]{3,2,1,0:T(8,128)}), f32[32,2,8,2048]{3,2,1,0:T(8,128)}, u32[]{:S(2)}, u32[]{:S(2)}) %all-to-all-start.3) | async-done | bytes 4194336 | tf_op jit(solution)/shard_map/all_to_all | solution.py:261
  310.4 3.8 all-to-all-start.1
  314.3 9.9 %x_inverse.2 = (f32[64,32,512]{2,1,0:T(8,128)}, f32[64,32,512]{2,1,0:T(8,128)}) custom-call(f32[256,512]{1,0:T(8,128)} %constant.117.clone.table_ref, f32[32,2,8,2048]{3,2,1,0:T(8,128)} %all-to-all-done.3.value_ref), custom_call_target="tpu_custom_call" | custom-call | tf_op jit(solution)/shard_map/x_inverse/pallas_call | solution.py:107
  324.2 84.8 %all-to-all-done.1.value_ref = f32[32,2,8,2048]{3,2,1,0:T(8,128)} async-done(((f32[32,2,8,2048]{3,2,1,0:T(8,128)}), f32[32,2,8,2048]{3,2,1,0:T(8,128)}, u32[]{:S(2)}, u32[]{:S(2)}) %all-to-all-start.1) | async-done | bytes 4194336 | tf_op jit(solution)/shard_map/all_to_all | solution.py:261
  409.0 11.9 %x_inverse.3 = (f32[64,32,512]{2,1,0:T(8,128)}, f32[64,32,512]{2,1,0:T(8,128)}) custom-call(f32[256,512]{1,0:T(8,128)} %constant.118.clone.table_ref, f32[32,2,8,2048]{3,2,1,0:T(8,128)} %all-to-all-done.1.value_ref, f32[64,32,512]{2,1,0:T(8,128)} %get-tuple-element.4.refs_0_, f32[64,32,512]{2,1,0:T(8,128)} %get-tuple-element.5.refs_1_), custom_call_target="tpu_custom_call" | custom-call | tf_op jit(solution)/shard_map/x_inverse/pallas_call | solution.py:107
Async XLA Ops:
  10.9 102.4 %all-to-all-start.2 = ((f32[32,2,8,2048]{3,2,1,0:T(8,128)}), f32[32,2,8,2048]{3,2,1,0:T(8,128)}, u32[]{:S(2)}, u32[]{:S(2)}) async-start(f32[32,2,8,2048]{3,2,1,0:T(8,128)} %x_forward.3), calls=%async_computation.2 | async-start | bytes 8388608 | tf_op jit(solution)/shard_map/all_to_all | solution.py:261
  28.7 88.5 %copy-start = (f32[2,2,8]{2,1,0:T(2,128)S(1)}, f32[2,2,8]{2,1,0:T(2,128)}, u32[]{:S(2)}) copy-start(f32[2,2,8]{2,1,0:T(2,128)} %param.13) | copy-start | bytes 388
  28.7 89.9 %copy-start.1 = (f32[256]{0:T(256)S(1)}, f32[256]{0:T(256)}, u32[]{:S(2)}) copy-start(f32[256]{0:T(256)} %constant.129) | copy-start | bytes 3076
  28.7 89.9 %copy-start.2 = (f32[256]{0:T(256)S(1)}, f32[256]{0:T(256)}, u32[]{:S(2)}) copy-start(f32[256]{0:T(256)} %constant.124) | copy-start | bytes 3076
  113.3 98.5 %all-to-all-start = ((f32[32,2,8,2048]{3,2,1,0:T(8,128)}), f32[32,2,8,2048]{3,2,1,0:T(8,128)}, u32[]{:S(2)}, u32[]{:S(2)}) async-start(f32[32,2,8,2048]{3,2,1,0:T(8,128)} %x_forward.2), calls=%async_computation | async-start | bytes 8388608 | tf_op jit(solution)/shard_map/all_to_all | solution.py:261
  211.9 98.5 %all-to-all-start.3 = ((f32[32,2,8,2048]{3,2,1,0:T(8,128)}), f32[32,2,8,2048]{3,2,1,0:T(8,128)}, u32[]{:S(2)}, u32[]{:S(2)}) async-start(f32[32,2,8,2048]{3,2,1,0:T(8,128)} %bitcast.36), calls=%async_computation.3 | async-start | bytes 8388608 | tf_op jit(solution)/shard_map/all_to_all | solution.py:261
  310.4 98.5 %all-to-all-start.1 = ((f32[32,2,8,2048]{3,2,1,0:T(8,128)}), f32[32,2,8,2048]{3,2,1,0:T(8,128)}, u32[]{:S(2)}, u32[]{:S(2)}) async-start(f32[32,2,8,2048]{3,2,1,0:T(8,128)} %bitcast.37), calls=%async_computation.1 | async-start | bytes 8388608 | tf_op jit(solution)/shard_map/all_to_all | solution.py:261

commit v3 on v2

--- a/solution.py
+++ b/solution.py
@@ -12,6 +12,7 @@
 AXES = ("py", "pz")
 LANES = 128
 SUBLANES = 8
+BLOCKS = 2
 VMEM_LIMIT = 56 * 1024 * 1024
 
 
@@ -58,27 +59,39 @@
     return pltpu.CompilerParams(vmem_limit_bytes=VMEM_LIMIT)
 
 
-def x_forward_body(table_ref, one_ref, two_ref, out_ref):
+def x_groups(x_count, world):
+    table, freq = real_table(x_count), channel_freq(x_count)
+    if x_count // world % (2 * SUBLANES) or x_count // 2 % LANES:
+        return [(table, 0, freq)]
+    half = x_count // 2
+    return [(table[freq % 2 == odd][:, :half], 1 - 2 * odd, freq[freq % 2 == odd]) for odd in range(2)]
+
+
+def x_forward_body(sign, table_ref, one_ref, two_ref, out_ref):
     world, _, rows, cells = out_ref.shape
     for a, ref in enumerate((one_ref, two_ref)):
         values = ref[...].reshape(cells, ref.shape[-1])
+        if sign:
+            half = values.shape[1] // 2
+            values = values[:, :half] + values[:, half:] if sign > 0 else values[:, :half] - values[:, half:]
         out_ref[:, a] = dot(table_ref[...], values, 1, 1).reshape(world, rows, cells)
 
 
 def cell_blocks(y_local, z_local):
-    blocks = 4
+    blocks = BLOCKS
     while y_local % blocks or (y_local // blocks * z_local) % LANES:
         blocks //= 2
     return blocks
 
 
-def x_forward(table, fields, world, rows):
+def x_forward(table, sign, fields, world):
     y_local, z_local, x_count = fields[0].shape
+    rows = table.shape[0] // world
     blocks = cell_blocks(y_local, z_local)
     part = y_local // blocks
     field_spec = pl.BlockSpec((part, z_local, x_count), lambda i: (i, 0, 0))
     return pl.pallas_call(
-        x_forward_body,
+        functools.partial(x_forward_body, sign),
         grid=(blocks,),
         in_specs=[pl.BlockSpec(table.shape, lambda i: (0, 0)), field_spec, field_spec],
         out_specs=pl.BlockSpec((world, 2, rows, part * z_local), lambda i: (0, 0, 0, i)),
@@ -89,20 +102,23 @@
 
 
 def x_inverse_body(table_ref, value_ref, *refs):
-    outs = refs[-2:]
-    for a, out_ref in enumerate(outs):
+    for a, out_ref in enumerate(refs[-2:]):
         world, _, rows, cells = value_ref.shape
         value = value_ref[:, a].reshape(world * rows, cells)
-        total = dot(value, table_ref[...], 0, 0).reshape(out_ref.shape)
-        out_ref[...] = total if len(refs) == 2 else refs[a][...] + total
-
-
-def x_inverse(table, value, before, y_local, z_local):
+        total = dot(value, table_ref[...], 0, 0)
+        if len(refs) == 4:
+            even = refs[a][...].reshape(total.shape)
+            total = jnp.concatenate([even + total, even - total], axis=1)
+        out_ref[...] = total.reshape(out_ref.shape)
+
+
+def x_inverse(table, value, even, y_local, z_local):
     world, _, rows, cells = value.shape
-    x_count = table.shape[1]
+    width = table.shape[1]
     blocks = cell_blocks(y_local, z_local)
     part = y_local // blocks
-    field_spec = pl.BlockSpec((part, z_local, x_count), lambda i: (i, 0, 0))
+    block = lambda count: pl.BlockSpec((part, z_local, count), lambda i: (i, 0, 0))
+    x_count = 2 * width if even else width
     out = jax.ShapeDtypeStruct((y_local, z_local, x_count), jnp.float32)
     return pl.pallas_call(
         x_inverse_body,
@@ -111,12 +127,12 @@
             pl.BlockSpec(table.shape, lambda i: (0, 0)),
             pl.BlockSpec((world, 2, rows, part * z_local), lambda i: (0, 0, 0, i)),
         ]
-        + [field_spec] * len(before),
-        out_specs=(field_spec, field_spec),
+        + [block(width)] * len(even),
+        out_specs=(block(x_count), block(x_count)),
         out_shape=(out, out),
         compiler_params=params(),
         name="x_inverse",
-    )(table, value, *before)
+    )(table, value, *even)
 
 
 def swap_groups(values, width):
@@ -248,34 +264,28 @@
     y_count = y_local * py_count
     z_count = z_local * pz_count
     world = py_count * pz_count
-    per_device = x_count // world
-    groups = 2 if per_device % (2 * SUBLANES) == 0 else 1
-    rows = per_device // groups
-    x_table = real_table(x_count).reshape(world, groups, rows, x_count)
-    tables = [jnp.asarray(x_table[:, g].reshape(world * rows, x_count)) for g in range(groups)]
     me = lax.axis_index("py") * pz_count + lax.axis_index("pz")
     freq_y = jnp.asarray(channel_freq(y_count))
     freq_z = jnp.asarray(channel_freq(z_count))
+    groups = [(jnp.asarray(table), sign, freq) for table, sign, freq in x_groups(x_count, world)]
 
     def exchange(value):
         return lax.all_to_all(value, AXES, split_axis=0, concat_axis=0, tiled=True)
 
-    arrived = []
-    for group in range(groups):
-        arrived.append(exchange(x_forward(tables[group], (field_one, field_two), world, rows)))
+    arrived = [exchange(x_forward(table, sign, (field_one, field_two), world)) for table, sign, _ in groups]
     returned = []
-    for group in range(groups):
-        channel = me * per_device + group * rows + jnp.arange(rows)
-        freq_x = jnp.where(channel == 1, x_count // 2, channel // 2)
+    for value, (_, _, freq) in zip(arrived, groups):
+        rows = freq.size // world
+        freq_x = lax.dynamic_slice_in_dim(jnp.asarray(freq), me * rows, rows)
         kernel = make_kernel(
             coef,
             (freq_y[None, :, None], freq_z[None, None, :], freq_x[:, None, None]),
             (y_count, z_count, x_count),
         )
-        returned.append(exchange(yz_apply(arrived[group], kernel, sizes)))
+        returned.append(exchange(yz_apply(value, kernel, sizes)))
     results = ()
-    for group in range(groups):
-        results = x_inverse(tables[group], returned[group], results, y_local, z_local)
+    for value, (table, _, _) in zip(returned, groups):
+        results = x_inverse(table, value, results, y_local, z_local)
     return tuple(results)
 
 

time: 422 us -> 416 us (0.986)
  Pallas kernels: 99.6 us -> 88.5 us
  waiting for transfers between devices: 238 us -> 244 us
    pallas_call x2, Pallas kernels: 20.6 us -> 14.8 us  [x_forward(): pl.pallas_call(functools.partial(x_forward_body, sign), grid=(blocks,), i...]
    all_to_all x4, waiting for transfers between devices: 238 us -> 244 us  [exchange(): return lax.all_to_all(value, AXES, split_axis=0, concat_axis=0, tiled=True)]
    pallas_call x2, Pallas kernels: 21.8 us -> 16.5 us  [x_inverse(): pl.pallas_call(x_inverse_body, grid=(blocks,), in_specs=[pl.BlockSpec(tab...]
  transfers between devices with their start and end apart: 4 -> 4, of which waited for: 4 -> 4; matrix products, arithmetic and copies ran while one was open for 15% -> 15% of each run, Pallas kernels for 18% -> 17%
where the time goes in v3:
time: 416 us; the launch traced here: 415 us
  waiting for transfers between devices  244 us (59%)
  Pallas kernels  88.5 us (21%)
  other arithmetic  62.2 us (15%)
  starting transfers between devices  18.6 us (4%)
    all_to_all x4, waiting for transfers between devices, exchange(): return lax.all_to_all(value, AXES, split_axis=0, concat_axis=0, tiled=True)  244 us
    mul x4, other arithmetic, make_kernel(): return [total[a][b] * smooth for a in range(2) for b in range(2)]  61.9 us
    pallas_call x2, Pallas kernels, yz_apply(): pl.pallas_call(yz_body, grid=(rows,), in_specs=[whole(value.shape), whole...  57.2 us
    all_to_all x4, starting transfers between devices, exchange(): return lax.all_to_all(value, AXES, split_axis=0, concat_axis=0, tiled=True)  18.6 us
    pallas_call x2, Pallas kernels, x_inverse(): pl.pallas_call(x_inverse_body, grid=(blocks,), in_specs=[pl.BlockSpec(tab...  16.5 us
    pallas_call x2, Pallas kernels, x_forward(): pl.pallas_call(functools.partial(x_forward_body, sign), grid=(blocks,), i...  14.8 us
  transfers between devices with their start and end apart: 4, of which 4 were waited for; matrix products, arithmetic and copies ran while one was open for 15% of the time, Pallas kernels for 17%

profile of v3, /device:TPU:0, one launch (start us, length us, event | category | flops | bytes accessed | tf_op | source)
XLA Modules:
  0.0 415.1 jit_solution(13945545377329166926)
XLA Ops:
  0.6 7.4 %x_forward.3 = f32[32,2,8,2048]{3,2,1,0:T(8,128)} custom-call(f32[256,256]{1,0:T(8,128)} %constant.100.clone.table_ref, f32[64,32,512]{2,1,0:T(8,128)} %one_ref.3, f32[64,32,512]{2,1,0:T(8,128)} %two_ref.3), custom_call_target="tpu_custom_call" | custom-call | tf_op jit(solution)/shard_map/x_forward/pallas_call | solution.py:93
  8.0 7.5 %all-to-all-start.2 = ((f32[32,2,8,2048]{3,2,1,0:T(8,128)}), f32[32,2,8,2048]{3,2,1,0:T(8,128)}, u32[]{:S(2)}, u32[]{:S(2)}) async-start(f32[32,2,8,2048]{3,2,1,0:T(8,128)} %x_forward.3), calls=%async_computation.2 | async-start | bytes 8388608 | tf_op jit(solution)/shard_map/all_to_all | solution.py:273
  15.5 7.4 %x_forward.2 = f32[32,2,8,2048]{3,2,1,0:T(8,128)} custom-call(f32[256,256]{1,0:T(8,128)} %constant.101.clone.table_ref, f32[64,32,512]{2,1,0:T(8,128)} %one_ref.3, f32[64,32,512]{2,1,0:T(8,128)} %two_ref.3), custom_call_target="tpu_custom_call" | custom-call | tf_op jit(solution)/shard_map/x_forward/pallas_call | solution.py:93
  22.9 0.0 copy-start.3
  22.9 0.0 copy-start.4
  22.9 0.0 copy-start
  22.9 0.0 copy-start.1
  22.9 0.0 copy-start.2
  22.9 87.5 %all-to-all-done.2 = f32[32,2,8,2048]{3,2,1,0:T(8,128)} async-done(((f32[32,2,8,2048]{3,2,1,0:T(8,128)}), f32[32,2,8,2048]{3,2,1,0:T(8,128)}, u32[]{:S(2)}, u32[]{:S(2)}) %all-to-all-start.2) | async-done | bytes 4194336 | tf_op jit(solution)/shard_map/all_to_all | solution.py:273
  110.4 3.8 all-to-all-start
  114.2 0.0 copy-done.3
  114.2 0.0 copy-done.4
  114.2 0.1 multiply_multiply_fusion.8
  114.4 0.0 copy-done
  114.4 0.7 fusion.1
  115.1 0.7 fusion
  115.8 0.0 copy-done.1
  115.8 0.0 copy-done.2
  115.8 0.1 broadcast_multiply_fusion
  115.9 15.6 %multiply_multiply_fusion.3 = (f32[8,256,256]{2,1,0:T(8,128)}, f32[8,256,256]{2,1,0:T(8,128)}) fusion(f32[8]{0:T(128)S(1)} %get-tuple-element.47, f32[8]{0:T(128)S(1)} %get-tuple-element.46, f32[256,256]{1,0:T(8,128)S(1)} %get-tuple-element.52, f32[]{:T(128)} %bitcast.8, f32[]{:T(128)} %bitcast.7, f32[]{:T(128)} %bitcast.6, f32[]{:T(128)} %bitcast.5, ...), kind=kLoop, calls=%fused_computation.3 | loop fusion | flops 54525952 | bytes 4718752 | tf_op jit(solution)/shard_map/mul | solution.py:50
  131.5 15.4 %multiply_multiply_fusion.2 = (f32[8,256,256]{2,1,0:T(8,128)}, f32[8,256,256]{2,1,0:T(8,128)}) fusion(f32[8]{0:T(128)S(1)} %get-tuple-element.47, f32[8]{0:T(128)S(1)} %get-tuple-element.46, f32[]{:T(128)} %bitcast.16, f32[]{:T(128)} %bitcast.15, f32[]{:T(128)} %bitcast.14, f32[]{:T(128)} %bitcast.13, f32[]{:T(128)} %bitcast.12, f32[]{:T(128)} %bitcast.11, ...), kind=kLoop, calls=%fused_computation.2 | loop fusion | flops 54525952 | bytes 4718752 | tf_op jit(solution)/shard_map/mul | solution.py:50
  146.9 15.4 %multiply_multiply_fusion.1 = (f32[8,256,256]{2,1,0:T(8,128)}, f32[8,256,256]{2,1,0:T(8,128)}) fusion(f32[8]{0:T(128)S(1)} %get-tuple-element.47, f32[8]{0:T(128)S(1)} %get-tuple-element.46, f32[]{:T(128)} %bitcast.24, f32[]{:T(128)} %bitcast.23, f32[]{:T(128)} %bitcast.22, f32[]{:T(128)} %bitcast.21, f32[]{:T(128)} %bitcast.20, f32[]{:T(128)} %bitcast.19, ...), kind=kLoop, calls=%fused_computation.1 | loop fusion | flops 54525952 | bytes 4718752 | tf_op jit(solution)/shard_map/mul | solution.py:50
  162.3 15.6 %multiply_multiply_fusion = (f32[8,256,256]{2,1,0:T(8,128)}, f32[8,256,256]{2,1,0:T(8,128)}) fusion(f32[8]{0:T(128)S(1)} %get-tuple-element.47, f32[8]{0:T(128)S(1)} %get-tuple-element.46, f32[]{:T(128)} %bitcast.32, f32[]{:T(128)} %bitcast.31, f32[]{:T(128)} %bitcast.30, f32[]{:T(128)} %bitcast.29, f32[]{:T(128)} %bitcast.28, f32[]{:T(128)} %bitcast.27, ...), kind=kLoop, calls=%fused_computation | loop fusion | flops 54525952 | bytes 4718752 | tf_op jit(solution)/shard_map/mul | solution.py:50
  177.9 28.6 %yz_apply.3 = f32[4,8,2,8,2048]{4,3,2,1,0:T(8,128)} custom-call(f32[4,8,2,8,2048]{4,3,2,1,0:T(8,128)} %bitcast.34.value_ref, f32[256,256]{1,0:T(8,128)} %constant.104.clone.y_ref, f32[256,256]{1,0:T(8,128)} %constant.103.clone.z_ref, f32[8,256,256]{2,1,0:T(8,128)} %get-tuple-element.12.k00, f32[8,256,256]{2,1,0:T(8,128)} %get-tuple-element.10.k01, ...), custom_call_target="tpu_custom_call" | custom-call | tf_op jit(solution)/shard_map/yz_apply/pallas_call | solution.py:231
  206.4 2.5 all-to-all-done
  209.0 3.6 all-to-all-start.3
  212.6 28.6 %yz_apply.2 = f32[4,8,2,8,2048]{4,3,2,1,0:T(8,128)} custom-call(f32[4,8,2,8,2048]{4,3,2,1,0:T(8,128)} %bitcast.value_ref, f32[256,256]{1,0:T(8,128)} %constant.104.clone.y_ref, f32[256,256]{1,0:T(8,128)} %constant.103.clone.z_ref, f32[8,256,256]{2,1,0:T(8,128)} %get-tuple-element.13.k00, f32[8,256,256]{2,1,0:T(8,128)} %get-tuple-element.11.k01, ...), custom_call_target="tpu_custom_call" | custom-call | tf_op jit(solution)/shard_map/yz_apply/pallas_call | solution.py:231
  241.2 66.3 %all-to-all-done.3.value_ref = f32[32,2,8,2048]{3,2,1,0:T(8,128)} async-done(((f32[32,2,8,2048]{3,2,1,0:T(8,128)}), f32[32,2,8,2048]{3,2,1,0:T(8,128)}, u32[]{:S(2)}, u32[]{:S(2)}) %all-to-all-start.3) | async-done | bytes 4194336 | tf_op jit(solution)/shard_map/all_to_all | solution.py:273
  307.5 3.8 all-to-all-start.1
  311.3 7.4 %x_inverse.2 = (f32[64,32,256]{2,1,0:T(8,128)}, f32[64,32,256]{2,1,0:T(8,128)}) custom-call(f32[256,256]{1,0:T(8,128)} %constant.100.clone.table_ref, f32[32,2,8,2048]{3,2,1,0:T(8,128)} %all-to-all-done.3.value_ref), custom_call_target="tpu_custom_call" | custom-call | tf_op jit(solution)/shard_map/x_inverse/pallas_call | solution.py:123
  318.8 87.2 %all-to-all-done.1.value_ref = f32[32,2,8,2048]{3,2,1,0:T(8,128)} async-done(((f32[32,2,8,2048]{3,2,1,0:T(8,128)}), f32[32,2,8,2048]{3,2,1,0:T(8,128)}, u32[]{:S(2)}, u32[]{:S(2)}) %all-to-all-start.1) | async-done | bytes 4194336 | tf_op jit(solution)/shard_map/all_to_all | solution.py:273
  406.0 9.1 %x_inverse.3 = (f32[64,32,512]{2,1,0:T(8,128)}, f32[64,32,512]{2,1,0:T(8,128)}) custom-call(f32[256,256]{1,0:T(8,128)} %constant.101.clone.table_ref, f32[32,2,8,2048]{3,2,1,0:T(8,128)} %all-to-all-done.1.value_ref, f32[64,32,256]{2,1,0:T(8,128)} %get-tuple-element.4.refs_0_, f32[64,32,256]{2,1,0:T(8,128)} %get-tuple-element.5.refs_1_), custom_call_target="tpu_custom_call" | custom-call | tf_op jit(solution)/shard_map/x_inverse/pallas_call | solution.py:123
Async XLA Ops:
  8.0 102.4 %all-to-all-start.2 = ((f32[32,2,8,2048]{3,2,1,0:T(8,128)}), f32[32,2,8,2048]{3,2,1,0:T(8,128)}, u32[]{:S(2)}, u32[]{:S(2)}) async-start(f32[32,2,8,2048]{3,2,1,0:T(8,128)} %x_forward.3), calls=%async_computation.2 | async-start | bytes 8388608 | tf_op jit(solution)/shard_map/all_to_all | solution.py:273
  22.9 91.3 %copy-start.3 = (s32[256]{0:T(256)S(1)}, s32[256]{0:T(256)}, u32[]{:S(2)}) copy-start(s32[256]{0:T(256)} %constant.102.clone) | copy-start | bytes 3076
  22.9 91.3 %copy-start.4 = (s32[256]{0:T(256)S(1)}, s32[256]{0:T(256)}, u32[]{:S(2)}) copy-start(s32[256]{0:T(256)} %constant.105.clone) | copy-start | bytes 3076
  22.9 91.4 %copy-start = (f32[2,2,8]{2,1,0:T(2,128)S(1)}, f32[2,2,8]{2,1,0:T(2,128)}, u32[]{:S(2)}) copy-start(f32[2,2,8]{2,1,0:T(2,128)} %param.15) | copy-start | bytes 388
  22.9 92.9 %copy-start.1 = (f32[256]{0:T(256)S(1)}, f32[256]{0:T(256)}, u32[]{:S(2)}) copy-start(f32[256]{0:T(256)} %constant.113) | copy-start | bytes 3076
  22.9 92.9 %copy-start.2 = (f32[256]{0:T(256)S(1)}, f32[256]{0:T(256)}, u32[]{:S(2)}) copy-start(f32[256]{0:T(256)} %constant.108) | copy-start | bytes 3076
  110.4 98.5 %all-to-all-start = ((f32[32,2,8,2048]{3,2,1,0:T(8,128)}), f32[32,2,8,2048]{3,2,1,0:T(8,128)}, u32[]{:S(2)}, u32[]{:S(2)}) async-start(f32[32,2,8,2048]{3,2,1,0:T(8,128)} %x_forward.2), calls=%async_computation | async-start | bytes 8388608 | tf_op jit(solution)/shard_map/all_to_all | solution.py:273
  209.0 98.5 %all-to-all-start.3 = ((f32[32,2,8,2048]{3,2,1,0:T(8,128)}), f32[32,2,8,2048]{3,2,1,0:T(8,128)}, u32[]{:S(2)}, u32[]{:S(2)}) async-start(f32[32,2,8,2048]{3,2,1,0:T(8,128)} %bitcast.36), calls=%async_computation.3 | async-start | bytes 8388608 | tf_op jit(solution)/shard_map/all_to_all | solution.py:273
  307.5 98.5 %all-to-all-start.1 = ((f32[32,2,8,2048]{3,2,1,0:T(8,128)}), f32[32,2,8,2048]{3,2,1,0:T(8,128)}, u32[]{:S(2)}, u32[]{:S(2)}) async-start(f32[32,2,8,2048]{3,2,1,0:T(8,128)} %bitcast.37), calls=%async_computation.1 | async-start | bytes 8388608 | tf_op jit(solution)/shard_map/all_to_all | solution.py:273

commit v4 on v3

--- a/solution.py
+++ b/solution.py
@@ -8,11 +8,14 @@
 from jax.experimental.pallas import tpu as pltpu
 from jax.sharding import PartitionSpec as P
 
+
 HIGH = lax.Precision.HIGHEST
 AXES = ("py", "pz")
 LANES = 128
 SUBLANES = 8
 BLOCKS = 2
+PAIRED = 0
+MOST_PAIRS = 64
 VMEM_LIMIT = 56 * 1024 * 1024
 
 
@@ -31,23 +34,54 @@
     return (table * np.sqrt(np.where(single, 1.0, 2.0) / length)[:, None]).astype(np.float32)
 
 
-def spline(freq, length):
-    return (4.0 + 2.0 * jnp.cos(2.0 * jnp.pi / length * freq.astype(jnp.float32))) / 6.0
-
-
-def make_kernel(coef, freqs, lengths):
-    scaled = [freq.astype(jnp.float32) / length for freq, length in zip(freqs, lengths)]
-    ratio = 4.0 * (scaled[0] ** 2 + scaled[1] ** 2 + scaled[2] ** 2) / 3.0
-    volume = ratio * jnp.sqrt(ratio)
-    smooth = spline(freqs[0], lengths[0]) * spline(freqs[1], lengths[1]) * spline(freqs[2], lengths[2])
-    count = coef.shape[2]
-    total = [[0.0, 0.0], [0.0, 0.0]]
-    for index in range(count):
-        basis = jnp.exp(-jnp.square((volume - (index + 0.5) / count) * count))
-        for a in range(2):
-            for b in range(2):
-                total[a][b] = total[a][b] + coef[a, b, index] * basis
-    return [total[a][b] * smooth for a in range(2) for b in range(2)]
+def axis_terms(freq, length):
+    scaled = freq / length
+    return (scaled**2).astype(np.float32), ((4.0 + 2.0 * np.cos(2.0 * np.pi * scaled)) / 6.0).astype(np.float32)
+
+
+def radial_body(coef_ref, x_ref, y_ref, z_ref, *out_refs):
+    r = pl.program_id(0)
+    count = coef_ref.shape[0] // 4
+    _, y_count, z_count = out_refs[0].shape
+    chunk = min(2 * SUBLANES, y_count)
+    z_square, z_smooth = z_ref[0:1], z_ref[1:2]
+
+    def rows(step, carry):
+        part = pl.ds(step * chunk, chunk)
+        ratio = 4.0 * (y_ref[0, part] + x_ref[0, r] + z_square) / 3.0
+        volume = ratio * jnp.sqrt(ratio)
+        total = [jnp.zeros((chunk, z_count), jnp.float32) for _ in range(4)]
+        for index in range(count):
+            basis = jnp.exp(-jnp.square((volume - (index + 0.5) / count) * count))
+            total = [value + coef_ref[n * count + index] * basis for n, value in enumerate(total)]
+        smooth = y_ref[1, part] * x_ref[1, r] * z_smooth
+        for value, ref in zip(total, out_refs):
+            ref[0, part] = value * smooth
+        return carry
+
+    lax.fori_loop(0, y_count // chunk, rows, 0)
+
+
+def radial_kernel(coef, x_terms, y_freq, z_freq):
+    y_count, z_count = y_freq.size, z_freq.size
+    rows = x_terms.shape[1]
+    y_terms = jnp.asarray(np.stack(axis_terms(y_freq, y_count))[:, :, None])
+    z_terms = jnp.asarray(np.stack(axis_terms(z_freq, z_count)))
+    scalars = pl.BlockSpec(memory_space=pltpu.SMEM)
+    return pl.pallas_call(
+        radial_body,
+        grid=(rows,),
+        in_specs=[
+            scalars,
+            scalars,
+            pl.BlockSpec(y_terms.shape, lambda r: (0, 0, 0)),
+            pl.BlockSpec(z_terms.shape, lambda r: (0, 0)),
+        ],
+        out_specs=[pl.BlockSpec((1, y_count, z_count), lambda r: (r, 0, 0))] * 4,
+        out_shape=[jax.ShapeDtypeStruct((rows, y_count, z_count), jnp.float32)] * 4,
+        compiler_params=params(),
+        name="radial_kernel",
+    )(coef.reshape(-1), x_terms, y_terms, z_terms)
 
 
 def dot(left, right, left_dim, right_dim):
@@ -67,14 +101,25 @@
     return [(table[freq % 2 == odd][:, :half], 1 - 2 * odd, freq[freq % 2 == odd]) for odd in range(2)]
 
 
-def x_forward_body(sign, table_ref, one_ref, two_ref, out_ref):
+def place_table(base_ref, table_ref, placed):
+    @pl.when(pl.program_id(0) == 0)
+    def _():
+        for k in range(placed.shape[0]):
+            placed[k] = table_ref[k ^ base_ref[0]]
+
+    world, rows, width = placed.shape
+    return placed[...].reshape(world * rows, width)
+
+
+def x_forward_body(sign, base_ref, table_ref, one_ref, two_ref, out_ref, placed):
     world, _, rows, cells = out_ref.shape
+    table = place_table(base_ref, table_ref, placed)
     for a, ref in enumerate((one_ref, two_ref)):
         values = ref[...].reshape(cells, ref.shape[-1])
         if sign:
             half = values.shape[1] // 2
             values = values[:, :half] + values[:, half:] if sign > 0 else values[:, :half] - values[:, half:]
-        out_ref[:, a] = dot(table_ref[...], values, 1, 1).reshape(world, rows, cells)
+        out_ref[:, a] = dot(table, values, 1, 1).reshape(world, rows, cells)
 
 
 def cell_blocks(y_local, z_local):
@@ -84,37 +129,45 @@
     return blocks
 
 
-def x_forward(table, sign, fields, world):
+def x_forward(base, table, sign, fields):
     y_local, z_local, x_count = fields[0].shape
-    rows = table.shape[0] // world
+    world, rows, _ = table.shape
     blocks = cell_blocks(y_local, z_local)
     part = y_local // blocks
     field_spec = pl.BlockSpec((part, z_local, x_count), lambda i: (i, 0, 0))
     return pl.pallas_call(
         functools.partial(x_forward_body, sign),
         grid=(blocks,),
-        in_specs=[pl.BlockSpec(table.shape, lambda i: (0, 0)), field_spec, field_spec],
+        in_specs=[
+            pl.BlockSpec(memory_space=pltpu.SMEM),
+            pl.BlockSpec(table.shape, lambda i: (0, 0, 0)),
+            field_spec,
+            field_spec,
+        ],
         out_specs=pl.BlockSpec((world, 2, rows, part * z_local), lambda i: (0, 0, 0, i)),
         out_shape=jax.ShapeDtypeStruct((world, 2, rows, y_local * z_local), jnp.float32),
+        scratch_shapes=[pltpu.VMEM(table.shape, jnp.float32)],
         compiler_params=params(),
         name="x_forward",
-    )(table, *fields)
-
-
-def x_inverse_body(table_ref, value_ref, *refs):
+    )(base, table, *fields)
+
+
+def x_inverse_body(base_ref, table_ref, value_ref, *refs):
+    *refs, placed = refs
+    table = place_table(base_ref, table_ref, placed)
     for a, out_ref in enumerate(refs[-2:]):
         world, _, rows, cells = value_ref.shape
         value = value_ref[:, a].reshape(world * rows, cells)
-        total = dot(value, table_ref[...], 0, 0)
+        total = dot(value, table, 0, 0)
         if len(refs) == 4:
             even = refs[a][...].reshape(total.shape)
             total = jnp.concatenate([even + total, even - total], axis=1)
         out_ref[...] = total.reshape(out_ref.shape)
 
 
-def x_inverse(table, value, even, y_local, z_local):
-    world, _, rows, cells = value.shape
-    width = table.shape[1]
+def x_inverse(base, table, value, even, y_local, z_local):
+    world, _, rows, _ = value.shape
+    width = table.shape[2]
     blocks = cell_blocks(y_local, z_local)
     part = y_local // blocks
     block = lambda count: pl.BlockSpec((part, z_local, count), lambda i: (i, 0, 0))
@@ -124,15 +177,17 @@
         x_inverse_body,
         grid=(blocks,),
         in_specs=[
-            pl.BlockSpec(table.shape, lambda i: (0, 0)),
+            pl.BlockSpec(memory_space=pltpu.SMEM),
+            pl.BlockSpec(table.shape, lambda i: (0, 0, 0)),
             pl.BlockSpec((world, 2, rows, part * z_local), lambda i: (0, 0, 0, i)),
         ]
         + [block(width)] * len(even),
         out_specs=(block(x_count), block(x_count)),
         out_shape=(out, out),
+        scratch_shapes=[pltpu.VMEM(table.shape, jnp.float32)],
         compiler_params=params(),
         name="x_inverse",
-    )(table, value, *even)
+    )(base, table, value, *even)
 
 
 def swap_groups(values, width):
@@ -151,11 +206,13 @@
     return values
 
 
-def yz_body(value_ref, y_ref, z_ref, k00, k01, k10, k11, out_ref, scratch):
-    py, pz, _, rows, cells = value_ref.shape
+def yz_body(pz, base_ref, value_ref, y_ref, z_ref, k00, k01, k10, k11, out_ref, scratch):
+    world, _, rows, cells = value_ref.shape
+    py = world // pz
     y_count = y_ref.shape[0]
     z_count = z_ref.shape[0]
     z_local = z_count // pz
+    base = base_ref[0]
     split = LANES // z_local
     tiles = cells // LANES
     block = split * tiles * rows
@@ -171,7 +228,7 @@
                 for high in range(pz // split):
                     group = []
                     for low in range(split):
-                        value = value_ref[i, high * split + low, a]
+                        value = value_ref[(i * pz + high * split + low) ^ base, a]
                         group.append(
                             jnp.concatenate([value[:, t * LANES : (t + 1) * LANES] for t in range(tiles)], axis=0)
                         )
@@ -207,20 +264,20 @@
                     lanes = slice(high * LANES, (high + 1) * LANES)
                     group = swap_groups([lines[p * size : (p + 1) * size, lanes] for p in range(split)], z_local)
                     for low in range(split):
+                        slot = (i * pz + high * split + low) ^ base
                         for t in range(tiles):
                             piece = group[low][t * rows : (t + 1) * rows]
-                            out_ref[i, high * split + low, a, :, t * LANES : (t + 1) * LANES] = piece
+                            out_ref[slot, a, :, t * LANES : (t + 1) * LANES] = piece
                 return carry
 
             lax.fori_loop(0, py, backward, 0)
 
 
-def yz_apply(value, kernel, sizes):
+def yz_apply(base, value, kernel, sizes):
     py, pz, y_local, z_local = sizes
     _, _, rows, cells = value.shape
     y_count, z_count = py * y_local, pz * z_local
     y_table, z_table = real_table(y_count), jnp.asarray(real_table(z_count))
-    value = value.reshape(py, pz, 2, rows, cells)
     if rows % SUBLANES or LANES % z_local or cells % LANES or z_count % LANES or pz % (LANES // z_local):
         return yz_plain(value, kernel, sizes, jnp.asarray(y_table), z_table)
     split = LANES // z_local
@@ -228,22 +285,21 @@
     y_table = jnp.asarray(y_table[:, order])
     whole = lambda shape: pl.BlockSpec(shape, lambda r: (0,) * len(shape))
     k_spec = pl.BlockSpec((1, y_count, z_count), lambda r: (r, 0, 0))
-    out = pl.pallas_call(
-        yz_body,
+    return pl.pallas_call(
+        functools.partial(yz_body, pz),
         grid=(rows,),
-        in_specs=[whole(value.shape), whole(y_table.shape), whole(z_table.shape)] + [k_spec] * 4,
+        in_specs=[pl.BlockSpec(memory_space=pltpu.SMEM), whole(value.shape), whole(y_table.shape), whole(z_table.shape)] + [k_spec] * 4,
         out_specs=whole(value.shape),
         out_shape=jax.ShapeDtypeStruct(value.shape, jnp.float32),
         scratch_shapes=[pltpu.VMEM((2, z_count // LANES, y_count * rows, LANES), jnp.float32)],
         compiler_params=params(),
         name="yz_apply",
-    )(value, y_table, z_table, *kernel)
-    return out.reshape(py * pz, 2, rows, cells)
+    )(base, value, y_table, z_table, *kernel)
 
 
 def yz_plain(value, kernel, sizes, y_table, z_table):
     py, pz, y_local, z_local = sizes
-    rows = value.shape[3]
+    rows = value.shape[2]
     value = value.reshape(py, pz, 2, rows, y_local, z_local).transpose(2, 3, 0, 4, 1, 5)
     value = value.reshape(2, rows, py * y_local, pz * z_local)
     value = jnp.einsum("aryz,mz->arym", value, z_table, precision=HIGH)
@@ -265,27 +321,42 @@
     z_count = z_local * pz_count
     world = py_count * pz_count
     me = lax.axis_index("py") * pz_count + lax.axis_index("pz")
-    freq_y = jnp.asarray(channel_freq(y_count))
-    freq_z = jnp.asarray(channel_freq(z_count))
-    groups = [(jnp.asarray(table), sign, freq) for table, sign, freq in x_groups(x_count, world)]
-
-    def exchange(value):
+    freq_y, freq_z = channel_freq(y_count), channel_freq(z_count)
+    fields = (field_one, field_two)
+    groups = x_groups(x_count, world)
+
+    def all_at_once(value):
         return lax.all_to_all(value, AXES, split_axis=0, concat_axis=0, tiled=True)
 
-    arrived = [exchange(x_forward(table, sign, (field_one, field_two), world)) for table, sign, _ in groups]
+    def by_pairs(value):
+        parts = [value[:1]]
+        for k in range(1, world):
+            pairs = [(i, i ^ k) for i in range(world)]
+            parts.append(lax.ppermute(value[k : k + 1], AXES, pairs))
+        return jnp.concatenate(parts, axis=0)
+
+    paired = len(groups) == 2 and world & (world - 1) == 0 and world <= MOST_PAIRS
+    plans = []
+    for index, (table, sign, freq) in enumerate(groups):
+        rows = freq.size // world
+        x_terms = jnp.asarray(np.stack(axis_terms(freq, x_count)))
+        x_terms = lax.dynamic_slice_in_dim(x_terms, me * rows, rows, axis=1)
+        relative = paired and index == PAIRED
+        base = jnp.reshape(me if relative else jnp.zeros_like(me), (1,))
+        table = jnp.asarray(table.reshape(world, rows, -1))
+        plans.append((base, table, sign, x_terms, by_pairs if relative else all_at_once))
+
+    arrived = []
+    for base, table, sign, _, exchange in plans:
+        arrived.append(exchange(x_forward(base, table, sign, fields)))
     returned = []
-    for value, (_, _, freq) in zip(arrived, groups):
-        rows = freq.size // world
-        freq_x = lax.dynamic_slice_in_dim(jnp.asarray(freq), me * rows, rows)
-        kernel = make_kernel(
-            coef,
-            (freq_y[None, :, None], freq_z[None, None, :], freq_x[:, None, None]),
-            (y_count, z_count, x_count),
-        )
-        returned.append(exchange(yz_apply(value, kernel, sizes)))
+    for value, (base, _, _, x_terms, exchange) in zip(arrived, plans):
+        kernel = radial_kernel(coef, x_terms, freq_y, freq_z)
+        value = yz_apply(base, value, kernel, sizes)
+        returned.append(exchange(value))
     results = ()
-    for value, (table, _, _) in zip(returned, groups):
-        results = x_inverse(table, value, results, y_local, z_local)
+    for value, (base, table, _, _, _) in zip(returned, plans):
+        results = x_inverse(base, table, value, results, y_local, z_local)
     return tuple(results)
 
 

time: 416 us -> 463 us (1.11)
  starting transfers between devices: 18.6 us -> 127 us
  waiting for transfers between devices: 244 us -> 167 us
  other arithmetic: 62.2 us -> 0 us
  Pallas kernels: 88.5 us -> 132 us
  local copies, waits for them, and re-layouts: 1.44 us -> 32 us
    all_to_all x4 -> x2, waiting for transfers between devices: 244 us -> 0.01 us  [all_at_once(): return lax.all_to_all(value, AXES, split_axis=0, concat_axis=0, tiled=True)]
    ppermute x0 -> x62, waiting for transfers between devices: none -> 167 us  [by_pairs(): parts.append(lax.ppermute(value[k:k + 1], AXES, pairs))]
    ppermute x0 -> x62, starting transfers between devices: none -> 114 us  [by_pairs(): parts.append(lax.ppermute(value[k:k + 1], AXES, pairs))]
    mul x5 -> x0, other arithmetic: 62 us -> none  [the longest x4 61.9 us: make_kernel(): return [total[a][b] * smooth for a in range(2) for b in range(2)]]
    pallas_call x4 -> x6, Pallas kernels: 73.7 us -> 117 us  [the longest x2 57.7 us: yz_apply(): pl.pallas_call(functools.partial(yz_body, pz), grid=(rows,), in_specs=[pl...]
    unnamed x10 -> x68, local copies, waits for them, and re-layouts: 0.02 us -> 22.1 us
    slice x2 -> x4, local copies, waits for them, and re-layouts: 1.42 us -> 7.98 us  [by_pairs(): parts.append(lax.ppermute(value[k:k + 1], AXES, pairs))]
    all_to_all x4 -> x2, starting transfers between devices: 18.6 us -> 13.2 us  [all_at_once(): return lax.all_to_all(value, AXES, split_axis=0, concat_axis=0, tiled=True)]
  transfers between devices with their start and end apart: 4 -> 64, of which waited for: 4 -> 19; matrix products, arithmetic and copies ran while one was open for 15% -> 7% of each run, Pallas kernels for 17% -> 25%
where the time goes in v4:
time: 463 us; the launch traced here: 459 us
  waiting for transfers between devices  167 us (36%)
  Pallas kernels  132 us (29%)
  starting transfers between devices  127 us (27%)
  local copies, waits for them, and re-layouts  32 us (7%)
    ppermute x62, waiting for transfers between devices, by_pairs(): parts.append(lax.ppermute(value[k:k + 1], AXES, pairs))  167 us
    ppermute x62, starting transfers between devices, by_pairs(): parts.append(lax.ppermute(value[k:k + 1], AXES, pairs))  114 us
    pallas_call x2, Pallas kernels, yz_apply(): pl.pallas_call(functools.partial(yz_body, pz), grid=(rows,), in_specs=[pl...  57.7 us
    pallas_call x2, Pallas kernels, radial_kernel(): pl.pallas_call(radial_body, grid=(rows,), in_specs=[scalars, scalars, pl....  42.5 us
    unnamed x68, local copies, waits for them, and re-layouts  22.1 us
    pallas_call x2, Pallas kernels, x_inverse(): pl.pallas_call(x_inverse_body, grid=(blocks,), in_specs=[pl.BlockSpec(mem...  16.6 us
    pallas_call x2, Pallas kernels, x_forward(): pl.pallas_call(functools.partial(x_forward_body, sign), grid=(blocks,), i...  14.8 us
    all_to_all x2, starting transfers between devices, all_at_once(): return lax.all_to_all(value, AXES, split_axis=0, concat_axis=0, tiled=True)  13.2 us
  transfers between devices with their start and end apart: 64, of which 19 were waited for; matrix products, arithmetic and copies ran while one was open for 7% of the time, Pallas kernels for 25%

profile of v4, /device:TPU:0, one launch (start us, length us, event | category | flops | bytes accessed | tf_op | source)
XLA Modules:
  0.0 459.2 jit_solution(14807243570901827539)
XLA Ops:
  0.6 7.4 %x_forward.2 = f32[32,2,8,2048]{3,2,1,0:T(8,128)} custom-call(s32[1]{0:T(128)} %constant.13.clone.1.base_ref, f32[32,8,256]{2,1,0:T(8,128)} %constant.33.clone.table_ref, f32[64,32,512]{2,1,0:T(8,128)} %one_ref.3, f32[64,32,512]{2,1,0:T(8,128)} %two_ref.3), custom_call_target="tpu_custom_call" | custom-call | tf_op jit(solution)/shard_map/x_forward/pallas_call | solution.py:138
  8.0 7.5 %all-to-all-start = ((f32[32,2,8,2048]{3,2,1,0:T(8,128)}), f32[32,2,8,2048]{3,2,1,0:T(8,128)}, u32[]{:S(2)}, u32[]{:S(2)}) async-start(f32[32,2,8,2048]{3,2,1,0:T(8,128)} %x_forward.2), calls=%async_computation | async-start | bytes 8388608 | tf_op jit(solution)/shard_map/all_to_all | solution.py:329
  15.5 7.4 %x_forward.3 = f32[32,2,8,2048]{3,2,1,0:T(8,128)} custom-call(s32[1]{0:T(128)} %bitcast.base_ref, f32[32,8,256]{2,1,0:T(8,128)} %constant.31.clone.table_ref, f32[64,32,512]{2,1,0:T(8,128)} %one_ref.3, f32[64,32,512]{2,1,0:T(8,128)} %two_ref.3), custom_call_target="tpu_custom_call" | custom-call | tf_op jit(solution)/shard_map/x_forward/pallas_call | solution.py:138
  33.3 21.2 %radial_kernel.2 = (f32[8,256,256]{2,1,0:T(8,128)}, f32[8,256,256]{2,1,0:T(8,128)}, f32[8,256,256]{2,1,0:T(8,128)}, f32[8,256,256]{2,1,0:T(8,128)}) custom-call(f32[32]{0:T(128)} %reshape.11.coef_ref, f32[2,8]{1,0:T(2,128)} %get-tuple-element.87.x_ref, f32[2,256,1]{2,1,0:T(8,128)} %constant.34.clone.y_ref, f32[2,256]{1,0:T(2,128)} %constant.30.clone.z_ref), custom_call_target="tpu_custom_call" | custom-call | tf_op jit(solution)/shard_map/radial_kernel/pallas_call | solution.py:71
  54.5 21.3 %radial_kernel.3 = (f32[8,256,256]{2,1,0:T(8,128)}, f32[8,256,256]{2,1,0:T(8,128)}, f32[8,256,256]{2,1,0:T(8,128)}, f32[8,256,256]{2,1,0:T(8,128)}) custom-call(f32[32]{0:T(128)} %reshape.11.coef_ref, f32[2,8]{1,0:T(2,128)} %get-tuple-element.86.x_ref, f32[2,256,1]{2,1,0:T(8,128)} %constant.34.clone.y_ref, f32[2,256]{1,0:T(2,128)} %constant.30.clone.z_ref), custom_call_target="tpu_custom_call" | custom-call | tf_op jit(solution)/shard_map/radial_kernel/pallas_call | solution.py:71
  75.8 3.6 collective-permute-start.5
  80.0 7.2 %collective-permute-done.1 = f32[1,2,8,2048]{3,2,1,0:T(8,128)S(1)} collective-permute-done((f32[1,2,8,2048]{3,2,1,0:T(8,128)}, f32[1,2,8,2048]{3,2,1,0:T(8,128)S(1)}, u32[]{:S(2)}, u32[]{:S(2)}) %collective-permute-start.1) | collective-permute-done | bytes 131104 | tf_op jit(solution)/shard_map/ppermute | solution.py:335
  92.7 31.3 %collective-permute-done.3 = f32[1,2,8,2048]{3,2,1,0:T(8,128)S(1)} collective-permute-done((f32[1,2,8,2048]{3,2,1,0:T(8,128)}, f32[1,2,8,2048]{3,2,1,0:T(8,128)S(1)}, u32[]{:S(2)}, u32[]{:S(2)}) %collective-permute-start.3) | collective-permute-done | bytes 131104 | tf_op jit(solution)/shard_map/ppermute | solution.py:335
  143.0 6.3 %collective-permute-done.11 = f32[1,2,8,2048]{3,2,1,0:T(8,128)S(1)} collective-permute-done((f32[1,2,8,2048]{3,2,1,0:T(8,128)S(1)}, f32[1,2,8,2048]{3,2,1,0:T(8,128)S(1)}, u32[]{:S(2)}, u32[]{:S(2)}) %collective-permute-start.11) | collective-permute-done | bytes 131104 | tf_op jit(solution)/shard_map/ppermute | solution.py:335
  169.4 9.8 %collective-permute-done.19 = f32[1,2,8,2048]{3,2,1,0:T(8,128)S(1)} collective-permute-done((f32[1,2,8,2048]{3,2,1,0:T(8,128)S(1)}, f32[1,2,8,2048]{3,2,1,0:T(8,128)S(1)}, u32[]{:S(2)}, u32[]{:S(2)}) %collective-permute-start.19) | collective-permute-done | bytes 131104 | tf_op jit(solution)/shard_map/ppermute | solution.py:335
  181.4 4.1 collective-permute-start.26
  186.2 5.6 %collective-permute-start.27 = (f32[1,2,8,2048]{3,2,1,0:T(8,128)S(1)}, f32[1,2,8,2048]{3,2,1,0:T(8,128)S(1)}, u32[]{:S(2)}, u32[]{:S(2)}) collective-permute-start(f32[1,2,8,2048]{3,2,1,0:T(8,128)S(1)} %get-tuple-element.57), channel_id=1, source_target_pairs={{0,28},{1,29},{2,30},{3,31},{4,24},{5,25},{6,26},{7,27},{8,20},{9,... | collective-permute-start | bytes 393224 | tf_op jit(solution)/shard_map/ppermute | solution.py:335
  200.9 3.3 collective-permute-done.27
  204.9 5.8 %collective-permute-done.28 = f32[1,2,8,2048]{3,2,1,0:T(8,128)S(1)} collective-permute-done((f32[1,2,8,2048]{3,2,1,0:T(8,128)S(1)}, f32[1,2,8,2048]{3,2,1,0:T(8,128)S(1)}, u32[]{:S(2)}, u32[]{:S(2)}) %collective-permute-start.28) | collective-permute-done | bytes 131104 | tf_op jit(solution)/shard_map/ppermute | solution.py:335
  212.0 28.9 %yz_apply.2 = f32[32,2,8,2048]{3,2,1,0:T(8,128)} custom-call(s32[1]{0:T(128)} %constant.13.clone.1.base_ref, f32[32,2,8,2048]{3,2,1,0:T(8,128)} %all-to-all-done.value_ref, f32[256,256]{1,0:T(8,128)} %constant.36.clone.y_ref, f32[256,256]{1,0:T(8,128)} %constant.35.clone.z_ref, f32[8,256,256]{2,1,0:T(8,128)} %get-tuple-element.12.k00, ...), custom_call_target="tpu_custom_call" | custom-call | tf_op jit(solution)/shard_map/yz_apply/pallas_call | solution.py:288
  240.8 5.7 %all-to-all-start.1 = ((f32[32,2,8,2048]{3,2,1,0:T(8,128)}), f32[32,2,8,2048]{3,2,1,0:T(8,128)}, u32[]{:S(2)}, u32[]{:S(2)}) async-start(f32[32,2,8,2048]{3,2,1,0:T(8,128)} %yz_apply.2), calls=%async_computation.1 | async-start | bytes 8388608 | tf_op jit(solution)/shard_map/all_to_all | solution.py:329
  247.2 28.8 %yz_apply.3 = f32[32,2,8,2048]{3,2,1,0:T(8,128)} custom-call(s32[1]{0:T(128)} %bitcast.base_ref, f32[32,2,8,2048]{3,2,1,0:T(8,128)} %constant_dynamic-update-slice_fusion.value_ref, f32[256,256]{1,0:T(8,128)} %constant.36.clone.y_ref, f32[256,256]{1,0:T(8,128)} %constant.35.clone.z_ref, f32[8,256,256]{2,1,0:T(8,128)} %get-tuple-element.16.k00, ...), custom_call_target="tpu_custom_call" | custom-call | tf_op jit(solution)/shard_map/yz_apply/pallas_call | solution.py:288
  284.1 3.5 collective-permute-start.36
  287.6 30.5 %collective-permute-done.32 = f32[1,2,8,2048]{3,2,1,0:T(8,128)S(1)} collective-permute-done((f32[1,2,8,2048]{3,2,1,0:T(8,128)S(1)}, f32[1,2,8,2048]{3,2,1,0:T(8,128)S(1)}, u32[]{:S(2)}, u32[]{:S(2)}) %collective-permute-start.32) | collective-permute-done | bytes 131104 | tf_op jit(solution)/shard_map/ppermute | solution.py:335
  322.6 32.3 %collective-permute-done.34 = f32[1,2,8,2048]{3,2,1,0:T(8,128)S(1)} collective-permute-done((f32[1,2,8,2048]{3,2,1,0:T(8,128)S(1)}, f32[1,2,8,2048]{3,2,1,0:T(8,128)S(1)}, u32[]{:S(2)}, u32[]{:S(2)}) %collective-permute-start.34) | collective-permute-done | bytes 131104 | tf_op jit(solution)/shard_map/ppermute | solution.py:335
  356.6 3.6 collective-permute-start.41
  360.3 3.5 collective-permute-start.42
  370.2 9.0 %collective-permute-done.42 = f32[1,2,8,2048]{3,2,1,0:T(8,128)S(1)} collective-permute-done((f32[1,2,8,2048]{3,2,1,0:T(8,128)S(1)}, f32[1,2,8,2048]{3,2,1,0:T(8,128)S(1)}, u32[]{:S(2)}, u32[]{:S(2)}) %collective-permute-start.42) | collective-permute-done | bytes 131104 | tf_op jit(solution)/shard_map/ppermute | solution.py:335
  383.2 3.7 collective-permute-start.49
  396.2 12.4 %collective-permute-done.50 = f32[1,2,8,2048]{3,2,1,0:T(8,128)S(1)} collective-permute-done((f32[1,2,8,2048]{3,2,1,0:T(8,128)S(1)}, f32[1,2,8,2048]{3,2,1,0:T(8,128)S(1)}, u32[]{:S(2)}, u32[]{:S(2)}) %collective-permute-start.50) | collective-permute-done | bytes 131104 | tf_op jit(solution)/shard_map/ppermute | solution.py:335
  410.7 4.4 collective-permute-start.57
  415.2 6.6 %collective-permute-start.58 = (f32[1,2,8,2048]{3,2,1,0:T(8,128)S(1)}, f32[1,2,8,2048]{3,2,1,0:T(8,128)S(1)}, u32[]{:S(2)}, u32[]{:S(2)}) collective-permute-start(f32[1,2,8,2048]{3,2,1,0:T(8,128)S(1)} %get-tuple-element.25), channel_id=1, source_target_pairs={{0,28},{1,29},{2,30},{3,31},{4,24},{5,25},{6,26},{7,27},{8,20},{9,... | collective-permute-start | bytes 393224 | tf_op jit(solution)/shard_map/ppermute | solution.py:335
  422.5 3.4 collective-permute-start.60
  427.8 9.1 %collective-permute-done.58 = f32[1,2,8,2048]{3,2,1,0:T(8,128)S(1)} collective-permute-done((f32[1,2,8,2048]{3,2,1,0:T(8,128)S(1)}, f32[1,2,8,2048]{3,2,1,0:T(8,128)S(1)}, u32[]{:S(2)}, u32[]{:S(2)}) %collective-permute-start.58) | collective-permute-done | bytes 131104 | tf_op jit(solution)/shard_map/ppermute | solution.py:335
  436.9 3.6 collective-permute-done.59
  442.6 7.5 %x_inverse.2 = (f32[64,32,256]{2,1,0:T(8,128)}, f32[64,32,256]{2,1,0:T(8,128)}) custom-call(s32[1]{0:T(128)} %bitcast.base_ref, f32[32,8,256]{2,1,0:T(8,128)} %constant.31.clone.table_ref, f32[32,2,8,2048]{3,2,1,0:T(8,128)} %copy-done), custom_call_target="tpu_custom_call" | custom-call | tf_op jit(solution)/shard_map/x_inverse/pallas_call | solution.py:176
  450.1 9.1 %x_inverse.3 = (f32[64,32,512]{2,1,0:T(8,128)}, f32[64,32,512]{2,1,0:T(8,128)}) custom-call(s32[1]{0:T(128)} %constant.13.clone.1.base_ref, f32[32,8,256]{2,1,0:T(8,128)} %constant.33.clone.table_ref, f32[32,2,8,2048]{3,2,1,0:T(8,128)} %all-to-all-done.1.value_ref, f32[64,32,256]{2,1,0:T(8,128)} %get-tuple-element.20.refs_0_, ...), custom_call_target="tpu_custom_call" | custom-call | tf_op jit(solution)/shard_map/x_inverse/pallas_call | solution.py:176
  (180 shorter events, 110.8 us)
Async XLA Ops:
  8.0 203.9 %all-to-all-start = ((f32[32,2,8,2048]{3,2,1,0:T(8,128)}), f32[32,2,8,2048]{3,2,1,0:T(8,128)}, u32[]{:S(2)}, u32[]{:S(2)}) async-start(f32[32,2,8,2048]{3,2,1,0:T(8,128)} %x_forward.2), calls=%async_computation | async-start | bytes 8388608 | tf_op jit(solution)/shard_map/all_to_all | solution.py:329
  25.5 50.2 %collective-permute-start = (f32[1,2,8,2048]{3,2,1,0:T(8,128)}, f32[1,2,8,2048]{3,2,1,0:T(8,128)S(1)}, u32[]{:S(2)}, u32[]{:S(2)}) collective-permute-start(f32[1,2,8,2048]{3,2,1,0:T(8,128)} %get-tuple-element.84), channel_id=1, source_target_pairs={{0,1},{1,0},{2,3},{3,2},{4,5},{5,4},{6,7},{7,6},{8,9},{9,8},{10,11... | collective-permute-start | bytes 393224 | tf_op jit(solution)/shard_map/ppermute | solution.py:335
  25.7 61.5 %collective-permute-start.1 = (f32[1,2,8,2048]{3,2,1,0:T(8,128)}, f32[1,2,8,2048]{3,2,1,0:T(8,128)S(1)}, u32[]{:S(2)}, u32[]{:S(2)}) collective-permute-start(f32[1,2,8,2048]{3,2,1,0:T(8,128)} %get-tuple-element.83), channel_id=1, source_target_pairs={{0,2},{1,3},{2,0},{3,1},{4,6},{5,7},{6,4},{7,5},{8,10},{9,11},{10,... | collective-permute-start | bytes 393224 | tf_op jit(solution)/shard_map/ppermute | solution.py:335
  27.4 63.2 %collective-permute-start.2 = (f32[1,2,8,2048]{3,2,1,0:T(8,128)}, f32[1,2,8,2048]{3,2,1,0:T(8,128)S(1)}, u32[]{:S(2)}, u32[]{:S(2)}) collective-permute-start(f32[1,2,8,2048]{3,2,1,0:T(8,128)} %get-tuple-element.82), channel_id=1, source_target_pairs={{0,3},{1,2},{2,1},{3,0},{4,7},{5,6},{6,5},{7,4},{8,11},{9,10},{10,... | collective-permute-start | bytes 393224 | tf_op jit(solution)/shard_map/ppermute | solution.py:335
  27.4 96.6 %collective-permute-start.3 = (f32[1,2,8,2048]{3,2,1,0:T(8,128)}, f32[1,2,8,2048]{3,2,1,0:T(8,128)S(1)}, u32[]{:S(2)}, u32[]{:S(2)}) collective-permute-start(f32[1,2,8,2048]{3,2,1,0:T(8,128)} %get-tuple-element.81), channel_id=1, source_target_pairs={{0,4},{1,5},{2,6},{3,7},{4,0},{5,1},{6,2},{7,3},{8,12},{9,13},{10,... | collective-permute-start | bytes 393224 | tf_op jit(solution)/shard_map/ppermute | solution.py:335
  30.0 95.7 %collective-permute-start.4 = (f32[1,2,8,2048]{3,2,1,0:T(8,128)}, f32[1,2,8,2048]{3,2,1,0:T(8,128)S(1)}, u32[]{:S(2)}, u32[]{:S(2)}) collective-permute-start(f32[1,2,8,2048]{3,2,1,0:T(8,128)} %get-tuple-element.80), channel_id=1, source_target_pairs={{0,5},{1,4},{2,7},{3,6},{4,1},{5,0},{6,3},{7,2},{8,13},{9,12},{10,... | collective-permute-start | bytes 393224 | tf_op jit(solution)/shard_map/ppermute | solution.py:335
  75.8 50.6 %collective-permute-start.5 = (f32[1,2,8,2048]{3,2,1,0:T(8,128)}, f32[1,2,8,2048]{3,2,1,0:T(8,128)S(1)}, u32[]{:S(2)}, u32[]{:S(2)}) collective-permute-start(f32[1,2,8,2048]{3,2,1,0:T(8,128)} %get-tuple-element.79), channel_id=1, source_target_pairs={{0,6},{1,7},{2,4},{3,5},{4,2},{5,3},{6,0},{7,1},{8,14},{9,15},{10,... | collective-permute-start | bytes 393224 | tf_op jit(solution)/shard_map/ppermute | solution.py:335
  87.2 43.0 %collective-permute-start.6 = (f32[1,2,8,2048]{3,2,1,0:T(8,128)}, f32[1,2,8,2048]{3,2,1,0:T(8,128)S(1)}, u32[]{:S(2)}, u32[]{:S(2)}) collective-permute-start(f32[1,2,8,2048]{3,2,1,0:T(8,128)} %get-tuple-element.78), channel_id=1, source_target_pairs={{0,7},{1,6},{2,5},{3,4},{4,3},{5,2},{6,1},{7,0},{8,15},{9,14},{10,... | collective-permute-start | bytes 393224 | tf_op jit(solution)/shard_map/ppermute | solution.py:335
  90.5 43.0 %collective-permute-start.7 = (f32[1,2,8,2048]{3,2,1,0:T(8,128)}, f32[1,2,8,2048]{3,2,1,0:T(8,128)S(1)}, u32[]{:S(2)}, u32[]{:S(2)}) collective-permute-start(f32[1,2,8,2048]{3,2,1,0:T(8,128)} %get-tuple-element.77), channel_id=1, source_target_pairs={{0,8},{1,9},{2,10},{3,11},{4,12},{5,13},{6,14},{7,15},{8,0},{9,1},... | collective-permute-start | bytes 393224 | tf_op jit(solution)/shard_map/ppermute | solution.py:335
  137.6 19.5 %collective-permute-start.14 = (f32[1,2,8,2048]{3,2,1,0:T(8,128)S(1)}, f32[1,2,8,2048]{3,2,1,0:T(8,128)S(1)}, u32[]{:S(2)}, u32[]{:S(2)}) collective-permute-start(f32[1,2,8,2048]{3,2,1,0:T(8,128)S(1)} %get-tuple-element.70), channel_id=1, source_target_pairs={{0,15},{1,14},{2,13},{3,12},{4,11},{5,10},{6,9},{7,8},{8,7},{9,6},... | collective-permute-start | bytes 393224 | tf_op jit(solution)/shard_map/ppermute | solution.py:335
  157.2 22.0 %collective-permute-start.19 = (f32[1,2,8,2048]{3,2,1,0:T(8,128)S(1)}, f32[1,2,8,2048]{3,2,1,0:T(8,128)S(1)}, u32[]{:S(2)}, u32[]{:S(2)}) collective-permute-start(f32[1,2,8,2048]{3,2,1,0:T(8,128)S(1)} %get-tuple-element.65), channel_id=1, source_target_pairs={{0,20},{1,21},{2,22},{3,23},{4,16},{5,17},{6,18},{7,19},{8,28},{9,... | collective-permute-start | bytes 393224 | tf_op jit(solution)/shard_map/ppermute | solution.py:335
  159.4 21.0 %collective-permute-start.20 = (f32[1,2,8,2048]{3,2,1,0:T(8,128)S(1)}, f32[1,2,8,2048]{3,2,1,0:T(8,128)S(1)}, u32[]{:S(2)}, u32[]{:S(2)}) collective-permute-start(f32[1,2,8,2048]{3,2,1,0:T(8,128)S(1)} %get-tuple-element.64), channel_id=1, source_target_pairs={{0,21},{1,20},{2,23},{3,22},{4,17},{5,16},{6,19},{7,18},{8,29},{9,... | collective-permute-start | bytes 393224 | tf_op jit(solution)/shard_map/ppermute | solution.py:335
  161.6 19.8 %collective-permute-start.21 = (f32[1,2,8,2048]{3,2,1,0:T(8,128)S(1)}, f32[1,2,8,2048]{3,2,1,0:T(8,128)S(1)}, u32[]{:S(2)}, u32[]{:S(2)}) collective-permute-start(f32[1,2,8,2048]{3,2,1,0:T(8,128)S(1)} %get-tuple-element.63), channel_id=1, source_target_pairs={{0,22},{1,23},{2,20},{3,21},{4,18},{5,19},{6,16},{7,17},{8,30},{9,... | collective-permute-start | bytes 393224 | tf_op jit(solution)/shard_map/ppermute | solution.py:335
  164.3 22.0 %collective-permute-start.22 = (f32[1,2,8,2048]{3,2,1,0:T(8,128)S(1)}, f32[1,2,8,2048]{3,2,1,0:T(8,128)S(1)}, u32[]{:S(2)}, u32[]{:S(2)}) collective-permute-start(f32[1,2,8,2048]{3,2,1,0:T(8,128)S(1)} %get-tuple-element.62), channel_id=1, source_target_pairs={{0,23},{1,22},{2,21},{3,20},{4,19},{5,18},{6,17},{7,16},{8,31},{9,... | collective-permute-start | bytes 393224 | tf_op jit(solution)/shard_map/ppermute | solution.py:335
  167.8 24.7 %collective-permute-start.23 = (f32[1,2,8,2048]{3,2,1,0:T(8,128)S(1)}, f32[1,2,8,2048]{3,2,1,0:T(8,128)S(1)}, u32[]{:S(2)}, u32[]{:S(2)}) collective-permute-start(f32[1,2,8,2048]{3,2,1,0:T(8,128)S(1)} %get-tuple-element.61), channel_id=1, source_target_pairs={{0,24},{1,25},{2,26},{3,27},{4,28},{5,29},{6,30},{7,31},{8,16},{9,... | collective-permute-start | bytes 393224 | tf_op jit(solution)/shard_map/ppermute | solution.py:335
  197.7 48.9 %collective-permute-start.30 = (f32[1,2,8,2048]{3,2,1,0:T(8,128)S(1)}, f32[1,2,8,2048]{3,2,1,0:T(8,128)S(1)}, u32[]{:S(2)}, u32[]{:S(2)}) collective-permute-start(f32[1,2,8,2048]{3,2,1,0:T(8,128)S(1)} %get-tuple-element.54), channel_id=1, source_target_pairs={{0,31},{1,30},{2,29},{3,28},{4,27},{5,26},{6,25},{7,24},{8,23},{9,... | collective-permute-start | bytes 393224 | tf_op jit(solution)/shard_map/ppermute | solution.py:335
  240.8 209.3 %all-to-all-start.1 = ((f32[32,2,8,2048]{3,2,1,0:T(8,128)}), f32[32,2,8,2048]{3,2,1,0:T(8,128)}, u32[]{:S(2)}, u32[]{:S(2)}) async-start(f32[32,2,8,2048]{3,2,1,0:T(8,128)} %yz_apply.2), calls=%async_computation.1 | async-start | bytes 8388608 | tf_op jit(solution)/shard_map/all_to_all | solution.py:329
  279.6 38.5 %collective-permute-start.32 = (f32[1,2,8,2048]{3,2,1,0:T(8,128)S(1)}, f32[1,2,8,2048]{3,2,1,0:T(8,128)S(1)}, u32[]{:S(2)}, u32[]{:S(2)}) collective-permute-start(f32[1,2,8,2048]{3,2,1,0:T(8,128)S(1)} %get-tuple-element.51), channel_id=1, source_target_pairs={{0,2},{1,3},{2,0},{3,1},{4,6},{5,7},{6,4},{7,5},{8,10},{9,11},{10,... | collective-permute-start | bytes 393224 | tf_op jit(solution)/shard_map/ppermute | solution.py:335
  281.3 39.6 %collective-permute-start.33 = (f32[1,2,8,2048]{3,2,1,0:T(8,128)S(1)}, f32[1,2,8,2048]{3,2,1,0:T(8,128)S(1)}, u32[]{:S(2)}, u32[]{:S(2)}) collective-permute-start(f32[1,2,8,2048]{3,2,1,0:T(8,128)S(1)} %get-tuple-element.50), channel_id=1, source_target_pairs={{0,3},{1,2},{2,1},{3,0},{4,7},{5,6},{6,5},{7,4},{8,11},{9,10},{10,... | collective-permute-start | bytes 393224 | tf_op jit(solution)/shard_map/ppermute | solution.py:335
  281.5 73.4 %collective-permute-start.34 = (f32[1,2,8,2048]{3,2,1,0:T(8,128)S(1)}, f32[1,2,8,2048]{3,2,1,0:T(8,128)S(1)}, u32[]{:S(2)}, u32[]{:S(2)}) collective-permute-start(f32[1,2,8,2048]{3,2,1,0:T(8,128)S(1)} %get-tuple-element.49), channel_id=1, source_target_pairs={{0,4},{1,5},{2,6},{3,7},{4,0},{5,1},{6,2},{7,3},{8,12},{9,13},{10,... | collective-permute-start | bytes 393224 | tf_op jit(solution)/shard_map/ppermute | solution.py:335
  284.0 72.6 %collective-permute-start.35 = (f32[1,2,8,2048]{3,2,1,0:T(8,128)S(1)}, f32[1,2,8,2048]{3,2,1,0:T(8,128)S(1)}, u32[]{:S(2)}, u32[]{:S(2)}) collective-permute-start(f32[1,2,8,2048]{3,2,1,0:T(8,128)S(1)} %get-tuple-element.48), channel_id=1, source_target_pairs={{0,5},{1,4},{2,7},{3,6},{4,1},{5,0},{6,3},{7,2},{8,13},{9,12},{10,... | collective-permute-start | bytes 393224 | tf_op jit(solution)/shard_map/ppermute | solution.py:335
  284.1 72.5 %collective-permute-start.36 = (f32[1,2,8,2048]{3,2,1,0:T(8,128)S(1)}, f32[1,2,8,2048]{3,2,1,0:T(8,128)S(1)}, u32[]{:S(2)}, u32[]{:S(2)}) collective-permute-start(f32[1,2,8,2048]{3,2,1,0:T(8,128)S(1)} %get-tuple-element.47), channel_id=1, source_target_pairs={{0,6},{1,7},{2,4},{3,5},{4,2},{5,3},{6,0},{7,1},{8,14},{9,15},{10,... | collective-permute-start | bytes 393224 | tf_op jit(solution)/shard_map/ppermute | solution.py:335
  318.1 42.1 %collective-permute-start.37 = (f32[1,2,8,2048]{3,2,1,0:T(8,128)S(1)}, f32[1,2,8,2048]{3,2,1,0:T(8,128)S(1)}, u32[]{:S(2)}, u32[]{:S(2)}) collective-permute-start(f32[1,2,8,2048]{3,2,1,0:T(8,128)S(1)} %get-tuple-element.46), channel_id=1, source_target_pairs={{0,7},{1,6},{2,5},{3,4},{4,3},{5,2},{6,1},{7,0},{8,15},{9,14},{10,... | collective-permute-start | bytes 393224 | tf_op jit(solution)/shard_map/ppermute | solution.py:335
  320.9 42.8 %collective-permute-start.38 = (f32[1,2,8,2048]{3,2,1,0:T(8,128)S(1)}, f32[1,2,8,2048]{3,2,1,0:T(8,128)S(1)}, u32[]{:S(2)}, u32[]{:S(2)}) collective-permute-start(f32[1,2,8,2048]{3,2,1,0:T(8,128)S(1)} %get-tuple-element.45), channel_id=1, source_target_pairs={{0,8},{1,9},{2,10},{3,11},{4,12},{5,13},{6,14},{7,15},{8,0},{9,1},... | collective-permute-start | bytes 393224 | tf_op jit(solution)/shard_map/ppermute | solution.py:335
  366.4 20.5 %collective-permute-start.45 = (f32[1,2,8,2048]{3,2,1,0:T(8,128)S(1)}, f32[1,2,8,2048]{3,2,1,0:T(8,128)S(1)}, u32[]{:S(2)}, u32[]{:S(2)}) collective-permute-start(f32[1,2,8,2048]{3,2,1,0:T(8,128)S(1)} %get-tuple-element.38), channel_id=1, source_target_pairs={{0,15},{1,14},{2,13},{3,12},{4,11},{5,10},{6,9},{7,8},{8,7},{9,6},... | collective-permute-start | bytes 393224 | tf_op jit(solution)/shard_map/ppermute | solution.py:335
  368.6 20.6 %collective-permute-start.46 = (f32[1,2,8,2048]{3,2,1,0:T(8,128)S(1)}, f32[1,2,8,2048]{3,2,1,0:T(8,128)S(1)}, u32[]{:S(2)}, u32[]{:S(2)}) collective-permute-start(f32[1,2,8,2048]{3,2,1,0:T(8,128)S(1)} %get-tuple-element.37), channel_id=1, source_target_pairs={{0,16},{1,17},{2,18},{3,19},{4,20},{5,21},{6,22},{7,23},{8,24},{9,... | collective-permute-start | bytes 393224 | tf_op jit(solution)/shard_map/ppermute | solution.py:335
  386.9 21.7 %collective-permute-start.50 = (f32[1,2,8,2048]{3,2,1,0:T(8,128)S(1)}, f32[1,2,8,2048]{3,2,1,0:T(8,128)S(1)}, u32[]{:S(2)}, u32[]{:S(2)}) collective-permute-start(f32[1,2,8,2048]{3,2,1,0:T(8,128)S(1)} %get-tuple-element.33), channel_id=1, source_target_pairs={{0,20},{1,21},{2,22},{3,23},{4,16},{5,17},{6,18},{7,19},{8,28},{9,... | collective-permute-start | bytes 393224 | tf_op jit(solution)/shard_map/ppermute | solution.py:335
  389.2 19.7 %collective-permute-start.51 = (f32[1,2,8,2048]{3,2,1,0:T(8,128)S(1)}, f32[1,2,8,2048]{3,2,1,0:T(8,128)S(1)}, u32[]{:S(2)}, u32[]{:S(2)}) collective-permute-start(f32[1,2,8,2048]{3,2,1,0:T(8,128)S(1)} %get-tuple-element.32), channel_id=1, source_target_pairs={{0,21},{1,20},{2,23},{3,22},{4,17},{5,16},{6,19},{7,18},{8,29},{9,... | collective-permute-start | bytes 393224 | tf_op jit(solution)/shard_map/ppermute | solution.py:335
  389.8 20.9 %collective-permute-start.52 = (f32[1,2,8,2048]{3,2,1,0:T(8,128)S(1)}, f32[1,2,8,2048]{3,2,1,0:T(8,128)S(1)}, u32[]{:S(2)}, u32[]{:S(2)}) collective-permute-start(f32[1,2,8,2048]{3,2,1,0:T(8,128)S(1)} %get-tuple-element.31), channel_id=1, source_target_pairs={{0,22},{1,23},{2,20},{3,21},{4,18},{5,19},{6,16},{7,17},{8,30},{9,... | collective-permute-start | bytes 393224 | tf_op jit(solution)/shard_map/ppermute | solution.py:335
  392.3 22.9 %collective-permute-start.53 = (f32[1,2,8,2048]{3,2,1,0:T(8,128)S(1)}, f32[1,2,8,2048]{3,2,1,0:T(8,128)S(1)}, u32[]{:S(2)}, u32[]{:S(2)}) collective-permute-start(f32[1,2,8,2048]{3,2,1,0:T(8,128)S(1)} %get-tuple-element.30), channel_id=1, source_target_pairs={{0,23},{1,22},{2,21},{3,20},{4,19},{5,18},{6,17},{7,16},{8,31},{9,... | collective-permute-start | bytes 393224 | tf_op jit(solution)/shard_map/ppermute | solution.py:335
  395.2 26.5 %collective-permute-start.54 = (f32[1,2,8,2048]{3,2,1,0:T(8,128)S(1)}, f32[1,2,8,2048]{3,2,1,0:T(8,128)S(1)}, u32[]{:S(2)}, u32[]{:S(2)}) collective-permute-start(f32[1,2,8,2048]{3,2,1,0:T(8,128)S(1)} %get-tuple-element.29), channel_id=1, source_target_pairs={{0,24},{1,25},{2,26},{3,27},{4,28},{5,29},{6,30},{7,31},{8,16},{9,... | collective-permute-start | bytes 393224 | tf_op jit(solution)/shard_map/ppermute | solution.py:335
  415.2 21.8 %collective-permute-start.58 = (f32[1,2,8,2048]{3,2,1,0:T(8,128)S(1)}, f32[1,2,8,2048]{3,2,1,0:T(8,128)S(1)}, u32[]{:S(2)}, u32[]{:S(2)}) collective-permute-start(f32[1,2,8,2048]{3,2,1,0:T(8,128)S(1)} %get-tuple-element.25), channel_id=1, source_target_pairs={{0,28},{1,29},{2,30},{3,31},{4,24},{5,25},{6,26},{7,27},{8,20},{9,... | collective-permute-start | bytes 393224 | tf_op jit(solution)/shard_map/ppermute | solution.py:335
  (36 other events, 511.8 us)

commit v5 on v4

--- a/solution.py
+++ b/solution.py
@@ -16,6 +16,7 @@
 BLOCKS = 2
 PAIRED = 0
 MOST_PAIRS = 64
+EARLY = 4
 VMEM_LIMIT = 56 * 1024 * 1024
 
 
@@ -89,6 +90,18 @@
     return lax.dot_general(left, right, dims, precision=HIGH, preferred_element_type=jnp.float32)
 
 
+def in_halves(value):
+    high = value.astype(jnp.bfloat16)
+    return high, (value - high.astype(jnp.float32)).astype(jnp.bfloat16)
+
+
+def dot_in_halves(left, right, left_dim, right_dim):
+    dims = (((left_dim,), (right_dim,)), ((), ()))
+    mul = lambda one, two: lax.dot_general(one, two, dims, preferred_element_type=jnp.float32)
+    (left_high, left_low), (right_high, right_low) = in_halves(left), in_halves(right)
+    return mul(left_high, right_high) + (mul(left_high, right_low) + mul(left_low, right_high))
+
+
 def params():
     return pltpu.CompilerParams(vmem_limit_bytes=VMEM_LIMIT)
 
@@ -101,25 +114,29 @@
     return [(table[freq % 2 == odd][:, :half], 1 - 2 * odd, freq[freq % 2 == odd]) for odd in range(2)]
 
 
-def place_table(base_ref, table_ref, placed):
+def place_table(base_ref, table_ref, slots, placed):
     @pl.when(pl.program_id(0) == 0)
     def _():
-        for k in range(placed.shape[0]):
-            placed[k] = table_ref[k ^ base_ref[0]]
+        for n, k in enumerate(slots):
+            placed[n] = table_ref[k ^ base_ref[0]]
 
     world, rows, width = placed.shape
     return placed[...].reshape(world * rows, width)
 
 
-def x_forward_body(sign, base_ref, table_ref, one_ref, two_ref, out_ref, placed):
-    world, _, rows, cells = out_ref.shape
-    table = place_table(base_ref, table_ref, placed)
+def x_forward_body(sign, slots, base_ref, table_ref, one_ref, two_ref, *refs):
+    *outs, placed = refs
+    table = place_table(base_ref, table_ref, slots, placed)
     for a, ref in enumerate((one_ref, two_ref)):
-        values = ref[...].reshape(cells, ref.shape[-1])
+        values = ref[...].reshape(-1, ref.shape[-1])
         if sign:
             half = values.shape[1] // 2
             values = values[:, :half] + values[:, half:] if sign > 0 else values[:, :half] - values[:, half:]
-        out_ref[:, a] = dot(table, values, 1, 1).reshape(world, rows, cells)
+        spectrum = dot(table, values, 1, 1)
+        for n, out_ref in enumerate(outs):
+            count, _, rows, cells = out_ref.shape
+            size = count * rows
+            out_ref[:, a] = spectrum[n * size : (n + 1) * size].reshape(count, rows, cells)
 
 
 def cell_blocks(y_local, z_local):
@@ -129,14 +146,16 @@
     return blocks
 
 
-def x_forward(base, table, sign, fields):
+def x_forward(base, slots, table, sign, fields, pieces):
     y_local, z_local, x_count = fields[0].shape
-    world, rows, _ = table.shape
+    _, rows, width = table.shape
     blocks = cell_blocks(y_local, z_local)
     part = y_local // blocks
+    count = len(slots) // pieces
     field_spec = pl.BlockSpec((part, z_local, x_count), lambda i: (i, 0, 0))
+    out = jax.ShapeDtypeStruct((count, 2, rows, y_local * z_local), jnp.float32)
     return pl.pallas_call(
-        functools.partial(x_forward_body, sign),
+        functools.partial(x_forward_body, sign, slots),
         grid=(blocks,),
         in_specs=[
             pl.BlockSpec(memory_space=pltpu.SMEM),
@@ -144,28 +163,30 @@
             field_spec,
             field_spec,
         ],
-        out_specs=pl.BlockSpec((world, 2, rows, part * z_local), lambda i: (0, 0, 0, i)),
-        out_shape=jax.ShapeDtypeStruct((world, 2, rows, y_local * z_local), jnp.float32),
-        scratch_shapes=[pltpu.VMEM(table.shape, jnp.float32)],
+        out_specs=[pl.BlockSpec((count, 2, rows, part * z_local), lambda i: (0, 0, 0, i))] * pieces,
+        out_shape=[out] * pieces,
+        scratch_shapes=[pltpu.VMEM((len(slots), rows, width), jnp.float32)],
         compiler_params=params(),
         name="x_forward",
     )(base, table, *fields)
 
 
-def x_inverse_body(base_ref, table_ref, value_ref, *refs):
+def x_inverse_body(slots, base_ref, table_ref, value_ref, *refs):
     *refs, placed = refs
-    table = place_table(base_ref, table_ref, placed)
+    table = place_table(base_ref, table_ref, slots, placed)
     for a, out_ref in enumerate(refs[-2:]):
         world, _, rows, cells = value_ref.shape
         value = value_ref[:, a].reshape(world * rows, cells)
-        total = dot(value, table, 0, 0)
         if len(refs) == 4:
+            total = dot_in_halves(value, table, 0, 0)
             even = refs[a][...].reshape(total.shape)
             total = jnp.concatenate([even + total, even - total], axis=1)
+        else:
+            total = dot(value, table, 0, 0)
         out_ref[...] = total.reshape(out_ref.shape)
 
 
-def x_inverse(base, table, value, even, y_local, z_local):
+def x_inverse(base, slots, table, value, even, y_local, z_local):
     world, _, rows, _ = value.shape
     width = table.shape[2]
     blocks = cell_blocks(y_local, z_local)
@@ -174,7 +195,7 @@
     x_count = 2 * width if even else width
     out = jax.ShapeDtypeStruct((y_local, z_local, x_count), jnp.float32)
     return pl.pallas_call(
-        x_inverse_body,
+        functools.partial(x_inverse_body, slots),
         grid=(blocks,),
         in_specs=[
             pl.BlockSpec(memory_space=pltpu.SMEM),
@@ -206,13 +227,12 @@
     return values
 
 
-def yz_body(pz, base_ref, value_ref, y_ref, z_ref, k00, k01, k10, k11, out_ref, scratch):
+def yz_body(pz, base_ref, place_ref, value_ref, y_ref, z_ref, k00, k01, k10, k11, out_ref, scratch):
     world, _, rows, cells = value_ref.shape
     py = world // pz
     y_count = y_ref.shape[0]
     z_count = z_ref.shape[0]
     z_local = z_count // pz
-    base = base_ref[0]
     split = LANES // z_local
     tiles = cells // LANES
     block = split * tiles * rows
@@ -228,7 +248,7 @@
                 for high in range(pz // split):
                     group = []
                     for low in range(split):
-                        value = value_ref[(i * pz + high * split + low) ^ base, a]
+                        value = value_ref[place_ref[(i * pz + high * split + low) ^ base_ref[0]], a]
                         group.append(
                             jnp.concatenate([value[:, t * LANES : (t + 1) * LANES] for t in range(tiles)], axis=0)
                         )
@@ -264,7 +284,7 @@
                     lanes = slice(high * LANES, (high + 1) * LANES)
                     group = swap_groups([lines[p * size : (p + 1) * size, lanes] for p in range(split)], z_local)
                     for low in range(split):
-                        slot = (i * pz + high * split + low) ^ base
+                        slot = place_ref[(i * pz + high * split + low) ^ base_ref[0]]
                         for t in range(tiles):
                             piece = group[low][t * rows : (t + 1) * rows]
                             out_ref[slot, a, :, t * LANES : (t + 1) * LANES] = piece
@@ -273,7 +293,7 @@
             lax.fori_loop(0, py, backward, 0)
 
 
-def yz_apply(base, value, kernel, sizes):
+def yz_apply(base, slots, value, kernel, sizes):
     py, pz, y_local, z_local = sizes
     _, _, rows, cells = value.shape
     y_count, z_count = py * y_local, pz * z_local
@@ -288,13 +308,13 @@
     return pl.pallas_call(
         functools.partial(yz_body, pz),
         grid=(rows,),
-        in_specs=[pl.BlockSpec(memory_space=pltpu.SMEM), whole(value.shape), whole(y_table.shape), whole(z_table.shape)] + [k_spec] * 4,
+        in_specs=[pl.BlockSpec(memory_space=pltpu.SMEM)] * 2 + [whole(value.shape), whole(y_table.shape), whole(z_table.shape)] + [k_spec] * 4,
         out_specs=whole(value.shape),
         out_shape=jax.ShapeDtypeStruct(value.shape, jnp.float32),
         scratch_shapes=[pltpu.VMEM((2, z_count // LANES, y_count * rows, LANES), jnp.float32)],
         compiler_params=params(),
         name="yz_apply",
-    )(base, value, y_table, z_table, *kernel)
+    )(base, jnp.asarray(np.argsort(slots).astype(np.int32)), value, y_table, z_table, *kernel)
 
 
 def yz_plain(value, kernel, sizes, y_table, z_table):
@@ -328,35 +348,44 @@
     def all_at_once(value):
         return lax.all_to_all(value, AXES, split_axis=0, concat_axis=0, tiled=True)
 
-    def by_pairs(value):
-        parts = [value[:1]]
-        for k in range(1, world):
-            pairs = [(i, i ^ k) for i in range(world)]
-            parts.append(lax.ppermute(value[k : k + 1], AXES, pairs))
-        return jnp.concatenate(parts, axis=0)
-
-    paired = len(groups) == 2 and world & (world - 1) == 0 and world <= MOST_PAIRS
+    def swap(value, k):
+        return value if k == 0 else lax.ppermute(value, AXES, [(i, i ^ k) for i in range(world)])
+
+    paired = len(groups) == 2 and world & (world - 1) == 0 and 2 * EARLY <= world <= MOST_PAIRS
+    by_distance = sorted(range(world), key=lambda k: (k & (pz_count // 2) == 0, k == 0, k))
     plans = []
     for index, (table, sign, freq) in enumerate(groups):
         rows = freq.size // world
         x_terms = jnp.asarray(np.stack(axis_terms(freq, x_count)))
         x_terms = lax.dynamic_slice_in_dim(x_terms, me * rows, rows, axis=1)
         relative = paired and index == PAIRED
+        slots = by_distance if relative else list(range(world))
         base = jnp.reshape(me if relative else jnp.zeros_like(me), (1,))
-        table = jnp.asarray(table.reshape(world, rows, -1))
-        plans.append((base, table, sign, x_terms, by_pairs if relative else all_at_once))
+        plans.append((base, slots, jnp.asarray(table.reshape(world, rows, -1)), sign, x_terms, relative))
 
     arrived = []
-    for base, table, sign, _, exchange in plans:
-        arrived.append(exchange(x_forward(base, table, sign, fields)))
+    for base, slots, table, sign, _, relative in plans:
+        if relative:
+            values = []
+            for some in (slots[:EARLY], slots[EARLY:]):
+                sent = x_forward(base, some, table, sign, fields, len(some))
+                values += [swap(value, k) for value, k in zip(sent, some)]
+            arrived.append(jnp.concatenate(values, axis=0))
+        else:
+            (sent,) = x_forward(base, slots, table, sign, fields, 1)
+            arrived.append(all_at_once(sent))
     returned = []
-    for value, (base, _, _, x_terms, exchange) in zip(arrived, plans):
+    for value, (base, slots, _, _, x_terms, relative) in zip(arrived, plans):
         kernel = radial_kernel(coef, x_terms, freq_y, freq_z)
-        value = yz_apply(base, value, kernel, sizes)
-        returned.append(exchange(value))
+        value = yz_apply(base, slots, value, kernel, sizes)
+        if relative:
+            values = [swap(value[n : n + 1], k) for n, k in enumerate(slots)]
+            returned.append(jnp.concatenate(values, axis=0))
+        else:
+            returned.append(all_at_once(value))
     results = ()
-    for value, (base, table, _, _, _) in zip(returned, plans):
-        results = x_inverse(base, table, value, results, y_local, z_local)
+    for value, (base, slots, table, _, _, _) in zip(returned, plans):
+        results = x_inverse(base, slots, table, value, results, y_local, z_local)
     return tuple(results)
 
 

time: 463 us -> 527 us (1.14)
  waiting for transfers between devices: 167 us -> 232 us
  local copies, waits for them, and re-layouts: 32 us -> 10.9 us
  starting transfers between devices: 127 us -> 145 us
    ppermute x62, waiting for transfers between devices: 167 us -> 232 us  [swap(): lax.ppermute(value, AXES, [(i, i ^ k) for i in range(world)])]
    ppermute x62, starting transfers between devices: 114 us -> 133 us  [swap(): lax.ppermute(value, AXES, [(i, i ^ k) for i in range(world)])]
    unnamed x68 -> x98, local copies, waits for them, and re-layouts: 22.1 us -> 4.71 us
    pallas_call x4 -> x5, Pallas kernels: 31.5 us -> 36.5 us  [the longest x3 22 us: x_forward(): pl.pallas_call(functools.partial(x_forward_body, sign, slots), grid=(bloc...]
  transfers between devices with their start and end apart: 64 -> 64, of which waited for: 19 -> 24; matrix products, arithmetic and copies ran while one was open for 7% -> 1% of each run, Pallas kernels for 25% -> 18%
where the time goes in v5:
time: 527 us
  waiting for transfers between devices  232 us (44%)
  starting transfers between devices  145 us (28%)
  Pallas kernels  137 us (26%)
  local copies, waits for them, and re-layouts  10.9 us (2%)
    ppermute x62, waiting for transfers between devices, swap(): lax.ppermute(value, AXES, [(i, i ^ k) for i in range(world)])  232 us
    ppermute x62, starting transfers between devices, swap(): lax.ppermute(value, AXES, [(i, i ^ k) for i in range(world)])  133 us
    pallas_call x2, Pallas kernels, yz_apply(): pl.pallas_call(functools.partial(yz_body, pz), grid=(rows,), in_specs=[pl...  57.9 us
    pallas_call x2, Pallas kernels, radial_kernel(): pl.pallas_call(radial_body, grid=(rows,), in_specs=[scalars, scalars, pl....  42.5 us
    pallas_call x3, Pallas kernels, x_forward(): pl.pallas_call(functools.partial(x_forward_body, sign, slots), grid=(bloc...  22 us
    pallas_call x2, Pallas kernels, x_inverse(): pl.pallas_call(functools.partial(x_inverse_body, slots), grid=(blocks,),...  14.5 us
    all_to_all x2, starting transfers between devices, all_at_once(): return lax.all_to_all(value, AXES, split_axis=0, concat_axis=0, tiled=True)  12 us
  transfers between devices with their start and end apart: 64, of which 24 were waited for; matrix products, arithmetic and copies ran while one was open for 1% of the time, Pallas kernels for 18%

profile of v5, /device:TPU:0, one launch (start us, length us, event | category | flops | bytes accessed | tf_op | source)
XLA Modules:
  0.0 526.7 jit_solution(16143739288130509489)
XLA Ops:
  0.6 7.4 %x_forward.3 = f32[32,2,8,2048]{3,2,1,0:T(8,128)} custom-call(s32[1]{0:T(128)} %constant.14.clone.1.base_ref, f32[32,8,256]{2,1,0:T(8,128)} %constant.37.clone.table_ref, f32[64,32,512]{2,1,0:T(8,128)} %one_ref.5, f32[64,32,512]{2,1,0:T(8,128)} %two_ref.5), custom_call_target="tpu_custom_call" | custom-call | tf_op jit(solution)/shard_map/x_forward/pallas_call | solution.py:157
  8.0 7.5 %all-to-all-start = ((f32[32,2,8,2048]{3,2,1,0:T(8,128)}), f32[32,2,8,2048]{3,2,1,0:T(8,128)}, u32[]{:S(2)}, u32[]{:S(2)}) async-start(f32[32,2,8,2048]{3,2,1,0:T(8,128)} %x_forward.3), calls=%async_computation | async-start | bytes 8388608 | tf_op jit(solution)/shard_map/all_to_all | solution.py:349
  15.5 6.8 %x_forward.4 = (f32[1,2,8,2048]{3,2,1,0:T(8,128)}, f32[1,2,8,2048]{3,2,1,0:T(8,128)}, f32[1,2,8,2048]{3,2,1,0:T(8,128)}, f32[1,2,8,2048]{3,2,1,0:T(8,128)}) custom-call(s32[1]{0:T(128)} %bitcast.base_ref, f32[32,8,256]{2,1,0:T(8,128)} %constant.35.clone.table_ref, f32[64,32,512]{2,1,0:T(8,128)} %one_ref.5, f32[64,32,512]{2,1,0:T(8,128)} %two_ref.5), custom_call_target="tpu_custom_call" | custom-call | tf_op jit(solution)/shard_map/x_forward/pallas_call | solution.py:157
  28.6 7.8 %x_forward.5 = (f32[1,2,8,2048]{3,2,1,0:T(8,128)}, f32[1,2,8,2048]{3,2,1,0:T(8,128)}, f32[1,2,8,2048]{3,2,1,0:T(8,128)}, f32[1,2,8,2048]{3,2,1,0:T(8,128)}, f32[...) custom-call(s32[1]{0:T(128)} %bitcast.base_ref, ...), custom_call_target="tpu_custom_call" | custom-call | tf_op jit(solution)/shard_map/x_forward/pallas_call | solution.py:157
  39.5 21.2 %radial_kernel.2 = (f32[8,256,256]{2,1,0:T(8,128)}, f32[8,256,256]{2,1,0:T(8,128)}, f32[8,256,256]{2,1,0:T(8,128)}, f32[8,256,256]{2,1,0:T(8,128)}) custom-call(f32[32]{0:T(128)} %reshape.11.coef_ref, f32[2,8]{1,0:T(2,128)} %get-tuple-element.118.x_ref, f32[2,256,1]{2,1,0:T(8,128)} %constant.38.clone.y_ref, f32[2,256]{1,0:T(2,128)} %constant.34.clone.z_ref), custom_call_target="tpu_custom_call" | custom-call | tf_op jit(solution)/shard_map/radial_kernel/pallas_call | solution.py:72
  60.8 21.3 %radial_kernel.3 = (f32[8,256,256]{2,1,0:T(8,128)}, f32[8,256,256]{2,1,0:T(8,128)}, f32[8,256,256]{2,1,0:T(8,128)}, f32[8,256,256]{2,1,0:T(8,128)}) custom-call(f32[32]{0:T(128)} %reshape.11.coef_ref, f32[2,8]{1,0:T(2,128)} %get-tuple-element.117.x_ref, f32[2,256,1]{2,1,0:T(8,128)} %constant.38.clone.y_ref, f32[2,256]{1,0:T(2,128)} %constant.34.clone.z_ref), custom_call_target="tpu_custom_call" | custom-call | tf_op jit(solution)/shard_map/radial_kernel/pallas_call | solution.py:72
  82.0 44.8 %collective-permute-done = f32[1,2,8,2048]{3,2,1,0:T(8,128)S(1)} collective-permute-done((f32[1,2,8,2048]{3,2,1,0:T(8,128)}, f32[1,2,8,2048]{3,2,1,0:T(8,128)S(1)}, u32[]{:S(2)}, u32[]{:S(2)}) %collective-permute-start) | collective-permute-done | bytes 131104 | tf_op jit(solution)/shard_map/ppermute | solution.py:352
  131.0 5.5 %collective-permute-start.7 = (f32[1,2,8,2048]{3,2,1,0:T(8,128)}, f32[1,2,8,2048]{3,2,1,0:T(8,128)S(1)}, u32[]{:S(2)}, u32[]{:S(2)}) collective-permute-start(f32[1,2,8,2048]{3,2,1,0:T(8,128)} %get-tuple-element.55), channel_id=1, source_target_pairs={{0,15},{1,14},{2,13},{3,12},{4,11},{5,10},{6,9},{7,8},{8,7},{9,6},... | collective-permute-start | bytes 393224 | tf_op jit(solution)/shard_map/ppermute | solution.py:352
  136.4 7.8 %collective-permute-start.8 = (f32[1,2,8,2048]{3,2,1,0:T(8,128)}, f32[1,2,8,2048]{3,2,1,0:T(8,128)S(1)}, u32[]{:S(2)}, u32[]{:S(2)}) collective-permute-start(f32[1,2,8,2048]{3,2,1,0:T(8,128)} %get-tuple-element.56), channel_id=1, source_target_pairs={{0,20},{1,21},{2,22},{3,23},{4,16},{5,17},{6,18},{7,19},{8,28},{9,... | collective-permute-start | bytes 393224 | tf_op jit(solution)/shard_map/ppermute | solution.py:352
  148.7 8.4 %collective-permute-start.10 = (f32[1,2,8,2048]{3,2,1,0:T(8,128)}, f32[1,2,8,2048]{3,2,1,0:T(8,128)S(1)}, u32[]{:S(2)}, u32[]{:S(2)}) collective-permute-start(f32[1,2,8,2048]{3,2,1,0:T(8,128)} %get-tuple-element.58), channel_id=1, source_target_pairs={{0,22},{1,23},{2,20},{3,21},{4,18},{5,19},{6,16},{7,17},{8,30},{9,... | collective-permute-start | bytes 393224 | tf_op jit(solution)/shard_map/ppermute | solution.py:352
  159.5 10.6 %collective-permute-start.12 = (f32[1,2,8,2048]{3,2,1,0:T(8,128)}, f32[1,2,8,2048]{3,2,1,0:T(8,128)S(1)}, u32[]{:S(2)}, u32[]{:S(2)}) collective-permute-start(f32[1,2,8,2048]{3,2,1,0:T(8,128)} %get-tuple-element.60), channel_id=1, source_target_pairs={{0,28},{1,29},{2,30},{3,31},{4,24},{5,25},{6,26},{7,27},{8,20},{9,... | collective-permute-start | bytes 393224 | tf_op jit(solution)/shard_map/ppermute | solution.py:352
  170.1 5.4 %collective-permute-done.8 = f32[1,2,8,2048]{3,2,1,0:T(8,128)S(1)} collective-permute-done((f32[1,2,8,2048]{3,2,1,0:T(8,128)}, f32[1,2,8,2048]{3,2,1,0:T(8,128)S(1)}, u32[]{:S(2)}, u32[]{:S(2)}) %collective-permute-start.8) | collective-permute-done | bytes 131104 | tf_op jit(solution)/shard_map/ppermute | solution.py:352
  177.2 6.0 %collective-permute-start.15 = (f32[1,2,8,2048]{3,2,1,0:T(8,128)}, f32[1,2,8,2048]{3,2,1,0:T(8,128)S(1)}, u32[]{:S(2)}, u32[]{:S(2)}) collective-permute-start(f32[1,2,8,2048]{3,2,1,0:T(8,128)} %get-tuple-element.63), channel_id=1, source_target_pairs={{0,31},{1,30},{2,29},{3,28},{4,27},{5,26},{6,25},{7,24},{8,23},{9,... | collective-permute-start | bytes 393224 | tf_op jit(solution)/shard_map/ppermute | solution.py:352
  183.3 9.6 %collective-permute-done.12 = f32[1,2,8,2048]{3,2,1,0:T(8,128)S(1)} collective-permute-done((f32[1,2,8,2048]{3,2,1,0:T(8,128)}, f32[1,2,8,2048]{3,2,1,0:T(8,128)S(1)}, u32[]{:S(2)}, u32[]{:S(2)}) %collective-permute-start.12) | collective-permute-done | bytes 131104 | tf_op jit(solution)/shard_map/ppermute | solution.py:352
  197.1 5.3 %collective-permute-start.21 = (f32[1,2,8,2048]{3,2,1,0:T(8,128)S(1)}, f32[1,2,8,2048]{3,2,1,0:T(8,128)S(1)}, u32[]{:S(2)}, u32[]{:S(2)}) collective-permute-start(f32[1,2,8,2048]{3,2,1,0:T(8,128)S(1)} %copy-done.15), channel_id=1, source_target_pairs={{0,10},{1,11},{2,8},{3,9},{4,14},{5,15},{6,12},{7,13},{8,2},{9,3},... | collective-permute-start | bytes 393224 | tf_op jit(solution)/shard_map/ppermute | solution.py:352
  204.2 5.3 collective-permute-done.20
  221.7 6.7 %collective-permute-done.27 = f32[1,2,8,2048]{3,2,1,0:T(8,128)S(1)} collective-permute-done((f32[1,2,8,2048]{3,2,1,0:T(8,128)S(1)}, f32[1,2,8,2048]{3,2,1,0:T(8,128)S(1)}, u32[]{:S(2)}, u32[]{:S(2)}) %collective-permute-start.27) | collective-permute-done | bytes 131104 | tf_op jit(solution)/shard_map/ppermute | solution.py:352
  231.8 29.0 %yz_apply.3 = f32[32,2,8,2048]{3,2,1,0:T(8,128)} custom-call(s32[1]{0:T(128)} %bitcast.base_ref, s32[32]{0:T(128)} %constant.41.clone.place_ref, f32[32,2,8,2048]{3,2,1,0:T(8,128)} %copy-done, f32[256,256]{1,0:T(8,128)} %constant.40.clone.y_ref, f32[256,256]{1,0:T(8,128)} %constant.39.clone.z_ref, f32[8,256,256]{2,1,0:T(8,128)} %get-tuple-element.80.k00, ...), custom_call_target="tpu_custom_call" | custom-call | tf_op jit(solution)/shard_map/yz_apply/pallas_call | solution.py:308
  261.2 29.0 %yz_apply.2 = f32[32,2,8,2048]{3,2,1,0:T(8,128)} custom-call(s32[1]{0:T(128)} %constant.14.clone.1.base_ref, s32[32]{0:T(128)} %call_exported.0.place_ref, f32[32,2,8,2048]{3,2,1,0:T(8,128)} %all-to-all-done.value_ref, f32[256,256]{1,0:T(8,128)} %constant.40.clone.y_ref, f32[256,256]{1,0:T(8,128)} %constant.39.clone.z_ref, ...), custom_call_target="tpu_custom_call" | custom-call | tf_op jit(solution)/shard_map/yz_apply/pallas_call | solution.py:308
  306.3 99.9 %collective-permute-done.31 = f32[1,2,8,2048]{3,2,1,0:T(8,128)S(1)} collective-permute-done((f32[1,2,8,2048]{3,2,1,0:T(8,128)S(1)}, f32[1,2,8,2048]{3,2,1,0:T(8,128)S(1)}, u32[]{:S(2)}, u32[]{:S(2)}) %collective-permute-start.31) | collective-permute-done | bytes 131104 | tf_op jit(solution)/shard_map/ppermute | solution.py:352
  410.3 5.5 %collective-permute-start.38 = (f32[1,2,8,2048]{3,2,1,0:T(8,128)S(1)}, f32[1,2,8,2048]{3,2,1,0:T(8,128)S(1)}, u32[]{:S(2)}, u32[]{:S(2)}) collective-permute-start(f32[1,2,8,2048]{3,2,1,0:T(8,128)S(1)} %get-tuple-element.109), channel_id=1, source_target_pairs={{0,15},{1,14},{2,13},{3,12},{4,11},{5,10},{6,9},{7,8},{8,7},{9,6},... | collective-permute-start | bytes 393224 | tf_op jit(solution)/shard_map/ppermute | solution.py:352
  415.7 7.7 %collective-permute-start.39 = (f32[1,2,8,2048]{3,2,1,0:T(8,128)S(1)}, f32[1,2,8,2048]{3,2,1,0:T(8,128)S(1)}, u32[]{:S(2)}, u32[]{:S(2)}) collective-permute-start(f32[1,2,8,2048]{3,2,1,0:T(8,128)S(1)} %get-tuple-element.108), channel_id=1, source_target_pairs={{0,20},{1,21},{2,22},{3,23},{4,16},{5,17},{6,18},{7,19},{8,28},{9,... | collective-permute-start | bytes 393224 | tf_op jit(solution)/shard_map/ppermute | solution.py:352
  426.4 7.3 %collective-permute-done.36 = f32[1,2,8,2048]{3,2,1,0:T(8,128)S(1)} collective-permute-done((f32[1,2,8,2048]{3,2,1,0:T(8,128)S(1)}, f32[1,2,8,2048]{3,2,1,0:T(8,128)S(1)}, u32[]{:S(2)}, u32[]{:S(2)}) %collective-permute-start.36) | collective-permute-done | bytes 131104 | tf_op jit(solution)/shard_map/ppermute | solution.py:352
  438.8 9.1 %collective-permute-start.43 = (f32[1,2,8,2048]{3,2,1,0:T(8,128)S(1)}, f32[1,2,8,2048]{3,2,1,0:T(8,128)S(1)}, u32[]{:S(2)}, u32[]{:S(2)}) collective-permute-start(f32[1,2,8,2048]{3,2,1,0:T(8,128)S(1)} %get-tuple-element.104), channel_id=1, source_target_pairs={{0,28},{1,29},{2,30},{3,31},{4,24},{5,25},{6,26},{7,27},{8,20},{9,... | collective-permute-start | bytes 393224 | tf_op jit(solution)/shard_map/ppermute | solution.py:352
  447.9 6.9 %collective-permute-done.39 = f32[1,2,8,2048]{3,2,1,0:T(8,128)S(1)} collective-permute-done((f32[1,2,8,2048]{3,2,1,0:T(8,128)S(1)}, f32[1,2,8,2048]{3,2,1,0:T(8,128)S(1)}, u32[]{:S(2)}, u32[]{:S(2)}) %collective-permute-start.39) | collective-permute-done | bytes 131104 | tf_op jit(solution)/shard_map/ppermute | solution.py:352
  456.5 6.0 %collective-permute-start.46 = (f32[1,2,8,2048]{3,2,1,0:T(8,128)S(1)}, f32[1,2,8,2048]{3,2,1,0:T(8,128)S(1)}, u32[]{:S(2)}, u32[]{:S(2)}) collective-permute-start(f32[1,2,8,2048]{3,2,1,0:T(8,128)S(1)} %get-tuple-element.101), channel_id=1, source_target_pairs={{0,31},{1,30},{2,29},{3,28},{4,27},{5,26},{6,25},{7,24},{8,23},{9,... | collective-permute-start | bytes 393224 | tf_op jit(solution)/shard_map/ppermute | solution.py:352
  462.6 9.6 %collective-permute-done.43 = f32[1,2,8,2048]{3,2,1,0:T(8,128)S(1)} collective-permute-done((f32[1,2,8,2048]{3,2,1,0:T(8,128)S(1)}, f32[1,2,8,2048]{3,2,1,0:T(8,128)S(1)}, u32[]{:S(2)}, u32[]{:S(2)}) %collective-permute-start.43) | collective-permute-done | bytes 131104 | tf_op jit(solution)/shard_map/ppermute | solution.py:352
  476.4 5.2 collective-permute-start.52
  483.4 5.4 %collective-permute-done.51 = f32[1,2,8,2048]{3,2,1,0:T(8,128)S(1)} collective-permute-done((f32[1,2,8,2048]{3,2,1,0:T(8,128)S(1)}, f32[1,2,8,2048]{3,2,1,0:T(8,128)S(1)}, u32[]{:S(2)}, u32[]{:S(2)}) %collective-permute-start.51) | collective-permute-done | bytes 131104 | tf_op jit(solution)/shard_map/ppermute | solution.py:352
  501.8 6.3 %collective-permute-done.58 = f32[1,2,8,2048]{3,2,1,0:T(8,128)S(1)} collective-permute-done((f32[1,2,8,2048]{3,2,1,0:T(8,128)S(1)}, f32[1,2,8,2048]{3,2,1,0:T(8,128)S(1)}, u32[]{:S(2)}, u32[]{:S(2)}) %collective-permute-start.58) | collective-permute-done | bytes 131104 | tf_op jit(solution)/shard_map/ppermute | solution.py:352
  512.2 7.5 %x_inverse.2 = (f32[64,32,256]{2,1,0:T(8,128)}, f32[64,32,256]{2,1,0:T(8,128)}) custom-call(s32[1]{0:T(128)} %bitcast.base_ref, f32[32,8,256]{2,1,0:T(8,128)} %constant.35.clone.table_ref, f32[32,2,8,2048]{3,2,1,0:T(8,128)} %copy-done.1), custom_call_target="tpu_custom_call" | custom-call | tf_op jit(solution)/shard_map/x_inverse/pallas_call | solution.py:197
  519.7 6.9 %x_inverse.3 = (f32[64,32,512]{2,1,0:T(8,128)}, f32[64,32,512]{2,1,0:T(8,128)}) custom-call(s32[1]{0:T(128)} %constant.14.clone.1.base_ref, f32[32,8,256]{2,1,0:T(8,128)} %constant.37.clone.table_ref, f32[32,2,8,2048]{3,2,1,0:T(8,128)} %all-to-all-done.1.value_ref, f32[64,32,256]{2,1,0:T(8,128)} %get-tuple-element.84.refs_0_, ...), custom_call_target="tpu_custom_call" | custom-call | tf_op jit(solution)/shard_map/x_inverse/pallas_call | solution.py:197
  (210 shorter events, 96.7 us)
Async XLA Ops:
  8.0 252.7 %all-to-all-start = ((f32[32,2,8,2048]{3,2,1,0:T(8,128)}), f32[32,2,8,2048]{3,2,1,0:T(8,128)}, u32[]{:S(2)}, u32[]{:S(2)}) async-start(f32[32,2,8,2048]{3,2,1,0:T(8,128)} %x_forward.3), calls=%async_computation | async-start | bytes 8388608 | tf_op jit(solution)/shard_map/all_to_all | solution.py:349
  22.3 104.5 %collective-permute-start = (f32[1,2,8,2048]{3,2,1,0:T(8,128)}, f32[1,2,8,2048]{3,2,1,0:T(8,128)S(1)}, u32[]{:S(2)}, u32[]{:S(2)}) collective-permute-start(f32[1,2,8,2048]{3,2,1,0:T(8,128)} %get-tuple-element.48), channel_id=1, source_target_pairs={{0,4},{1,5},{2,6},{3,7},{4,0},{5,1},{6,2},{7,3},{8,12},{9,13},{10,... | collective-permute-start | bytes 393224 | tf_op jit(solution)/shard_map/ppermute | solution.py:352
  24.9 103.6 %collective-permute-start.1 = (f32[1,2,8,2048]{3,2,1,0:T(8,128)}, f32[1,2,8,2048]{3,2,1,0:T(8,128)S(1)}, u32[]{:S(2)}, u32[]{:S(2)}) collective-permute-start(f32[1,2,8,2048]{3,2,1,0:T(8,128)} %get-tuple-element.49), channel_id=1, source_target_pairs={{0,5},{1,4},{2,7},{3,6},{4,1},{5,0},{6,3},{7,2},{8,13},{9,12},{10,... | collective-permute-start | bytes 393224 | tf_op jit(solution)/shard_map/ppermute | solution.py:352
  24.9 106.0 %collective-permute-start.2 = (f32[1,2,8,2048]{3,2,1,0:T(8,128)}, f32[1,2,8,2048]{3,2,1,0:T(8,128)S(1)}, u32[]{:S(2)}, u32[]{:S(2)}) collective-permute-start(f32[1,2,8,2048]{3,2,1,0:T(8,128)} %get-tuple-element.50), channel_id=1, source_target_pairs={{0,6},{1,7},{2,4},{3,5},{4,2},{5,3},{6,0},{7,1},{8,14},{9,15},{10,... | collective-permute-start | bytes 393224 | tf_op jit(solution)/shard_map/ppermute | solution.py:352
  28.3 108.2 %collective-permute-start.3 = (f32[1,2,8,2048]{3,2,1,0:T(8,128)}, f32[1,2,8,2048]{3,2,1,0:T(8,128)S(1)}, u32[]{:S(2)}, u32[]{:S(2)}) collective-permute-start(f32[1,2,8,2048]{3,2,1,0:T(8,128)} %get-tuple-element.51), channel_id=1, source_target_pairs={{0,7},{1,6},{2,5},{3,4},{4,3},{5,2},{6,1},{7,0},{8,15},{9,14},{10,... | collective-permute-start | bytes 393224 | tf_op jit(solution)/shard_map/ppermute | solution.py:352
  36.5 110.5 %collective-permute-start.4 = (f32[1,2,8,2048]{3,2,1,0:T(8,128)}, f32[1,2,8,2048]{3,2,1,0:T(8,128)S(1)}, u32[]{:S(2)}, u32[]{:S(2)}) collective-permute-start(f32[1,2,8,2048]{3,2,1,0:T(8,128)} %get-tuple-element.52), channel_id=1, source_target_pairs={{0,12},{1,13},{2,14},{3,15},{4,8},{5,9},{6,10},{7,11},{8,4},{9,5},... | collective-permute-start | bytes 393224 | tf_op jit(solution)/shard_map/ppermute | solution.py:352
  126.8 21.9 %collective-permute-start.5 = (f32[1,2,8,2048]{3,2,1,0:T(8,128)}, f32[1,2,8,2048]{3,2,1,0:T(8,128)S(1)}, u32[]{:S(2)}, u32[]{:S(2)}) collective-permute-start(f32[1,2,8,2048]{3,2,1,0:T(8,128)} %get-tuple-element.53), channel_id=1, source_target_pairs={{0,13},{1,12},{2,15},{3,14},{4,9},{5,8},{6,11},{7,10},{8,5},{9,4},... | collective-permute-start | bytes 393224 | tf_op jit(solution)/shard_map/ppermute | solution.py:352
  128.5 28.6 %collective-permute-start.6 = (f32[1,2,8,2048]{3,2,1,0:T(8,128)}, f32[1,2,8,2048]{3,2,1,0:T(8,128)S(1)}, u32[]{:S(2)}, u32[]{:S(2)}) collective-permute-start(f32[1,2,8,2048]{3,2,1,0:T(8,128)} %get-tuple-element.54), channel_id=1, source_target_pairs={{0,14},{1,15},{2,12},{3,13},{4,10},{5,11},{6,8},{7,9},{8,6},{9,7},... | collective-permute-start | bytes 393224 | tf_op jit(solution)/shard_map/ppermute | solution.py:352
  131.0 28.5 %collective-permute-start.7 = (f32[1,2,8,2048]{3,2,1,0:T(8,128)}, f32[1,2,8,2048]{3,2,1,0:T(8,128)S(1)}, u32[]{:S(2)}, u32[]{:S(2)}) collective-permute-start(f32[1,2,8,2048]{3,2,1,0:T(8,128)} %get-tuple-element.55), channel_id=1, source_target_pairs={{0,15},{1,14},{2,13},{3,12},{4,11},{5,10},{6,9},{7,8},{8,7},{9,6},... | collective-permute-start | bytes 393224 | tf_op jit(solution)/shard_map/ppermute | solution.py:352
  136.4 39.1 %collective-permute-start.8 = (f32[1,2,8,2048]{3,2,1,0:T(8,128)}, f32[1,2,8,2048]{3,2,1,0:T(8,128)S(1)}, u32[]{:S(2)}, u32[]{:S(2)}) collective-permute-start(f32[1,2,8,2048]{3,2,1,0:T(8,128)} %get-tuple-element.56), channel_id=1, source_target_pairs={{0,20},{1,21},{2,22},{3,23},{4,16},{5,17},{6,18},{7,19},{8,28},{9,... | collective-permute-start | bytes 393224 | tf_op jit(solution)/shard_map/ppermute | solution.py:352
  147.1 30.1 %collective-permute-start.9 = (f32[1,2,8,2048]{3,2,1,0:T(8,128)}, f32[1,2,8,2048]{3,2,1,0:T(8,128)S(1)}, u32[]{:S(2)}, u32[]{:S(2)}) collective-permute-start(f32[1,2,8,2048]{3,2,1,0:T(8,128)} %get-tuple-element.57), channel_id=1, source_target_pairs={{0,21},{1,20},{2,23},{3,22},{4,17},{5,16},{6,19},{7,18},{8,29},{9,... | collective-permute-start | bytes 393224 | tf_op jit(solution)/shard_map/ppermute | solution.py:352
  148.7 28.5 %collective-permute-start.10 = (f32[1,2,8,2048]{3,2,1,0:T(8,128)}, f32[1,2,8,2048]{3,2,1,0:T(8,128)S(1)}, u32[]{:S(2)}, u32[]{:S(2)}) collective-permute-start(f32[1,2,8,2048]{3,2,1,0:T(8,128)} %get-tuple-element.58), channel_id=1, source_target_pairs={{0,22},{1,23},{2,20},{3,21},{4,18},{5,19},{6,16},{7,17},{8,30},{9,... | collective-permute-start | bytes 393224 | tf_op jit(solution)/shard_map/ppermute | solution.py:352
  157.2 26.0 %collective-permute-start.11 = (f32[1,2,8,2048]{3,2,1,0:T(8,128)}, f32[1,2,8,2048]{3,2,1,0:T(8,128)S(1)}, u32[]{:S(2)}, u32[]{:S(2)}) collective-permute-start(f32[1,2,8,2048]{3,2,1,0:T(8,128)} %get-tuple-element.59), channel_id=1, source_target_pairs={{0,23},{1,22},{2,21},{3,20},{4,19},{5,18},{6,17},{7,16},{8,31},{9,... | collective-permute-start | bytes 393224 | tf_op jit(solution)/shard_map/ppermute | solution.py:352
  159.5 33.5 %collective-permute-start.12 = (f32[1,2,8,2048]{3,2,1,0:T(8,128)}, f32[1,2,8,2048]{3,2,1,0:T(8,128)S(1)}, u32[]{:S(2)}, u32[]{:S(2)}) collective-permute-start(f32[1,2,8,2048]{3,2,1,0:T(8,128)} %get-tuple-element.60), channel_id=1, source_target_pairs={{0,28},{1,29},{2,30},{3,31},{4,24},{5,25},{6,26},{7,27},{8,20},{9,... | collective-permute-start | bytes 393224 | tf_op jit(solution)/shard_map/ppermute | solution.py:352
  175.5 19.1 %collective-permute-start.13 = (f32[1,2,8,2048]{3,2,1,0:T(8,128)}, f32[1,2,8,2048]{3,2,1,0:T(8,128)S(1)}, u32[]{:S(2)}, u32[]{:S(2)}) collective-permute-start(f32[1,2,8,2048]{3,2,1,0:T(8,128)} %get-tuple-element.61), channel_id=1, source_target_pairs={{0,29},{1,28},{2,31},{3,30},{4,25},{5,24},{6,27},{7,26},{8,21},{9,... | collective-permute-start | bytes 393224 | tf_op jit(solution)/shard_map/ppermute | solution.py:352
  177.2 18.4 %collective-permute-start.15 = (f32[1,2,8,2048]{3,2,1,0:T(8,128)}, f32[1,2,8,2048]{3,2,1,0:T(8,128)S(1)}, u32[]{:S(2)}, u32[]{:S(2)}) collective-permute-start(f32[1,2,8,2048]{3,2,1,0:T(8,128)} %get-tuple-element.63), channel_id=1, source_target_pairs={{0,31},{1,30},{2,29},{3,28},{4,27},{5,26},{6,25},{7,24},{8,23},{9,... | collective-permute-start | bytes 393224 | tf_op jit(solution)/shard_map/ppermute | solution.py:352
  290.2 229.5 %all-to-all-start.1 = ((f32[32,2,8,2048]{3,2,1,0:T(8,128)}), f32[32,2,8,2048]{3,2,1,0:T(8,128)}, u32[]{:S(2)}, u32[]{:S(2)}) async-start(f32[32,2,8,2048]{3,2,1,0:T(8,128)} %yz_apply.2), calls=%async_computation.1 | async-start | bytes 8388608 | tf_op jit(solution)/shard_map/all_to_all | solution.py:349
  296.3 109.8 %collective-permute-start.31 = (f32[1,2,8,2048]{3,2,1,0:T(8,128)S(1)}, f32[1,2,8,2048]{3,2,1,0:T(8,128)S(1)}, u32[]{:S(2)}, u32[]{:S(2)}) collective-permute-start(f32[1,2,8,2048]{3,2,1,0:T(8,128)S(1)} %get-tuple-element.116), channel_id=1, source_target_pairs={{0,4},{1,5},{2,6},{3,7},{4,0},{5,1},{6,2},{7,3},{8,12},{9,13},{10,... | collective-permute-start | bytes 393224 | tf_op jit(solution)/shard_map/ppermute | solution.py:352
  300.9 106.9 %collective-permute-start.32 = (f32[1,2,8,2048]{3,2,1,0:T(8,128)S(1)}, f32[1,2,8,2048]{3,2,1,0:T(8,128)S(1)}, u32[]{:S(2)}, u32[]{:S(2)}) collective-permute-start(f32[1,2,8,2048]{3,2,1,0:T(8,128)S(1)} %get-tuple-element.115), channel_id=1, source_target_pairs={{0,5},{1,4},{2,7},{3,6},{4,1},{5,0},{6,3},{7,2},{8,13},{9,12},{10,... | collective-permute-start | bytes 393224 | tf_op jit(solution)/shard_map/ppermute | solution.py:352
  301.0 109.3 %collective-permute-start.33 = (f32[1,2,8,2048]{3,2,1,0:T(8,128)S(1)}, f32[1,2,8,2048]{3,2,1,0:T(8,128)S(1)}, u32[]{:S(2)}, u32[]{:S(2)}) collective-permute-start(f32[1,2,8,2048]{3,2,1,0:T(8,128)S(1)} %get-tuple-element.114), channel_id=1, source_target_pairs={{0,6},{1,7},{2,4},{3,5},{4,2},{5,3},{6,0},{7,1},{8,14},{9,15},{10,... | collective-permute-start | bytes 393224 | tf_op jit(solution)/shard_map/ppermute | solution.py:352
  304.3 111.4 %collective-permute-start.34 = (f32[1,2,8,2048]{3,2,1,0:T(8,128)S(1)}, f32[1,2,8,2048]{3,2,1,0:T(8,128)S(1)}, u32[]{:S(2)}, u32[]{:S(2)}) collective-permute-start(f32[1,2,8,2048]{3,2,1,0:T(8,128)S(1)} %get-tuple-element.113), channel_id=1, source_target_pairs={{0,7},{1,6},{2,5},{3,4},{4,3},{5,2},{6,1},{7,0},{8,15},{9,14},{10,... | collective-permute-start | bytes 393224 | tf_op jit(solution)/shard_map/ppermute | solution.py:352
  304.6 121.8 %collective-permute-start.35 = (f32[1,2,8,2048]{3,2,1,0:T(8,128)S(1)}, f32[1,2,8,2048]{3,2,1,0:T(8,128)S(1)}, u32[]{:S(2)}, u32[]{:S(2)}) collective-permute-start(f32[1,2,8,2048]{3,2,1,0:T(8,128)S(1)} %get-tuple-element.112), channel_id=1, source_target_pairs={{0,12},{1,13},{2,14},{3,15},{4,8},{5,9},{6,10},{7,11},{8,4},{9,5},... | collective-permute-start | bytes 393224 | tf_op jit(solution)/shard_map/ppermute | solution.py:352
  406.1 27.5 %collective-permute-start.36 = (f32[1,2,8,2048]{3,2,1,0:T(8,128)S(1)}, f32[1,2,8,2048]{3,2,1,0:T(8,128)S(1)}, u32[]{:S(2)}, u32[]{:S(2)}) collective-permute-start(f32[1,2,8,2048]{3,2,1,0:T(8,128)S(1)} %get-tuple-element.111), channel_id=1, source_target_pairs={{0,13},{1,12},{2,15},{3,14},{4,9},{5,8},{6,11},{7,10},{8,5},{9,4},... | collective-permute-start | bytes 393224 | tf_op jit(solution)/shard_map/ppermute | solution.py:352
  407.8 28.6 %collective-permute-start.37 = (f32[1,2,8,2048]{3,2,1,0:T(8,128)S(1)}, f32[1,2,8,2048]{3,2,1,0:T(8,128)S(1)}, u32[]{:S(2)}, u32[]{:S(2)}) collective-permute-start(f32[1,2,8,2048]{3,2,1,0:T(8,128)S(1)} %get-tuple-element.110), channel_id=1, source_target_pairs={{0,14},{1,15},{2,12},{3,13},{4,10},{5,11},{6,8},{7,9},{8,6},{9,7},... | collective-permute-start | bytes 393224 | tf_op jit(solution)/shard_map/ppermute | solution.py:352
  410.3 28.5 %collective-permute-start.38 = (f32[1,2,8,2048]{3,2,1,0:T(8,128)S(1)}, f32[1,2,8,2048]{3,2,1,0:T(8,128)S(1)}, u32[]{:S(2)}, u32[]{:S(2)}) collective-permute-start(f32[1,2,8,2048]{3,2,1,0:T(8,128)S(1)} %get-tuple-element.109), channel_id=1, source_target_pairs={{0,15},{1,14},{2,13},{3,12},{4,11},{5,10},{6,9},{7,8},{8,7},{9,6},... | collective-permute-start | bytes 393224 | tf_op jit(solution)/shard_map/ppermute | solution.py:352
  415.7 39.1 %collective-permute-start.39 = (f32[1,2,8,2048]{3,2,1,0:T(8,128)S(1)}, f32[1,2,8,2048]{3,2,1,0:T(8,128)S(1)}, u32[]{:S(2)}, u32[]{:S(2)}) collective-permute-start(f32[1,2,8,2048]{3,2,1,0:T(8,128)S(1)} %get-tuple-element.108), channel_id=1, source_target_pairs={{0,20},{1,21},{2,22},{3,23},{4,16},{5,17},{6,18},{7,19},{8,28},{9,... | collective-permute-start | bytes 393224 | tf_op jit(solution)/shard_map/ppermute | solution.py:352
  426.4 30.1 %collective-permute-start.40 = (f32[1,2,8,2048]{3,2,1,0:T(8,128)S(1)}, f32[1,2,8,2048]{3,2,1,0:T(8,128)S(1)}, u32[]{:S(2)}, u32[]{:S(2)}) collective-permute-start(f32[1,2,8,2048]{3,2,1,0:T(8,128)S(1)} %get-tuple-element.107), channel_id=1, source_target_pairs={{0,21},{1,20},{2,23},{3,22},{4,17},{5,16},{6,19},{7,18},{8,29},{9,... | collective-permute-start | bytes 393224 | tf_op jit(solution)/shard_map/ppermute | solution.py:352
  433.6 22.9 %collective-permute-start.41 = (f32[1,2,8,2048]{3,2,1,0:T(8,128)S(1)}, f32[1,2,8,2048]{3,2,1,0:T(8,128)S(1)}, u32[]{:S(2)}, u32[]{:S(2)}) collective-permute-start(f32[1,2,8,2048]{3,2,1,0:T(8,128)S(1)} %get-tuple-element.106), channel_id=1, source_target_pairs={{0,22},{1,23},{2,20},{3,21},{4,18},{5,19},{6,16},{7,17},{8,30},{9,... | collective-permute-start | bytes 393224 | tf_op jit(solution)/shard_map/ppermute | solution.py:352
  436.4 26.0 %collective-permute-start.42 = (f32[1,2,8,2048]{3,2,1,0:T(8,128)S(1)}, f32[1,2,8,2048]{3,2,1,0:T(8,128)S(1)}, u32[]{:S(2)}, u32[]{:S(2)}) collective-permute-start(f32[1,2,8,2048]{3,2,1,0:T(8,128)S(1)} %get-tuple-element.105), channel_id=1, source_target_pairs={{0,23},{1,22},{2,21},{3,20},{4,19},{5,18},{6,17},{7,16},{8,31},{9,... | collective-permute-start | bytes 393224 | tf_op jit(solution)/shard_map/ppermute | solution.py:352
  438.8 33.5 %collective-permute-start.43 = (f32[1,2,8,2048]{3,2,1,0:T(8,128)S(1)}, f32[1,2,8,2048]{3,2,1,0:T(8,128)S(1)}, u32[]{:S(2)}, u32[]{:S(2)}) collective-permute-start(f32[1,2,8,2048]{3,2,1,0:T(8,128)S(1)} %get-tuple-element.104), channel_id=1, source_target_pairs={{0,28},{1,29},{2,30},{3,31},{4,24},{5,25},{6,26},{7,27},{8,20},{9,... | collective-permute-start | bytes 393224 | tf_op jit(solution)/shard_map/ppermute | solution.py:352
  454.8 19.1 %collective-permute-start.44 = (f32[1,2,8,2048]{3,2,1,0:T(8,128)S(1)}, f32[1,2,8,2048]{3,2,1,0:T(8,128)S(1)}, u32[]{:S(2)}, u32[]{:S(2)}) collective-permute-start(f32[1,2,8,2048]{3,2,1,0:T(8,128)S(1)} %get-tuple-element.103), channel_id=1, source_target_pairs={{0,29},{1,28},{2,31},{3,30},{4,25},{5,24},{6,27},{7,26},{8,21},{9,... | collective-permute-start | bytes 393224 | tf_op jit(solution)/shard_map/ppermute | solution.py:352
  456.5 18.4 %collective-permute-start.46 = (f32[1,2,8,2048]{3,2,1,0:T(8,128)S(1)}, f32[1,2,8,2048]{3,2,1,0:T(8,128)S(1)}, u32[]{:S(2)}, u32[]{:S(2)}) collective-permute-start(f32[1,2,8,2048]{3,2,1,0:T(8,128)S(1)} %get-tuple-element.101), channel_id=1, source_target_pairs={{0,31},{1,30},{2,29},{3,28},{4,27},{5,26},{6,25},{7,24},{8,23},{9,... | collective-permute-start | bytes 393224 | tf_op jit(solution)/shard_map/ppermute | solution.py:352
  (50 other events, 2636.5 us)
